TPU v7x, 32 devices: a whole 2x2x4 slice. The times are simulated.
32 devices in a mesh: seq: 4 (over y, x), tp: 8 (over z, core).
Axes of the slice: x: 2, y: 2, z: 4, core: 2. Of those that a mesh axis runs over, the one named last changes fastest.
Arguments:
- hidden: bfloat16 [4096, 4096], P(('seq', 'tp')), may hold values from -6 to 6
- norm_gain: float32 [4096], replicated, may hold values from 0.5 to 1.5
- inner_weight: bfloat16 [4096, 2, 2048], P(None, None, 'tp'), may hold values from -0.09375 to 0.09375
- group_weight: bfloat16 [4096, 1024], P(None, 'tp'), may hold values from -0.09375 to 0.09375
- step_weight: bfloat16 [4096, 32], P(None, 'tp'), may hold values from -0.09375 to 0.09375
- step_bias: float32 [32], P('tp'), may hold values from -2 to 1
- decay_rate: float32 [32], P('tp'), may hold values from 0.0001 to 0.1
- filter_inner: bfloat16 [4, 2048], P(None, 'tp'), may hold values from -3 to 3
- filter_group: bfloat16 [4, 1024], P(None, 'tp'), may hold values from -3 to 3
- skip_gain: float32 [32], P('tp'), may hold values from 0.5 to 1.5
- mixer_gain: float32 [2048], P('tp'), may hold values from 0.5 to 1.5
- output_weight: bfloat16 [2048, 4096], P('tp'), may hold values from -0.125 to 0.125
- segment_ids: int32 [4096], replicated, may hold values from 0 to 3, never falling along the last dimension, each value on 1 to 2048 neighbouring positions
Outputs:
- layer_out: bfloat16 [4096, 4096], P(('seq', 'tp'))
Inputs may be any that keep to these rules, and one draw needn't show every extreme that they name: `segment_ids`: ids never fall along the pack; every id names at least one token, and one request has exactly 2048 tokens.
All inputs are finite; a program needn't handle non-finite values.
Results may differ from a plain program's by a relative error of at most 0.0051.
Values may be sent and summed in bfloat16 or wider, within the bound.
A program may use at most 128 MiB of HBM per device.

v0:
```python
import jax
import jax.numpy as jnp
from jax import lax
from jax.sharding import PartitionSpec as P

STRETCH = 256


EPS = 1e-05
HIGH = lax.Precision.HIGHEST


def swapped(block, axis, stride):
    count = lax.axis_size(axis)
    route = []
    for low in range(count):
        high = low | 1 << stride
        if high != low and high < count:
            route += [(low, high), (high, low)]
    return lax.ppermute(block, axis, route)


def from_behind(array, axis, by):
    size = lax.axis_size(axis)
    pairs = [(i, i + by) for i in range(size) if 0 <= i + by < size]
    return lax.ppermute(array, axis, pairs)


def entering_2(value, axis, join, neutral):
    count, mine = (lax.axis_size(axis), lax.axis_index(axis))
    pieces = jax.tree.map(lambda part: lax.all_gather(part, axis), value)
    total = jax.tree.map(
        lambda part, zero: jnp.full_like(part, 0) + jnp.asarray(zero, part.dtype), value, neutral
    )

    def hop(position, total):
        longer = join(total, jax.tree.map(lambda part: part[position], pieces))
        return jax.tree.map(lambda new, old: jnp.where(position < mine, new, old), longer, total)

    return lax.fori_loop(0, count - 1, hop, total)


def combine(earlier, later):
    return (earlier[0] * later[0], later[0][:, None, None] * earlier[1] + later[1])


def body(
    hidden,
    norm_gain,
    inner_weight,
    group_weight,
    step_weight,
    step_bias,
    decay_rate,
    filter_inner,
    filter_group,
    skip_gain,
    mixer_gain,
    output_weight,
    segment_ids,
):
    rows = hidden.shape[0]
    length = rows * lax.axis_size("tp")
    width = hidden.shape[1]
    inner_dev = inner_weight.shape[2]
    heads_dev = step_weight.shape[1]
    head_dim = inner_dev // heads_dev
    state_dim = group_weight.shape[1]
    taps = filter_inner.shape[0]
    first_row = lax.axis_index("seq") * length
    is_first = lax.axis_index("tp") % 2 == 0
    hidden_f = hidden.astype(jnp.float32)
    normed = (
        hidden_f
        * lax.rsqrt(jnp.mean(hidden_f * hidden_f, axis=-1, keepdims=True) + EPS)
        * norm_gain
    ).astype(jnp.bfloat16)
    other_weight, other_filter = swapped((group_weight, filter_group), "tp", 0)
    group_cols = (
        jnp.where(is_first, group_weight, other_weight),
        jnp.where(is_first, other_weight, group_weight),
    )
    filters = jnp.concatenate(
        [
            filter_inner,
            jnp.where(is_first, filter_group, other_filter),
            jnp.where(is_first, other_filter, filter_group),
        ],
        axis=1,
    )
    matrices = (inner_weight.reshape(width, 2 * inner_dev),) + group_cols + (step_weight,)
    piece = lax.all_gather(normed, "tp", axis=0, tiled=True)
    projected = jnp.concatenate(
        [jnp.dot(piece, matrix, preferred_element_type=jnp.float32) for matrix in matrices], axis=1
    )
    gate_z = projected[:, :inner_dev]
    conv_in = projected[:, inner_dev:-heads_dev]
    step_raw = projected[:, -heads_dev:]
    seg_pad = jnp.concatenate([jnp.full((taps - 1,), -1, jnp.int32), segment_ids])
    seg_ext = lax.dynamic_slice_in_dim(seg_pad, first_row, length + taps - 1)
    seg_local = seg_ext[taps - 1 :]
    before = from_behind(conv_in[length - (taps - 1) :], "seq", 1)
    extended = jnp.concatenate([before, conv_in], axis=0)
    filters_f = filters.astype(jnp.float32)
    total = jnp.zeros_like(conv_in)
    for offset in range(taps):
        same = (seg_ext[offset : offset + length] == seg_local).astype(jnp.float32)
        total = total + filters_f[offset] * extended[offset : offset + length] * same[:, None]
    active = jax.nn.silu(total)
    inner_x = active[:, :inner_dev]
    input_map = active[:, inner_dev : inner_dev + state_dim]
    output_map = active[:, inner_dev + state_dim :]
    starts = seg_local != seg_ext[taps - 2 : taps - 2 + length]
    step = jax.nn.softplus(step_raw + step_bias)
    log_decay = -step * decay_rate
    blocks = length // STRETCH
    block_x = inner_x.reshape(blocks, STRETCH, heads_dev, head_dim)
    block_b = input_map.reshape(blocks, STRETCH, state_dim)
    block_c = output_map.reshape(blocks, STRETCH, state_dim)
    step_heads = step.reshape(blocks, STRETCH, heads_dev).transpose(0, 2, 1)
    cumul = jnp.cumsum(log_decay.reshape(blocks, STRETCH, heads_dev), axis=1).transpose(0, 2, 1)
    block_seg = seg_local.reshape(blocks, STRETCH)
    block_start = starts.reshape(blocks, STRETCH)
    causal = jnp.tril(jnp.ones((STRETCH, STRETCH), jnp.bool_))
    same_seg = ((block_seg[:, :, None] == block_seg[:, None, :]) & causal)[:, None]
    gaps = cumul[:, :, :, None] - cumul[:, :, None, :]
    decay = jnp.where(same_seg, jnp.exp(jnp.where(same_seg, gaps, 0.0)), 0.0)
    products = jnp.einsum("cin,cjn->cij", block_c, block_b, precision=HIGH)
    mixing = decay * products[:, None] * step_heads[:, :, None, :]
    local_y = jnp.einsum("chij,cjhp->cihp", mixing, block_x, precision=HIGH)
    same_last = (block_seg == block_seg[:, -1:])[:, None, :]
    last_gap = cumul[:, :, -1:] - cumul
    end_weight = (
        jnp.where(same_last, jnp.exp(jnp.where(same_last, last_gap, 0.0)), 0.0) * step_heads
    )
    block_state = jnp.einsum("chj,cjhp,cjn->chpn", end_weight, block_x, block_b, precision=HIGH)
    clean = jnp.logical_not(jnp.any(block_start, axis=1)).astype(jnp.float32)
    block_keep = jnp.exp(cumul[:, :, -1]) * clean[:, None]

    def carry_blocks(carry, inputs):
        acc_state, acc_keep = carry
        keep, fresh = inputs
        return ((keep[:, None, None] * acc_state + fresh, acc_keep * keep), (acc_state, acc_keep))

    empty_state = jnp.zeros((heads_dev, head_dim, state_dim), jnp.float32)
    unit_keep = jnp.ones((heads_dev,), jnp.float32)
    (device_state, device_keep), (prior_state, prior_keep) = lax.scan(
        carry_blocks, (empty_state, unit_keep), (block_keep, block_state)
    )
    entering = entering_2((device_keep, device_state), "seq", combine, (unit_keep, empty_state))
    incoming = entering[1]
    entry_state = prior_state + prior_keep[:, :, None, None] * incoming[None]
    alive = (jnp.cumsum(block_start.astype(jnp.int32), axis=1) == 0).astype(jnp.float32)
    entry_weight = jnp.exp(cumul) * alive[:, None, :]
    carried_y = jnp.einsum("chi,cin,chpn->cihp", entry_weight, block_c, entry_state, precision=HIGH)
    ssm_out = (local_y + carried_y).reshape(length, heads_dev, head_dim) + skip_gain[
        None, :, None
    ] * inner_x.reshape(length, heads_dev, head_dim)
    gated = ssm_out.reshape(length, inner_dev) * jax.nn.silu(gate_z)
    own_squares = jnp.sum(gated * gated, axis=-1)
    other_squares = swapped(own_squares, "tp", 0)
    group_mean = (own_squares + other_squares) / (2 * inner_dev)
    mixed = (gated * lax.rsqrt(group_mean + EPS)[:, None] * mixer_gain).astype(jnp.bfloat16)
    partial_out = jnp.dot(mixed, output_weight, preferred_element_type=jnp.float32)
    mine = lax.psum_scatter(partial_out, "tp", scatter_dimension=0, tiled=True)
    return (hidden_f + mine).astype(jnp.bfloat16)


def solution(mesh):
    in_specs = (
        P(("seq", "tp"), None),
        P(),
        P(None, None, "tp"),
        P(None, "tp"),
        P(None, "tp"),
        P("tp"),
        P("tp"),
        P(None, "tp"),
        P(None, "tp"),
        P("tp"),
        P("tp"),
        P("tp", None),
        P(),
    )
    out_specs = P(("seq", "tp"), None)
    return jax.shard_map(body, mesh=mesh, in_specs=in_specs, out_specs=out_specs, check_vma=False)
```

profile of v0, /device:TPU:0, one launch (start us, length us, event | category | flops | bytes accessed | tf_op | source)
XLA Modules:
  0.0 372.5 jit_solution(9451892559120451516)
XLA Ops:
  6.6 1.7 fusion.20
  8.3 2.5 fusion.22
  10.9 0.5 collective-permute-start
  11.6 1.2 reduce-window.16
  13.6 1.0 compare_and_fusion
  14.8 4.9 %copy.92 = bf16[512,8,2,256]{3,1,2,0:T(8,128)(2,1)} copy(bf16[512,8,2,256]{3,2,1,0:T(2,128)(2,1)} %bitcast.91) | data formatting | bytes 8388608
  19.7 0.6 dynamic-slice
  21.1 74.7 %all-gather.4.cloned.1.call-done = bf16[1024,4096]{1,0:T(8,128)(2,1)} async-done(((bf16[128,4096]{1,0:T(8,128)(2,1)}), bf16[1024,4096]{1,0:T(8,128)(2,1)}) %all-gather.4.cloned.1.call-update) | async-done | bytes 8388624 | tf_op jit(solution)/shard_map/all_gather | solution.py:92
  95.8 5.7 %negate_multiply_fusion = (f32[1024,4]{0,1:T(4,128)S(1)}, f32[1024,4]{0,1:T(4,128)S(1)}) fusion(f32[4]{0:T(128)S(1)} %copy-done.15, f32[4]{0:T(128)S(1)} %copy-done.16, bf16[1024,4096]{1,0:T(8,128)(2,1)} %all-gather.4.cloned.1.call-done, bf16[4096,4]{0,1:T(4,128)(2,1)S(1)} %copy-done.13), kind=kOutput, calls=%fused_computation.96 | convolution fusion | flops 33591296 | bytes 8454176 | tf_op jit(solution)/shard_map/dot_general | solution.py:94
  101.5 4.8 %reduce-window.14 = f32[4,4,2,128]{3,2,1,0:T(2,128)S(1)} reduce-window(f32[4,4,2,128]{3,2,1,0:T(2,128)S(1)} %copy.83, f32[]{:T(128)} %constant.89.clone.1), window={size=1x1x1x128 pad=0_0x0_0x0_0x127_0}, to_apply=%region_1.2 | reduce-window | flops 520192 | bytes 32772 | tf_op jit(solution)/shard_map/reduce-window
  107.2 6.7 %fusion.38 = f32[1024,128]{0,1:T(8,128)S(1)} fusion(bf16[1024,4096]{1,0:T(8,128)(2,1)} %all-gather.4.cloned.1.call-done, bf16[4096,128]{1,0:T(8,128)(2,1)} %collective-permute-done.1, bf16[4096,128]{1,0:T(8,128)(2,1)S(1)} %copy-done.7, pred[]{:T(512)S(6)} %eq.59), kind=kOutput, calls=%fused_computation.58 | convolution fusion | flops 1074266112 | bytes 11010049 | tf_op jit(solution)/shard_map/dot_general | solution.py:94
  113.8 2.9 fusion.40
  116.8 6.5 %fusion.78 = f32[1024,512]{0,1:T(8,128)S(1)} fusion(bf16[1024,4096]{1,0:T(8,128)(2,1)S(1)} %copy-done.1, bf16[4096,512]{1,0:T(8,128)(2,1)} %bitcast.92), kind=kOutput, calls=%fused_computation.123 | convolution fusion | flops 4294967296 | bytes 14680064 | tf_op jit(solution)/shard_map/dot_general | solution.py:94
  123.4 3.6 collective-permute-start.2
  127.4 5.9 %collective-permute-done.2 = f32[3,512]{0,1:T(8,128)S(1)} collective-permute-done((f32[3,512]{0,1:T(8,128)S(1)}, f32[3,512]{0,1:T(8,128)S(1)}, u32[]{:S(2)}, u32[]{:S(2)}) %collective-permute-start.2) | collective-permute-done | bytes 6176 | tf_op jit(solution)/shard_map/ppermute | solution.py:26
  133.3 2.4 divide_multiply_fusion
  135.7 1.1 slice.107
  136.8 0.5 copy-done.2
  137.4 2.7 reshape.145
  140.1 1.0 reshape.150
  141.1 3.4 fusion.36
  144.5 6.9 %while.31 = (s32[]{:T(128)}, f32[4,64,128]{2,1,0:T(8,128)S(1)}, f32[4]{0:T(128)S(1)}, f32[4,4,64,128]{3,2,1,0:T(8,128)}, f32[4,4]{1,0:T(4,128)S(1)}, /*index=5*/...) while((s32[]{:T(128)}, f32[4,64,128]{2,1,0:T(8,128)S(1)}, f32[4]{0:T(128)S(1)}, ...), condition=%wide.region_7.8_spmd.clone, body=%wide.region_6.7_spmd.clone.sunk | while | flops 131083 | bytes 655617 | solution.py:147
  144.6 0.7 bitcast_dynamic-update-slice_fusion.2
  145.2 1.0 bitcast_add_fusion.3
  146.3 0.7 bitcast_dynamic-update-slice_fusion.2
  146.9 1.0 bitcast_add_fusion.3
  148.0 0.7 bitcast_dynamic-update-slice_fusion.2
  148.7 1.0 bitcast_add_fusion.3
  149.7 0.7 bitcast_dynamic-update-slice_fusion.2
  150.4 1.0 bitcast_add_fusion.3
  151.6 1.0 reshape.149
  152.7 10.8 %all-reduce.1 = f32[16]{0:T(128)S(1)} all-reduce(f32[16]{0:T(128)S(1)} %dynamic-update-slice), channel_id=2, replica_groups=mesh['seq'=4,'tp'=8] {'seq'}, use_global_device_ids=true, to_apply=%add.1 | all-reduce | flops 16 | bytes 128
  163.6 10.2 %all-gather.1 = f32[16,64,128]{2,1,0:T(8,128)} all-gather(f32[4,64,128]{2,1,0:T(8,128)S(1)} %get-tuple-element.142), channel_id=3, replica_groups=mesh['seq'=4,'tp'=8] {'seq'}, dimensions={0}, use_global_device_ids=true | all-gather | bytes 655360 | tf_op jit(solution)/shard_map/all_gather | solution.py:31
  173.8 3.1 while.32
  173.8 1.0 fusion.89
  174.9 1.0 fusion.89
  175.9 1.0 fusion.89
  176.9 1.0 fusion.47
  178.2 5.2 %fusion.33 = f32[4,256,4,64]{1,3,2,0:T(8,128)S(1)} fusion(f32[4,4,256]{2,1,0:T(4,128)S(1)} %copy.69, f32[4,256,256]{2,1,0:T(8,128)S(1)} %fusion.47, f32[4,4,256]{2,1,0:T(4,128)S(1)} %reduce_window_sum.41, pred[4,256,256]{2,1,0:T(8,128)(4,1)S(1)} %copy-done.11, f32[4,256,4,64]{1,0,3,2:T(4,128)S(1)} %copy-done.8), kind=kOutput, calls=%fused_computation.51 | convolution fusion | flops 810549248 | bytes 3440640 | tf_op jit(solution)/shard_map/chij,cjhp->cihp/dot_general | solution.py:130
  183.4 1.1 fusion.32
  184.6 0.7 copy.80
  185.5 0.7 copy-done.3
  186.1 0.6 copy-done.5
  186.8 0.4 multiply_reduce_fusion
  187.3 1.2 collective-permute-done.3
  188.4 8.2 %fusion.46 = f32[1024,4096]{1,0:T(8,128)} fusion(bf16[256,4096]{1,0:T(8,128)(2,1)S(1)} %copy-done, f32[1024,256]{0,1:T(8,128)S(1)} %get-tuple-element.213, f32[256]{0:T(256)S(1)} %copy-done.14, f32[1024]{0:T(1024)S(1)} %add_rsqrt_fusion), kind=kOutput, calls=%fused_computation.67 | convolution fusion | flops 2148270080 | bytes 19928064 | tf_op jit(solution)/shard_map/dot_general | solution.py:164
  196.7 166.2 %reduce-scatter.2.cloned.1.call-done = f32[128,4096]{1,0:T(8,128)} async-done(((f32[1024,4096]{1,0:T(8,128)}), f32[128,4096]{1,0:T(8,128)}) %reduce-scatter.2.cloned.1.call-update) | async-done | bytes 2097168 | tf_op jit(solution)/shard_map/reduce_scatter | solution.py:165
  362.8 2.8 fusion.23
  (111 shorter events, 3.8 us)
Async XLA Ops:
  6.5 181.9 %copy-start = (bf16[256,4096]{1,0:T(8,128)(2,1)S(1)}, bf16[256,4096]{1,0:T(8,128)(2,1)}, u32[]{:S(2)}) copy-start(bf16[256,4096]{1,0:T(8,128)(2,1)} %param.28) | copy-start | bytes 6291460
  6.5 4.3 %copy-start.18 = (bf16[4,128]{1,0:T(4,128)(2,1)S(1)}, bf16[4,128]{1,0:T(4,128)(2,1)}, u32[]{:S(2)}) copy-start(bf16[4,128]{1,0:T(4,128)(2,1)} %param.25) | copy-start | bytes 3076
  6.5 4.9 %copy-start.7 = (bf16[4096,128]{1,0:T(8,128)(2,1)S(1)}, bf16[4096,128]{1,0:T(8,128)(2,1)}, u32[]{:S(2)}) copy-start(bf16[4096,128]{1,0:T(8,128)(2,1)} %param.20) | copy-start | bytes 3145732
  6.5 5.0 %copy-start.12 = (s32[4096]{0:T(1024)S(1)}, s32[4096]{0:T(1024)}, u32[]{:S(2)}) copy-start(s32[4096]{0:T(1024)} %param.29) | copy-start | bytes 49156
  6.5 89.2 %all-gather.4.cloned.1.call-start = ((), (), s32[]{:S(2)}) async-start(), calls=%async_computation.1 | async-start | bytes 9437184 | tf_op jit(solution)/shard_map/all_gather | solution.py:92
  8.3 6.3 %copy-start.19 = (f32[4]{0:T(128)S(1)}, f32[4]{0:T(128)}, u32[]{:S(2)}) copy-start(f32[4]{0:T(128)} %param.26) | copy-start | bytes 52
  10.8 352.0 %reduce-scatter.2.cloned.1.call-start = ((), (), s32[]{:S(2)}) async-start(), calls=%async_computation.2 | async-start | bytes 18874368 | tf_op jit(solution)/shard_map/reduce_scatter | solution.py:165
  10.9 10.1 %collective-permute-start = (bf16[4,128]{1,0:T(4,128)(2,1)S(1)}, bf16[4,128]{1,0:T(4,128)(2,1)S(1)}, u32[]{:S(2)}, u32[]{:S(2)}) collective-permute-start(bf16[4,128]{1,0:T(4,128)(2,1)S(1)} %copy-done.18), channel_id=1, source_target_pairs={{0,1},{1,0},{2,3},{3,2},{4,5},{5,4},{6,7},{7,6},{8,9},{9,8},{10,11... | collective-permute-start | bytes 3080 | tf_op jit(solution)/shard_map/ppermute | solution.py:20
  11.4 95.7 %collective-permute-start.1 = (bf16[4096,128]{1,0:T(8,128)(2,1)S(1)}, bf16[4096,128]{1,0:T(8,128)(2,1)}, u32[]{:S(2)}, u32[]{:S(2)}) collective-permute-start(bf16[4096,128]{1,0:T(8,128)(2,1)S(1)} %copy-done.7), channel_id=1, source_target_pairs={{0,1},{1,0},{2,3},{3,2},{4,5},{5,4},{6,7},{7,6},{8,9},{9,8},{10,11... | collective-permute-start | bytes 3145736 | tf_op jit(solution)/shard_map/ppermute | solution.py:20
  14.8 5.0 %copy-start.20 = (u32[32]{0:T(128)S(1)}, u32[32]{0:T(128)}, u32[]{:S(2)}) copy-start(u32[32]{0:T(128)} %constant.107) | copy-start | bytes 388
  14.8 6.3 %copy-start.17 = (bf16[4,256]{1,0:T(4,128)(2,1)S(1)}, bf16[4,256]{1,0:T(4,128)(2,1)}, u32[]{:S(2)}) copy-start(bf16[4,256]{1,0:T(4,128)(2,1)} %param.24) | copy-start | bytes 6148
  14.8 81.0 %copy-start.13 = (bf16[4096,4]{0,1:T(4,128)(2,1)S(1)}, bf16[4096,4]{0,1:T(4,128)(2,1)}, u32[]{:S(2)}) copy-start(bf16[4096,4]{0,1:T(4,128)(2,1)} %param.21) | copy-start | bytes 98308
  14.8 81.0 %copy-start.15 = (f32[4]{0:T(128)S(1)}, f32[4]{0:T(128)}, u32[]{:S(2)}) copy-start(f32[4]{0:T(128)} %param.23) | copy-start | bytes 52
  14.8 81.0 %copy-start.16 = (f32[4]{0:T(128)S(1)}, f32[4]{0:T(128)}, u32[]{:S(2)}) copy-start(f32[4]{0:T(128)} %param.22) | copy-start | bytes 52
  107.1 6.7 %copy-start.1 = (bf16[1024,4096]{1,0:T(8,128)(2,1)S(1)}, bf16[1024,4096]{1,0:T(8,128)(2,1)}, u32[]{:S(2)}) copy-start(bf16[1024,4096]{1,0:T(8,128)(2,1)} %all-gather.4.cloned.1.call-done) | copy-start | bytes 25165828
  123.3 4.1 %copy-start.4 = (f32[1024,512]{0,1:T(8,128)}, f32[1024,512]{0,1:T(8,128)S(1)}, u32[]{:S(2)}) copy-start(f32[1024,512]{0,1:T(8,128)S(1)} %fusion.78) | copy-start | bytes 6291460
  123.4 9.8 %collective-permute-start.2 = (f32[3,512]{0,1:T(8,128)S(1)}, f32[3,512]{0,1:T(8,128)S(1)}, u32[]{:S(2)}, u32[]{:S(2)}) collective-permute-start(f32[3,512]{0,1:T(8,128)S(1)} %pad_maximum_fusion.3), channel_id=1, source_target_pairs={{0,8},{8,16},{16,24},{1,9},{9,17},{17,25},{2,10},{10,18},{18,26},{... | collective-permute-start | bytes 18440 | tf_op jit(solution)/shard_map/ppermute | solution.py:26
  135.6 1.6 copy-start.2
  176.9 1.2 copy-start.8
  176.9 1.3 copy-start.11
  178.2 5.2 %copy-start.9 = (f32[4,256,128]{1,0,2:T(4,128)S(1)}, f32[4,256,128]{1,0,2:T(4,128)}, u32[]{:S(2)}) copy-start(f32[4,256,128]{1,0,2:T(4,128)} %reshape.149) | copy-start | bytes 1572868
  178.2 5.2 %copy-start.10 = (f32[4,4,64,128]{3,2,1,0:T(8,128)S(1)}, f32[4,4,64,128]{3,2,1,0:T(8,128)}, u32[]{:S(2)}) copy-start(f32[4,4,64,128]{3,2,1,0:T(8,128)} %get-tuple-element.139) | copy-start | bytes 1572868
  184.5 1.6 copy-start.3
  184.6 2.2 copy-start.5
  186.8 1.7 copy-start.14
  187.2 1.2 collective-permute-start.3
  196.7 166.2 %copy-start.6 = (bf16[128,4096]{1,0:T(8,128)(2,1)S(1)}, bf16[128,4096]{1,0:T(8,128)(2,1)}, u32[]{:S(2)}) copy-start(bf16[128,4096]{1,0:T(8,128)(2,1)} %param.17) | copy-start | bytes 3145732
Sparse Core Ops, SparseCore 0:
  10.9 84.7 all-gather.3
  196.8 165.9 reduce-scatter.1
where the time goes:
time: 373 us; the launch traced here: 372 us
  waiting for transfers between devices  248 us (66%)
  matrix products  40.7 us (11%)
  other arithmetic  27.4 us (7%)
  blocking collectives  21.1 us (6%)
  local copies, waits for them, and re-layouts  16.4 us (4%)
  between operations  14.5 us (4%)
  starting transfers between devices  4.37 us (1%)
    reduce_scatter x1, waiting for transfers between devices, body(): mine = lax.psum_scatter(partial_out, 'tp', scatter_dimension=0, tiled=True)  166 us
    all_gather x1, waiting for transfers between devices, body(): piece = lax.all_gather(normed, 'tp', axis=0, tiled=True)  74.7 us
    dot_general x4, matrix products, body(): jnp.dot(piece, matrix, preferred_element_type=jnp.float32)  21.8 us
    unnamed x1, blocking collectives  10.8 us
    all_gather x1, blocking collectives, entering_2(): pieces = jax.tree.map(lambda part: lax.all_gather(part, axis), value)  10.2 us
    unnamed x49, local copies, waits for them, and re-layouts  8.25 us
    dot_general x1, matrix products, body(): jnp.dot(mixed, output_weight, preferred_element_type=jnp.float32)  8.21 us
  transfers between devices with their start and end apart: 6, of which 4 were waited for; matrix products, arithmetic and copies ran while one was open for 5% of the time, Pallas kernels for 0%

commit v1 on v0

--- a/solution.py
+++ b/solution.py
@@ -20,10 +20,27 @@
     return lax.ppermute(block, axis, route)
 
 
-def from_behind(array, axis, by):
-    size = lax.axis_size(axis)
-    pairs = [(i, i + by) for i in range(size) if 0 <= i + by < size]
-    return lax.ppermute(array, axis, pairs)
+def crossed(block, axis, mask):
+    if mask == 0:
+        return block
+    return lax.ppermute(block, axis, [(i, i ^ mask) for i in range(lax.axis_size(axis))])
+
+
+def tail_of_previous(block):
+    spans, parts = lax.axis_size("seq"), lax.axis_size("tp")
+    total = None
+    for part in range(parts):
+        route = [(i * parts - 1, i * parts + part) for i in range(1, spans)]
+        got = lax.ppermute(block, ("seq", "tp"), route)
+        total = got if total is None else total + got
+    return total
+
+
+def spread_weight(weight, spans, chips):
+    cols = weight.shape[1] // spans
+    own = lax.dynamic_slice_in_dim(weight, lax.axis_index("seq") * cols, cols, axis=1)
+    along = [crossed(own, "tp", 2 * d) for d in range(chips)]
+    return [[crossed(part, "seq", e) for part in along] for e in range(spans)]
 
 
 def entering_2(value, axis, join, neutral):
@@ -42,6 +59,30 @@
 
 def combine(earlier, later):
     return (earlier[0] * later[0], later[0][:, None, None] * earlier[1] + later[1])
+
+
+def project_out(hidden, mixed, weights):
+    rows, spans, chips = hidden.shape[0], len(weights), len(weights[0])
+    chip, core = lax.axis_index("tp") // 2, lax.axis_index("tp") % 2
+    span = lax.axis_index("seq")
+    cols = hidden.shape[1] // spans
+    taken = []
+    for d in range(chips):
+        block = lax.dynamic_slice_in_dim(mixed, (chip ^ d) * 2 * rows, 2 * rows, axis=0)
+        taken.append(crossed(block, "tp", 2 * d))
+    out = jnp.zeros(hidden.shape, jnp.bfloat16)
+    for e in range(spans):
+        part = sum(
+            jnp.dot(m, w, preferred_element_type=jnp.float32) for m, w in zip(taken, weights[e])
+        )
+        own = lax.dynamic_slice_in_dim(part, core * rows, rows, axis=0)
+        other = lax.dynamic_slice_in_dim(part, (1 - core) * rows, rows, axis=0)
+        other = crossed(other.astype(jnp.bfloat16), "tp", 1).astype(jnp.float32)
+        start = (span ^ e) * cols
+        base = lax.dynamic_slice_in_dim(hidden, start, cols, axis=1).astype(jnp.float32)
+        done = (base + own + other).astype(jnp.bfloat16)
+        out = lax.dynamic_update_slice_in_dim(out, done, start, axis=1)
+    return out
 
 
 def body(
@@ -88,18 +129,25 @@
         ],
         axis=1,
     )
-    matrices = (inner_weight.reshape(width, 2 * inner_dev),) + group_cols + (step_weight,)
+    spans, chips = lax.axis_size("seq"), lax.axis_size("tp") // 2
+    weights = spread_weight(output_weight, spans, chips)
+    tail = tail_of_previous(normed[rows - 8 :])
+    matrix = jnp.concatenate(
+        (inner_weight.reshape(width, 2 * inner_dev),)
+        + group_cols
+        + (jnp.pad(step_weight, ((0, 0), (0, 128 - heads_dev))),),
+        axis=1,
+    )
+    before = jnp.dot(tail, matrix[:, inner_dev:-128], preferred_element_type=jnp.float32)
+    before = before[8 - (taps - 1) :]
     piece = lax.all_gather(normed, "tp", axis=0, tiled=True)
-    projected = jnp.concatenate(
-        [jnp.dot(piece, matrix, preferred_element_type=jnp.float32) for matrix in matrices], axis=1
-    )
+    projected = jnp.dot(piece, matrix, preferred_element_type=jnp.float32)
     gate_z = projected[:, :inner_dev]
-    conv_in = projected[:, inner_dev:-heads_dev]
-    step_raw = projected[:, -heads_dev:]
+    conv_in = projected[:, inner_dev:-128]
+    step_raw = projected[:, -128 : heads_dev - 128]
     seg_pad = jnp.concatenate([jnp.full((taps - 1,), -1, jnp.int32), segment_ids])
     seg_ext = lax.dynamic_slice_in_dim(seg_pad, first_row, length + taps - 1)
     seg_local = seg_ext[taps - 1 :]
-    before = from_behind(conv_in[length - (taps - 1) :], "seq", 1)
     extended = jnp.concatenate([before, conv_in], axis=0)
     filters_f = filters.astype(jnp.float32)
     total = jnp.zeros_like(conv_in)
@@ -161,9 +209,7 @@
     other_squares = swapped(own_squares, "tp", 0)
     group_mean = (own_squares + other_squares) / (2 * inner_dev)
     mixed = (gated * lax.rsqrt(group_mean + EPS)[:, None] * mixer_gain).astype(jnp.bfloat16)
-    partial_out = jnp.dot(mixed, output_weight, preferred_element_type=jnp.float32)
-    mine = lax.psum_scatter(partial_out, "tp", scatter_dimension=0, tiled=True)
-    return (hidden_f + mine).astype(jnp.bfloat16)
+    return project_out(hidden, mixed, weights)
 
 
 def solution(mesh):

time: 373 us -> 294 us (0.79)
  waiting for transfers between devices: 248 us -> 115 us
  starting transfers between devices: 4.37 us -> 41.1 us
  local copies, waits for them, and re-layouts: 16.4 us -> 30 us
  other arithmetic: 27.4 us -> 36.4 us
  matrix products: 40.7 us -> 35.1 us
    reduce_scatter x1 -> x0, waiting for transfers between devices: 166 us -> none  [body(): mine = lax.psum_scatter(partial_out, 'tp', scatter_dimension=0, tiled=True)]
    ppermute x1 -> x30, waiting for transfers between devices: 5.88 us -> 60.6 us  [the longest x22 60.6 us: crossed(): lax.ppermute(block, axis, [(i, i ^ mask) for i in range(lax.axis_size(axi...]
    ppermute x1 -> x30, starting transfers between devices: 3.61 us -> 40.6 us  [the longest x22 33.9 us: crossed(): lax.ppermute(block, axis, [(i, i ^ mask) for i in range(lax.axis_size(axi...]
    all_gather x1, waiting for transfers between devices: 74.7 us -> 54.6 us  [body(): piece = lax.all_gather(normed, 'tp', axis=0, tiled=True)]
    dot_general x5 -> x18, matrix products: 30 us -> 23.5 us  [the longest x1 14 us: body(): projected = jnp.dot(piece, matrix, preferred_element_type=jnp.float32)]
    unnamed x49 -> x66, local copies, waits for them, and re-layouts: 8.25 us -> 12.3 us
  transfers between devices with their start and end apart: 6 -> 34, of which waited for: 4 -> 11; matrix products, arithmetic and copies ran while one was open for 5% -> 11% of each run, Pallas kernels for 0% -> 0%
where the time goes in v1:
time: 294 us; the launch traced here: 293 us
  waiting for transfers between devices  115 us (39%)
  starting transfers between devices  41.1 us (14%)
  other arithmetic  36.4 us (12%)
  matrix products  35.1 us (12%)
  local copies, waits for them, and re-layouts  30 us (10%)
  blocking collectives  19.7 us (7%)
  between operations  15.2 us (5%)
    ppermute x22, waiting for transfers between devices, crossed(): lax.ppermute(block, axis, [(i, i ^ mask) for i in range(lax.axis_size(axi...  60.6 us
    all_gather x1, waiting for transfers between devices, body(): piece = lax.all_gather(normed, 'tp', axis=0, tiled=True)  54.6 us
    ppermute x22, starting transfers between devices, crossed(): lax.ppermute(block, axis, [(i, i ^ mask) for i in range(lax.axis_size(axi...  33.9 us
    dot_general x1, matrix products, body(): projected = jnp.dot(piece, matrix, preferred_element_type=jnp.float32)  14 us
    unnamed x66, local copies, waits for them, and re-layouts  12.3 us
    all_gather x1, blocking collectives, entering_2(): pieces = jax.tree.map(lambda part: lax.all_gather(part, axis), value)  10.6 us
    unnamed x1, blocking collectives  9.13 us
    dot_general x16, matrix products, project_out(): jnp.dot(m, w, preferred_element_type=jnp.float32)  7.96 us
  transfers between devices with their start and end apart: 34, of which 11 were waited for; matrix products, arithmetic and copies ran while one was open for 11% of the time, Pallas kernels for 0%

profile of v1, /device:TPU:0, one launch (start us, length us, event | category | flops | bytes accessed | tf_op | source)
XLA Modules:
  0.0 292.9 jit_solution(16914379334231628703)
XLA Ops:
  6.5 1.7 fusion.25
  8.2 2.5 fusion.27
  10.8 1.5 slice.114
  12.9 1.3 collective-permute-start.2
  14.2 1.3 collective-permute-start.3
  19.9 1.4 fusion.88
  22.3 5.7 %copy.100 = bf16[512,8,2,256]{3,1,2,0:T(8,128)(2,1)} copy(bf16[512,8,2,256]{3,2,1,0:T(2,128)(2,1)} %bitcast.110) | data formatting | bytes 8388608
  28.0 1.4 copy.98
  37.5 1.4 broadcast_select_fusion.2
  40.2 1.6 fusion.15
  41.8 54.6 %all-gather.4.cloned.1.call-done = bf16[1024,4096]{1,0:T(8,128)(2,1)} async-done(((bf16[128,4096]{1,0:T(8,128)(2,1)}), bf16[1024,4096]{1,0:T(8,128)(2,1)}) %all-gather.4.cloned.1.call-update) | async-done | bytes 8388624 | tf_op jit(solution)/shard_map/all_gather | solution.py:143
  96.4 14.0 %fusion.6 = f32[1024,896]{1,0:T(8,128)S(1)} fusion(bf16[1024,4096]{1,0:T(8,128)(2,1)} %all-gather.4.cloned.1.call-done, bf16[4096,4]{1,0:T(8,128)(2,1)S(1)} %copy-done.8, bf16[4096,128]{1,0:T(8,128)(2,1)} %copy-done.7, bf16[4096,128]{1,0:T(8,128)(2,1)} %copy-done.6, bf16[4096,512]{1,0:T(8,128)(2,1)} %bitcast.111), kind=kOutput, calls=%fused_computation.13 | convolution fusion | flops 7552892928 | bytes 18382848 | tf_op jit(solution)/shard_map/dot_general | solution.py:144
  111.7 1.9 divide_multiply_fusion
  115.3 1.2 copy.96
  116.7 4.8 %reduce-window.14 = f32[4,4,2,128]{3,2,1,0:T(2,128)S(1)} reduce-window(f32[4,4,2,128]{3,2,1,0:T(2,128)S(1)} %copy.93, f32[]{:T(128)} %constant.116.clone.1), window={size=1x1x1x128 pad=0_0x0_0x0_0x127_0}, to_apply=%region_1.2 | reduce-window | flops 520192 | bytes 32772 | tf_op jit(solution)/shard_map/reduce-window
  122.3 2.5 copy.76
  124.9 2.7 reshape.145
  127.7 1.4 broadcast_multiply_fusion
  129.1 1.9 fusion.53
  131.1 6.9 %while.31 = (s32[]{:T(128)}, f32[4,64,128]{2,1,0:T(8,128)S(1)}, f32[4]{0:T(128)S(1)}, f32[4,4,64,128]{3,2,1,0:T(8,128)}, f32[4,4]{1,0:T(4,128)S(1)}, /*index=5*/...) while((s32[]{:T(128)}, f32[4,64,128]{2,1,0:T(8,128)S(1)}, f32[4]{0:T(128)S(1)}, ...), condition=%wide.region_7.8_spmd.clone, body=%wide.region_6.7_spmd.clone.sunk | while | flops 131083 | bytes 656117 | solution.py:195
  138.2 10.6 %all-gather.1 = f32[16,64,128]{2,1,0:T(8,128)} all-gather(f32[4,64,128]{2,1,0:T(8,128)S(1)} %get-tuple-element.142), channel_id=3, replica_groups=mesh['seq'=4,'tp'=8] {'seq'}, dimensions={0}, use_global_device_ids=true | all-gather | bytes 655360 | tf_op jit(solution)/shard_map/all_gather | solution.py:48
  148.8 9.1 %all-reduce.2 = f32[16]{0:T(128)S(1)} all-reduce(f32[16]{0:T(128)S(1)} %dynamic-update-slice), channel_id=2, replica_groups=mesh['seq'=4,'tp'=8] {'seq'}, use_global_device_ids=true, to_apply=%add.2 | all-reduce | flops 16 | bytes 128
  158.0 3.1 %while.32 = (s32[]{:T(128)}, f32[4,64,128]{2,1,0:T(8,128)S(1)}, s32[]{:T(128)}, f32[4,4]{1,0:T(4,128)S(1)}, f32[4,4,64,128]{3,2,1,0:T(8,128)}, /*index=5*/s32[]{:T(128)}, s32[]{:T(128)}) while((s32[]{:T(128)}, f32[4,64,128]{2,1,0:T(8,128)S(1)}, s32[]{:T(128)}, f32[4,4]{1,0:T(4,128)S(1)}, f32[4,4,64,128]{3,2,1,0:T(8,128)}, ...), condition=%wide.region_9.10_spmd.clone, body=%wide.region_8.9_spmd.clone.sunk | while | flops 131076 | bytes 393369 | solution.py:57
  162.1 6.6 %fusion.50 = f32[4,256,4,64]{1,3,2,0:T(8,128)S(1)} fusion(f32[4,4,256]{2,1,0:T(4,128)S(1)} %copy.81, f32[4,256,256]{2,1,0:T(8,128)S(1)} %fusion.98, f32[4,4,256]{2,1,0:T(4,128)S(1)} %reduce_window_sum.41, pred[4,256,256]{2,1,0:T(8,128)(4,1)} %compare_and_fusion, f32[4,256,4,64]{1,0,3,2:T(4,128)} %reshape.145), kind=kOutput, calls=%fused_computation.73 | convolution fusion | flops 810549248 | bytes 3440640 | tf_op jit(solution)/shard_map/chij,cjhp->cihp/dot_general | solution.py:178
  168.7 2.1 fusion.49
  170.8 2.8 copy.94
  173.6 2.8 reshape.166
  176.3 2.9 multiply_reduce_fusion
  180.6 3.9 %collective-permute-start.16 = (bf16[256,1024]{1,0:T(8,128)(2,1)S(1)}, bf16[256,1024]{1,0:T(8,128)(2,1)S(1)}, u32[]{:S(2)}, u32[]{:S(2)}) collective-permute-start(bf16[256,1024]{1,0:T(8,128)(2,1)S(1)} %constant_dynamic-slice_fusion.4), channel_id=1, source_target_pairs={{0,6},{1,7},{2,4},{3,5},{4,2},{5,3},{6,0},{7,1},{8,14},{9,15},{10,... | collective-permute-start | bytes 1572872 | tf_op jit(solution)/shard_map/ppermute | solution.py:26
  185.1 1.4 multiply_convert_fusion
  186.9 7.8 %collective-permute-done.28 = bf16[256,1024]{1,0:T(8,128)(2,1)} collective-permute-done((bf16[256,1024]{1,0:T(8,128)(2,1)S(1)}, bf16[256,1024]{1,0:T(8,128)(2,1)}, u32[]{:S(2)}, u32[]{:S(2)}) %collective-permute-start.28) | collective-permute-done | bytes 524320 | tf_op jit(solution)/shard_map/ppermute | solution.py:26
  195.3 2.0 collective-permute-start.29
  197.3 1.3 fusion.64
  198.6 9.9 %collective-permute-done.16 = bf16[256,1024]{1,0:T(8,128)(2,1)S(1)} collective-permute-done((bf16[256,1024]{1,0:T(8,128)(2,1)S(1)}, bf16[256,1024]{1,0:T(8,128)(2,1)S(1)}, u32[]{:S(2)}, u32[]{:S(2)}) %collective-permute-start.16) | collective-permute-done | bytes 524320 | tf_op jit(solution)/shard_map/ppermute | solution.py:26
  209.2 2.3 collective-permute-start.31
  211.8 11.2 %collective-permute-start.11 = (bf16[256,256]{1,0:T(8,128)(2,1)S(1)}, bf16[256,256]{1,0:T(8,128)(2,1)S(1)}, u32[]{:S(2)}, u32[]{:S(2)}) collective-permute-start(bf16[256,256]{1,0:T(8,128)(2,1)S(1)} %get-tuple-element.226), channel_id=1, source_target_pairs={{0,2},{1,3},{2,0},{3,1},{4,6},{5,7},{6,4},{7,5},{8,10},{9,11},{10,... | collective-permute-start | bytes 393224 | tf_op jit(solution)/shard_map/ppermute | solution.py:26
  223.3 6.2 %collective-permute-done.14 = bf16[256,1024]{1,0:T(8,128)(2,1)} collective-permute-done((bf16[256,1024]{1,0:T(8,128)(2,1)S(1)}, bf16[256,1024]{1,0:T(8,128)(2,1)}, u32[]{:S(2)}, u32[]{:S(2)}) %collective-permute-start.14) | collective-permute-done | bytes 524320 | tf_op jit(solution)/shard_map/ppermute | solution.py:26
  230.4 2.0 collective-permute-start.30
  232.5 2.4 collective-permute-start.15
  236.4 3.0 %collective-permute-done.15 = bf16[256,256]{1,0:T(8,128)(2,1)S(1)} collective-permute-done((bf16[256,256]{1,0:T(8,128)(2,1)S(1)}, bf16[256,256]{1,0:T(8,128)(2,1)S(1)}, u32[]{:S(2)}, u32[]{:S(2)}) %collective-permute-start.15) | collective-permute-done | bytes 131104 | tf_op jit(solution)/shard_map/ppermute | solution.py:26
  239.6 6.8 %collective-permute-done.30 = bf16[256,1024]{1,0:T(8,128)(2,1)S(1)} collective-permute-done((bf16[256,1024]{1,0:T(8,128)(2,1)}, bf16[256,1024]{1,0:T(8,128)(2,1)S(1)}, u32[]{:S(2)}, u32[]{:S(2)}) %collective-permute-start.30) | collective-permute-done | bytes 524320 | tf_op jit(solution)/shard_map/ppermute | solution.py:26
  247.5 1.5 collective-permute-start.19
  249.4 7.9 %collective-permute-done.21 = bf16[256,1024]{1,0:T(8,128)(2,1)S(1)} collective-permute-done((bf16[256,1024]{1,0:T(8,128)(2,1)S(1)}, bf16[256,1024]{1,0:T(8,128)(2,1)S(1)}, u32[]{:S(2)}, u32[]{:S(2)}) %collective-permute-start.21) | collective-permute-done | bytes 524320 | tf_op jit(solution)/shard_map/ppermute | solution.py:26
  257.3 1.5 collective-permute-start.20
  259.1 9.4 %collective-permute-done.19 = bf16[256,1024]{1,0:T(8,128)(2,1)S(1)} collective-permute-done((bf16[256,1024]{1,0:T(8,128)(2,1)}, bf16[256,1024]{1,0:T(8,128)(2,1)S(1)}, u32[]{:S(2)}, u32[]{:S(2)}) %collective-permute-start.19) | collective-permute-done | bytes 524320 | tf_op jit(solution)/shard_map/ppermute | solution.py:26
  268.8 8.7 %collective-permute-done.20 = bf16[256,1024]{1,0:T(8,128)(2,1)S(1)} collective-permute-done((bf16[256,1024]{1,0:T(8,128)(2,1)}, bf16[256,1024]{1,0:T(8,128)(2,1)S(1)}, u32[]{:S(2)}, u32[]{:S(2)}) %collective-permute-start.20) | collective-permute-done | bytes 524320 | tf_op jit(solution)/shard_map/ppermute | solution.py:26
  277.9 1.3 convolution_add_fusion.7
  279.6 1.3 fusion.48
  (211 shorter events, 44.2 us)
Async XLA Ops:
  6.5 172.7 %copy-start = (bf16[256,4096]{1,0:T(8,128)(2,1)S(1)}, bf16[256,4096]{1,0:T(8,128)(2,1)}, u32[]{:S(2)}) copy-start(bf16[256,4096]{1,0:T(8,128)(2,1)} %param.28) | copy-start | bytes 6291460
  6.5 8.9 %copy-start.5 = (bf16[4096,128]{1,0:T(8,128)(2,1)S(1)}, bf16[4096,128]{1,0:T(8,128)(2,1)}, u32[]{:S(2)}) copy-start(bf16[4096,128]{1,0:T(8,128)(2,1)} %param.20) | copy-start | bytes 3145732
  6.5 9.4 %copy-start.11 = (s32[4096]{0:T(1024)S(1)}, s32[4096]{0:T(1024)}, u32[]{:S(2)}) copy-start(s32[4096]{0:T(1024)} %param.29) | copy-start | bytes 49156
  6.5 89.8 %all-gather.4.cloned.1.call-start = ((), (), s32[]{:S(2)}) async-start(), calls=%async_computation | async-start | bytes 9437184 | tf_op jit(solution)/shard_map/all_gather | solution.py:143
  12.2 21.5 %collective-permute-start.1 = (bf16[8,4096]{1,0:T(8,128)(2,1)}, bf16[8,4096]{1,0:T(8,128)(2,1)S(1)}, u32[]{:S(2)}, u32[]{:S(2)}) collective-permute-start(bf16[8,4096]{1,0:T(8,128)(2,1)} %slice.114), channel_id=1, source_target_pairs={{7,8},{15,16},{23,24}} | collective-permute-start | bytes 196616 | tf_op jit(solution)/shard_map/ppermute | solution.py:34
  12.9 21.5 %collective-permute-start.2 = (bf16[8,4096]{1,0:T(8,128)(2,1)}, bf16[8,4096]{1,0:T(8,128)(2,1)}, u32[]{:S(2)}, u32[]{:S(2)}) collective-permute-start(bf16[8,4096]{1,0:T(8,128)(2,1)} %slice.114), channel_id=1, source_target_pairs={{7,9},{15,17},{23,25}} | collective-permute-start | bytes 196616 | tf_op jit(solution)/shard_map/ppermute | solution.py:34
  14.2 21.8 %collective-permute-start.3 = (bf16[8,4096]{1,0:T(8,128)(2,1)}, bf16[8,4096]{1,0:T(8,128)(2,1)}, u32[]{:S(2)}, u32[]{:S(2)}) collective-permute-start(bf16[8,4096]{1,0:T(8,128)(2,1)} %slice.114), channel_id=1, source_target_pairs={{7,10},{15,18},{23,26}} | collective-permute-start | bytes 196616 | tf_op jit(solution)/shard_map/ppermute | solution.py:34
  15.5 21.2 %collective-permute-start.9 = (bf16[4096,128]{1,0:T(8,128)(2,1)S(1)}, bf16[4096,128]{1,0:T(8,128)(2,1)}, u32[]{:S(2)}, u32[]{:S(2)}) collective-permute-start(bf16[4096,128]{1,0:T(8,128)(2,1)S(1)} %copy-done.5), channel_id=1, source_target_pairs={{0,1},{1,0},{2,3},{3,2},{4,5},{5,4},{6,7},{7,6},{8,9},{9,8},{10,11... | collective-permute-start | bytes 3145736 | tf_op jit(solution)/shard_map/ppermute | solution.py:20
  15.9 15.8 %collective-permute-start = (bf16[4,128]{1,0:T(4,128)(2,1)}, bf16[4,128]{1,0:T(4,128)(2,1)}, u32[]{:S(2)}, u32[]{:S(2)}) collective-permute-start(bf16[4,128]{1,0:T(4,128)(2,1)} %param.25), channel_id=1, source_target_pairs={{0,1},{1,0},{2,3},{3,2},{4,5},{5,4},{6,7},{7,6},{8,9},{9,8},{10,11... | collective-permute-start | bytes 3080 | tf_op jit(solution)/shard_map/ppermute | solution.py:20
  22.3 7.1 %copy-start.15 = (f32[1,4,2,128]{3,2,1,0:T(2,128)S(1)}, f32[1,4,2,128]{3,2,1,0:T(2,128)}, u32[]{:S(2)}) copy-start(f32[1,4,2,128]{3,2,1,0:T(2,128)} %fusion.82) | copy-start | bytes 12292
  22.3 7.1 %copy-start.26 = (f32[4]{0:T(128)S(1)}, f32[4]{0:T(128)}, u32[]{:S(2)}) copy-start(f32[4]{0:T(128)} %param.26) | copy-start | bytes 52
  22.3 7.8 %copy-start.28 = (u32[32]{0:T(128)S(1)}, u32[32]{0:T(128)}, u32[]{:S(2)}) copy-start(u32[32]{0:T(128)} %constant.137) | copy-start | bytes 388
  22.3 10.8 %copy-start.21 = (bf16[4,256]{1,0:T(4,128)(2,1)S(1)}, bf16[4,256]{1,0:T(4,128)(2,1)}, u32[]{:S(2)}) copy-start(bf16[4,256]{1,0:T(4,128)(2,1)} %param.24) | copy-start | bytes 6148
  30.1 10.1 %copy-start.3 = (bf16[512,8,2,256]{3,1,2,0:T(8,128)(2,1)S(1)}, bf16[512,8,2,256]{3,1,2,0:T(8,128)(2,1)}, u32[]{:S(2)}) copy-start(bf16[512,8,2,256]{3,1,2,0:T(8,128)(2,1)} %copy.100) | copy-start | bytes 12582916
  31.8 7.1 %collective-permute-start.4 = (bf16[8,4096]{1,0:T(8,128)(2,1)}, bf16[8,4096]{1,0:T(8,128)(2,1)S(1)}, u32[]{:S(2)}, u32[]{:S(2)}) collective-permute-start(bf16[8,4096]{1,0:T(8,128)(2,1)} %slice.114), channel_id=1, source_target_pairs={{7,11},{15,19},{23,27}} | collective-permute-start | bytes 196616 | tf_op jit(solution)/shard_map/ppermute | solution.py:34
  33.7 5.2 %collective-permute-start.5 = (bf16[8,4096]{1,0:T(8,128)(2,1)}, bf16[8,4096]{1,0:T(8,128)(2,1)S(1)}, u32[]{:S(2)}, u32[]{:S(2)}) collective-permute-start(bf16[8,4096]{1,0:T(8,128)(2,1)} %slice.114), channel_id=1, source_target_pairs={{7,12},{15,20},{23,28}} | collective-permute-start | bytes 196616 | tf_op jit(solution)/shard_map/ppermute | solution.py:34
  34.4 4.5 %collective-permute-start.6 = (bf16[8,4096]{1,0:T(8,128)(2,1)}, bf16[8,4096]{1,0:T(8,128)(2,1)S(1)}, u32[]{:S(2)}, u32[]{:S(2)}) collective-permute-start(bf16[8,4096]{1,0:T(8,128)(2,1)} %slice.114), channel_id=1, source_target_pairs={{7,13},{15,21},{23,29}} | collective-permute-start | bytes 196616 | tf_op jit(solution)/shard_map/ppermute | solution.py:34
  35.9 3.0 %collective-permute-start.7 = (bf16[8,4096]{1,0:T(8,128)(2,1)}, bf16[8,4096]{1,0:T(8,128)(2,1)S(1)}, u32[]{:S(2)}, u32[]{:S(2)}) collective-permute-start(bf16[8,4096]{1,0:T(8,128)(2,1)} %slice.114), channel_id=1, source_target_pairs={{7,14},{15,22},{23,30}} | collective-permute-start | bytes 196616 | tf_op jit(solution)/shard_map/ppermute | solution.py:34
  36.6 2.3 collective-permute-start.8
  40.2 56.2 %copy-start.8 = (bf16[4096,4]{1,0:T(8,128)(2,1)S(1)}, bf16[4096,4]{1,0:T(8,128)(2,1)}, u32[]{:S(2)}) copy-start(bf16[4096,4]{1,0:T(8,128)(2,1)} %copy.98) | copy-start | bytes 98308
  115.2 12.3 %copy-start.19 = (pred[4,256]{1,0:T(4,128)(4,1)S(1)}, pred[4,256]{1,0:T(4,128)(4,1)}, u32[]{:S(2)}) copy-start(pred[4,256]{1,0:T(4,128)(4,1)} %get-tuple-element.233) | copy-start | bytes 3076
  124.9 6.2 %copy-start.16 = (f32[4]{0:T(128)S(1)}, f32[4]{0:T(128)}, u32[]{:S(2)}) copy-start(f32[4]{0:T(128)} %custom-call.1) | copy-start | bytes 52
  124.9 6.2 %copy-start.22 = (f32[4,4]{1,0:T(4,128)S(1)}, f32[4,4]{1,0:T(4,128)}, u32[]{:S(2)}) copy-start(f32[4,4]{1,0:T(4,128)} %custom-call.4) | copy-start | bytes 196
  162.1 6.6 %copy-start.10 = (f32[4,4,64,128]{3,2,1,0:T(8,128)S(1)}, f32[4,4,64,128]{3,2,1,0:T(8,128)}, u32[]{:S(2)}) copy-start(f32[4,4,64,128]{3,2,1,0:T(8,128)} %get-tuple-element.139) | copy-start | bytes 1572868
  173.6 11.6 %copy-start.23 = (f32[256]{0:T(256)S(1)}, f32[256]{0:T(256)}, u32[]{:S(2)}) copy-start(f32[256]{0:T(256)} %param.27) | copy-start | bytes 3076
  179.2 5.3 %collective-permute-start.10 = (f32[1024]{0:T(1024)S(1)}, f32[1024]{0:T(1024)S(1)}, u32[]{:S(2)}, u32[]{:S(2)}) collective-permute-start(f32[1024]{0:T(1024)S(1)} %get-tuple-element.212), channel_id=1, source_target_pairs={{0,1},{1,0},{2,3},{3,2},{4,5},{5,4},{6,7},{7,6},{8,9},{9,8},{10,11... | collective-permute-start | bytes 12296 | tf_op jit(solution)/shard_map/ppermute | solution.py:20
  179.2 15.5 %collective-permute-start.28 = (bf16[256,1024]{1,0:T(8,128)(2,1)S(1)}, bf16[256,1024]{1,0:T(8,128)(2,1)}, u32[]{:S(2)}, u32[]{:S(2)}) collective-permute-start(bf16[256,1024]{1,0:T(8,128)(2,1)S(1)} %constant_dynamic-slice_fusion.4), channel_id=1, source_target_pairs={{0,24},{8,16},{16,8},{24,0},{1,25},{9,17},{17,9},{25,1},{2,26},{10... | collective-permute-start | bytes 1572872 | tf_op jit(solution)/shard_map/ppermute | solution.py:26
  180.3 14.9 %collective-permute-start.12 = (bf16[256,1024]{1,0:T(8,128)(2,1)S(1)}, bf16[256,1024]{1,0:T(8,128)(2,1)}, u32[]{:S(2)}, u32[]{:S(2)}) collective-permute-start(bf16[256,1024]{1,0:T(8,128)(2,1)S(1)} %constant_dynamic-slice_fusion.4), channel_id=1, source_target_pairs={{0,2},{1,3},{2,0},{3,1},{4,6},{5,7},{6,4},{7,5},{8,10},{9,11},{10,... | collective-permute-start | bytes 1572872 | tf_op jit(solution)/shard_map/ppermute | solution.py:26
  180.6 27.9 %collective-permute-start.16 = (bf16[256,1024]{1,0:T(8,128)(2,1)S(1)}, bf16[256,1024]{1,0:T(8,128)(2,1)S(1)}, u32[]{:S(2)}, u32[]{:S(2)}) collective-permute-start(bf16[256,1024]{1,0:T(8,128)(2,1)S(1)} %constant_dynamic-slice_fusion.4), channel_id=1, source_target_pairs={{0,6},{1,7},{2,4},{3,5},{4,2},{5,3},{6,0},{7,1},{8,14},{9,15},{10,... | collective-permute-start | bytes 1572872 | tf_op jit(solution)/shard_map/ppermute | solution.py:26
  184.5 45.0 %collective-permute-start.14 = (bf16[256,1024]{1,0:T(8,128)(2,1)S(1)}, bf16[256,1024]{1,0:T(8,128)(2,1)}, u32[]{:S(2)}, u32[]{:S(2)}) collective-permute-start(bf16[256,1024]{1,0:T(8,128)(2,1)S(1)} %constant_dynamic-slice_fusion.4), channel_id=1, source_target_pairs={{0,4},{1,5},{2,6},{3,7},{4,0},{5,1},{6,2},{7,3},{8,12},{9,13},{10,... | collective-permute-start | bytes 1572872 | tf_op jit(solution)/shard_map/ppermute | solution.py:26
  184.5 24.7 %collective-permute-start.23 = (bf16[256,1024]{1,0:T(8,128)(2,1)S(1)}, bf16[256,1024]{1,0:T(8,128)(2,1)S(1)}, u32[]{:S(2)}, u32[]{:S(2)}) collective-permute-start(bf16[256,1024]{1,0:T(8,128)(2,1)S(1)} %constant_dynamic-slice_fusion.4), channel_id=1, source_target_pairs={{0,16},{8,24},{16,0},{24,8},{1,17},{9,25},{17,1},{25,9},{2,18},{10... | collective-permute-start | bytes 1572872 | tf_op jit(solution)/shard_map/ppermute | solution.py:26
  194.8 17.0 %collective-permute-start.18 = (bf16[256,1024]{1,0:T(8,128)(2,1)S(1)}, bf16[256,1024]{1,0:T(8,128)(2,1)S(1)}, u32[]{:S(2)}, u32[]{:S(2)}) collective-permute-start(bf16[256,1024]{1,0:T(8,128)(2,1)S(1)} %constant_dynamic-slice_fusion.4), channel_id=1, source_target_pairs={{0,8},{8,0},{16,24},{24,16},{1,9},{9,1},{17,25},{25,17},{2,10},{10... | collective-permute-start | bytes 1572872 | tf_op jit(solution)/shard_map/ppermute | solution.py:26
  195.3 35.2 %collective-permute-start.29 = (bf16[256,1024]{1,0:T(8,128)(2,1)}, bf16[256,1024]{1,0:T(8,128)(2,1)S(1)}, u32[]{:S(2)}, u32[]{:S(2)}) collective-permute-start(bf16[256,1024]{1,0:T(8,128)(2,1)} %collective-permute-done.12), channel_id=1, source_target_pairs={{0,24},{8,16},{16,8},{24,0},{1,25},{9,17},{17,9},{25,1},{2,26},{10... | collective-permute-start | bytes 1572872 | tf_op jit(solution)/shard_map/ppermute | solution.py:26
  208.5 73.4 %collective-permute-start.24 = (bf16[256,1024]{1,0:T(8,128)(2,1)}, bf16[256,1024]{1,0:T(8,128)(2,1)S(1)}, u32[]{:S(2)}, u32[]{:S(2)}) collective-permute-start(bf16[256,1024]{1,0:T(8,128)(2,1)} %collective-permute-done.12), channel_id=1, source_target_pairs={{0,16},{8,24},{16,0},{24,8},{1,17},{9,25},{17,1},{25,9},{2,18},{10... | collective-permute-start | bytes 1572872 | tf_op jit(solution)/shard_map/ppermute | solution.py:26
  209.2 26.0 %collective-permute-start.31 = (bf16[256,1024]{1,0:T(8,128)(2,1)S(1)}, bf16[256,1024]{1,0:T(8,128)(2,1)S(1)}, u32[]{:S(2)}, u32[]{:S(2)}) collective-permute-start(bf16[256,1024]{1,0:T(8,128)(2,1)S(1)} %collective-permute-done.16), channel_id=1, source_target_pairs={{0,24},{8,16},{16,8},{24,0},{1,25},{9,17},{17,9},{25,1},{2,26},{10... | collective-permute-start | bytes 1572872 | tf_op jit(solution)/shard_map/ppermute | solution.py:26
  211.8 20.7 %collective-permute-start.11 = (bf16[256,256]{1,0:T(8,128)(2,1)S(1)}, bf16[256,256]{1,0:T(8,128)(2,1)S(1)}, u32[]{:S(2)}, u32[]{:S(2)}) collective-permute-start(bf16[256,256]{1,0:T(8,128)(2,1)S(1)} %get-tuple-element.226), channel_id=1, source_target_pairs={{0,2},{1,3},{2,0},{3,1},{4,6},{5,7},{6,4},{7,5},{8,10},{9,11},{10,... | collective-permute-start | bytes 393224 | tf_op jit(solution)/shard_map/ppermute | solution.py:26
  229.5 51.5 %collective-permute-start.26 = (bf16[256,1024]{1,0:T(8,128)(2,1)S(1)}, bf16[256,1024]{1,0:T(8,128)(2,1)S(1)}, u32[]{:S(2)}, u32[]{:S(2)}) collective-permute-start(bf16[256,1024]{1,0:T(8,128)(2,1)S(1)} %collective-permute-done.16), channel_id=1, source_target_pairs={{0,16},{8,24},{16,0},{24,8},{1,17},{9,25},{17,1},{25,9},{2,18},{10... | collective-permute-start | bytes 1572872 | tf_op jit(solution)/shard_map/ppermute | solution.py:26
  230.4 16.0 %collective-permute-start.30 = (bf16[256,1024]{1,0:T(8,128)(2,1)}, bf16[256,1024]{1,0:T(8,128)(2,1)S(1)}, u32[]{:S(2)}, u32[]{:S(2)}) collective-permute-start(bf16[256,1024]{1,0:T(8,128)(2,1)} %collective-permute-done.14), channel_id=1, source_target_pairs={{0,24},{8,16},{16,8},{24,0},{1,25},{9,17},{17,9},{25,1},{2,26},{10... | collective-permute-start | bytes 1572872 | tf_op jit(solution)/shard_map/ppermute | solution.py:26
  232.5 6.8 %collective-permute-start.15 = (bf16[256,256]{1,0:T(8,128)(2,1)S(1)}, bf16[256,256]{1,0:T(8,128)(2,1)S(1)}, u32[]{:S(2)}, u32[]{:S(2)}) collective-permute-start(bf16[256,256]{1,0:T(8,128)(2,1)S(1)} %get-tuple-element.225), channel_id=1, source_target_pairs={{0,6},{1,7},{2,4},{3,5},{4,2},{5,3},{6,0},{7,1},{8,14},{9,15},{10,... | collective-permute-start | bytes 393224 | tf_op jit(solution)/shard_map/ppermute | solution.py:26
  235.2 22.1 %collective-permute-start.21 = (bf16[256,1024]{1,0:T(8,128)(2,1)S(1)}, bf16[256,1024]{1,0:T(8,128)(2,1)S(1)}, u32[]{:S(2)}, u32[]{:S(2)}) collective-permute-start(bf16[256,1024]{1,0:T(8,128)(2,1)S(1)} %collective-permute-done.16), channel_id=1, source_target_pairs={{0,8},{8,0},{16,24},{24,16},{1,9},{9,1},{17,25},{25,17},{2,10},{10... | collective-permute-start | bytes 1572872 | tf_op jit(solution)/shard_map/ppermute | solution.py:26
  239.3 8.2 %collective-permute-start.13 = (bf16[256,256]{1,0:T(8,128)(2,1)S(1)}, bf16[256,256]{1,0:T(8,128)(2,1)S(1)}, u32[]{:S(2)}, u32[]{:S(2)}) collective-permute-start(bf16[256,256]{1,0:T(8,128)(2,1)S(1)} %get-tuple-element.224), channel_id=1, source_target_pairs={{0,4},{1,5},{2,6},{3,7},{4,0},{5,1},{6,2},{7,3},{8,12},{9,13},{10,... | collective-permute-start | bytes 393224 | tf_op jit(solution)/shard_map/ppermute | solution.py:26
  246.4 35.8 %collective-permute-start.25 = (bf16[256,1024]{1,0:T(8,128)(2,1)}, bf16[256,1024]{1,0:T(8,128)(2,1)S(1)}, u32[]{:S(2)}, u32[]{:S(2)}) collective-permute-start(bf16[256,1024]{1,0:T(8,128)(2,1)} %collective-permute-done.14), channel_id=1, source_target_pairs={{0,16},{8,24},{16,0},{24,8},{1,17},{9,25},{17,1},{25,9},{2,18},{10... | collective-permute-start | bytes 1572872 | tf_op jit(solution)/shard_map/ppermute | solution.py:26
  247.5 21.0 %collective-permute-start.19 = (bf16[256,1024]{1,0:T(8,128)(2,1)}, bf16[256,1024]{1,0:T(8,128)(2,1)S(1)}, u32[]{:S(2)}, u32[]{:S(2)}) collective-permute-start(bf16[256,1024]{1,0:T(8,128)(2,1)} %collective-permute-done.12), channel_id=1, source_target_pairs={{0,8},{8,0},{16,24},{24,16},{1,9},{9,1},{17,25},{25,17},{2,10},{10... | collective-permute-start | bytes 1572872 | tf_op jit(solution)/shard_map/ppermute | solution.py:26
  257.3 20.2 %collective-permute-start.20 = (bf16[256,1024]{1,0:T(8,128)(2,1)}, bf16[256,1024]{1,0:T(8,128)(2,1)S(1)}, u32[]{:S(2)}, u32[]{:S(2)}) collective-permute-start(bf16[256,1024]{1,0:T(8,128)(2,1)} %collective-permute-done.14), channel_id=1, source_target_pairs={{0,8},{8,0},{16,24},{24,16},{1,9},{9,1},{17,25},{25,17},{2,10},{10... | collective-permute-start | bytes 1572872 | tf_op jit(solution)/shard_map/ppermute | solution.py:26
  268.5 15.8 %collective-permute-start.32 = (bf16[128,1024]{1,0:T(8,128)(2,1)S(1)}, bf16[128,1024]{1,0:T(8,128)(2,1)S(1)}, u32[]{:S(2)}, u32[]{:S(2)}) collective-permute-start(bf16[128,1024]{1,0:T(8,128)(2,1)S(1)} %dynamic-slice_convert_fusion), channel_id=1, source_target_pairs={{0,1},{1,0},{2,3},{3,2},{4,5},{5,4},{6,7},{7,6},{8,9},{9,8},{10,11... | collective-permute-start | bytes 786440 | tf_op jit(solution)/shard_map/ppermute | solution.py:26
  277.9 5.3 %collective-permute-start.22 = (bf16[128,1024]{1,0:T(8,128)(2,1)S(1)}, bf16[128,1024]{1,0:T(8,128)(2,1)S(1)}, u32[]{:S(2)}, u32[]{:S(2)}) collective-permute-start(bf16[128,1024]{1,0:T(8,128)(2,1)S(1)} %dynamic-slice_convert_fusion.2), channel_id=1, source_target_pairs={{0,1},{1,0},{2,3},{3,2},{4,5},{5,4},{6,7},{7,6},{8,9},{9,8},{10,11... | collective-permute-start | bytes 786440 | tf_op jit(solution)/shard_map/ppermute | solution.py:26
  281.0 1.7 collective-permute-start.17
  282.6 1.6 collective-permute-start.27
  (15 other events, 41.4 us)
Sparse Core Ops, SparseCore 0:
  10.9 85.4 all-gather.3

commit v2 on v1

v2 whole, which is shorter than its diff:
```python
import jax
import jax.numpy as jnp
from jax import lax
from jax.experimental import pallas as pl
from jax.experimental.pallas import tpu as pltpu
from jax.sharding import PartitionSpec as P

STRETCH = 128
LANES = 128


EPS = 1e-05
HIGH = lax.Precision.HIGHEST


def swapped(block, axis, stride):
    count = lax.axis_size(axis)
    route = []
    for low in range(count):
        high = low | 1 << stride
        if high != low and high < count:
            route += [(low, high), (high, low)]
    return lax.ppermute(block, axis, route)


def crossed(block, axis, mask):
    if mask == 0:
        return block
    return lax.ppermute(block, axis, [(i, i ^ mask) for i in range(lax.axis_size(axis))])


def tail_of_previous(block):
    spans, parts = lax.axis_size("seq"), lax.axis_size("tp")
    total = None
    for part in range(parts):
        route = [(i * parts - 1, i * parts + part) for i in range(1, spans)]
        got = lax.ppermute(block, ("seq", "tp"), route)
        total = got if total is None else total + got
    return total


def spread_weight(weight, spans, chips):
    cols = weight.shape[1] // spans
    own = lax.dynamic_slice_in_dim(weight, lax.axis_index("seq") * cols, cols, axis=1)
    along = [crossed(own, "tp", 2 * d) for d in range(chips)]
    return [[crossed(part, "seq", e) for part in along] for e in range(spans)]


def silu(v):
    return v / (1.0 + jnp.exp(-v))


def widen(cols, heads, head_dim):
    rows = cols.shape[0]
    parts = [jnp.broadcast_to(cols[:, h : h + 1], (rows, head_dim)) for h in range(heads)]
    return jnp.concatenate(parts, axis=1)


def dot16(a, b, dims=((1,), (0,))):
    a, b = a.astype(jnp.bfloat16), b.astype(jnp.bfloat16)
    return lax.dot_general(a, b, (dims, ((), ())), preferred_element_type=jnp.float32)


def scan_kernel(
    heads, proj, before, aux, row_seg, taps, bias, rate, skip, y_out, c_out, w_out, s_out,
    edge, state, total,
):
    size, inner = y_out.shape
    states = c_out.shape[1]
    head_dim = inner // heads
    step_at = pl.program_id(0)

    @pl.when(step_at == 0)
    def _():
        edge[...] = before[...]
        state[...] = jnp.zeros_like(state)
        total[...] = jnp.zeros_like(total)

    conv = inner + 2 * states
    cur = proj[:, :conv]
    both = jnp.concatenate([edge[...], cur], axis=0)
    edge[...] = cur[size - 8 :]
    tap = taps[...]
    count = tap.shape[0]
    acc = tap[count - 1 : count] * cur
    for back in range(1, count):
        same = aux[:, back : back + 1]
        acc += tap[count - 1 - back : count - back] * both[8 - back : 8 - back + size] * same
    active = silu(acc)
    x = active[:, :inner]
    b_map = active[:, inner : inner + states]
    c_map = active[:, inner + states :]
    raw = proj[:, conv + inner :] + bias[...]
    step = jnp.maximum(raw, 0.0) + jnp.log1p(jnp.exp(-jnp.abs(raw)))
    log_decay = -step * rate[...]
    row_at = lax.broadcasted_iota(jnp.int32, (size, size), 0)
    col_at = lax.broadcasted_iota(jnp.int32, (size, size), 1)
    causal = row_at >= col_at
    cum = jnp.dot(
        causal.astype(jnp.float32), log_decay, precision=HIGH, preferred_element_type=jnp.float32
    )
    cum_rows = cum.T
    alive, in_last, alive_span = aux[:, 4:5], aux[:, 5:6], aux[:, 6:7]
    last = cum[size - 1 :]
    mask = causal & (aux[:, 0:1] == row_seg[0:1, :])
    xs = x * widen(step, heads, head_dim)
    xs16 = xs.astype(jnp.bfloat16)
    products = dot16(c_map, b_map, ((1,), (1,)))
    parts = []
    for h in range(heads):
        gap = cum[:, h : h + 1] - cum_rows[h : h + 1, :]
        mixing = products * jnp.exp(jnp.where(mask, gap, -1e30))
        parts.append(dot16(mixing, xs16[:, h * head_dim : (h + 1) * head_dim]))
    local = jnp.concatenate(parts, axis=1)
    entry = jnp.exp(cum) * alive
    carried = dot16(c_map, state[...]) * widen(entry, heads, head_dim)
    y_out[...] = local + carried + skip[...] * x
    c_out[...] = c_map.astype(jnp.bfloat16)
    w_span = jnp.exp(cum + total[...]) * alive_span
    w_out[...] = w_span
    end = jnp.exp(last - cum) * in_last
    fresh = dot16(b_map, xs * widen(end, heads, head_dim), ((0,), (0,)))
    state[...] = widen(entry[size - 1 :], heads, head_dim) * state[...] + fresh
    total[...] = total[...] + last

    @pl.when(step_at == pl.num_programs(0) - 1)
    def _():
        s_out[0:states] = state[...]
        s_out[states:] = jnp.broadcast_to(
            widen(w_span[size - 1 :], heads, head_dim), (8, inner)
        )


def local_scan(heads, states, proj, before, aux, row_seg, taps, bias, rate, skip):
    length = proj.shape[0]
    inner = skip.shape[1]
    whole = lambda a: pl.BlockSpec(a.shape, lambda i: (0,) * a.ndim)
    rows = lambda n: pl.BlockSpec((STRETCH, n), lambda i: (i, 0))
    return pl.pallas_call(
        lambda *refs: scan_kernel(heads, *refs),
        grid=(length // STRETCH,),
        in_specs=[
            rows(proj.shape[1]),
            whole(before),
            rows(aux.shape[1]),
            pl.BlockSpec((8, STRETCH), lambda i: (0, i)),
            whole(taps),
            whole(bias),
            whole(rate),
            whole(skip),
        ],
        out_specs=[
            rows(inner),
            rows(states),
            rows(LANES),
            pl.BlockSpec((states + 8, inner), lambda i: (0, 0)),
        ],
        out_shape=[
            jax.ShapeDtypeStruct((length, inner), jnp.float32),
            jax.ShapeDtypeStruct((length, states), jnp.bfloat16),
            jax.ShapeDtypeStruct((length, LANES), jnp.float32),
            jax.ShapeDtypeStruct((states + 8, inner), jnp.float32),
        ],
        scratch_shapes=[
            pltpu.VMEM((8, inner + 2 * states), jnp.float32),
            pltpu.VMEM((states, inner), jnp.float32),
            pltpu.VMEM((1, LANES), jnp.float32),
        ],
        compiler_params=pltpu.CompilerParams(vmem_limit_bytes=32 << 20),
        cost_estimate=pl.CostEstimate(
            flops=12_000_000_000, bytes_accessed=8_000_000, transcendentals=4_000_000
        ),
        name="local_scan",
    )(proj, before, aux, row_seg, taps, bias, rate, skip)


def gate_kernel(heads, y, c, w, gate, state, gated_out, sq_out):
    head_dim = y.shape[1] // heads
    carried = dot16(c[...], state[...]) * widen(w[...], heads, head_dim)
    gated = (y[...] + carried) * silu(gate[...])
    gated_out[...] = gated
    sq_out[...] = jnp.sum(gated * gated, axis=1, keepdims=True)


def gate_all(heads, y, c, w, proj, gate_block, state):
    length, inner = y.shape
    size = 256
    rows = lambda n: pl.BlockSpec((size, n), lambda i: (i, 0))
    return pl.pallas_call(
        lambda *refs: gate_kernel(heads, *refs),
        grid=(length // size,),
        in_specs=[
            rows(inner),
            rows(c.shape[1]),
            rows(LANES),
            pl.BlockSpec((size, inner), lambda i: (i, gate_block)),
            pl.BlockSpec(state.shape, lambda i: (0, 0)),
        ],
        out_specs=[rows(inner), rows(1)],
        out_shape=[
            jax.ShapeDtypeStruct((length, inner), jnp.float32),
            jax.ShapeDtypeStruct((length, 1), jnp.float32),
        ],
        compiler_params=pltpu.CompilerParams(vmem_limit_bytes=32 << 20),
        name="gate_all",
    )(y, c, w, proj, state)


def entering_state(packed, states):
    spans = lax.axis_size("seq")
    got = [
        lax.ppermute(packed, "seq", [(i, i + e) for i in range(spans - e)])
        for e in range(1, spans)
    ]
    total = jnp.zeros((states, packed.shape[1]), jnp.float32)
    for part in reversed(got):
        total = part[:states] + part[states : states + 1] * total
    return total


def project_out(hidden, mixed, weights):
    rows, spans, chips = hidden.shape[0], len(weights), len(weights[0])
    chip, core = lax.axis_index("tp") // 2, lax.axis_index("tp") % 2
    span = lax.axis_index("seq")
    cols = hidden.shape[1] // spans
    taken = []
    for d in range(chips):
        block = lax.dynamic_slice_in_dim(mixed, (chip ^ d) * 2 * rows, 2 * rows, axis=0)
        taken.append(crossed(block, "tp", 2 * d))
    out = jnp.zeros(hidden.shape, jnp.bfloat16)
    for e in range(spans):
        part = sum(
            jnp.dot(m, w, preferred_element_type=jnp.float32) for m, w in zip(taken, weights[e])
        )
        own = lax.dynamic_slice_in_dim(part, core * rows, rows, axis=0)
        other = lax.dynamic_slice_in_dim(part, (1 - core) * rows, rows, axis=0)
        other = crossed(other.astype(jnp.bfloat16), "tp", 1).astype(jnp.float32)
        start = (span ^ e) * cols
        base = lax.dynamic_slice_in_dim(hidden, start, cols, axis=1).astype(jnp.float32)
        done = (base + own + other).astype(jnp.bfloat16)
        out = lax.dynamic_update_slice_in_dim(out, done, start, axis=1)
    return out


def body(
    hidden,
    norm_gain,
    inner_weight,
    group_weight,
    step_weight,
    step_bias,
    decay_rate,
    filter_inner,
    filter_group,
    skip_gain,
    mixer_gain,
    output_weight,
    segment_ids,
):
    rows = hidden.shape[0]
    length = rows * lax.axis_size("tp")
    width = hidden.shape[1]
    inner_dev = inner_weight.shape[2]
    heads_dev = step_weight.shape[1]
    head_dim = inner_dev // heads_dev
    state_dim = group_weight.shape[1]
    taps = filter_inner.shape[0]
    first_row = lax.axis_index("seq") * length
    is_first = lax.axis_index("tp") % 2 == 0
    hidden_f = hidden.astype(jnp.float32)
    normed = (
        hidden_f
        * lax.rsqrt(jnp.mean(hidden_f * hidden_f, axis=-1, keepdims=True) + EPS)
        * norm_gain
    ).astype(jnp.bfloat16)
    other_weight, other_filter = swapped((group_weight, filter_group), "tp", 0)
    group_cols = (
        jnp.where(is_first, group_weight, other_weight),
        jnp.where(is_first, other_weight, group_weight),
    )
    filters = jnp.concatenate(
        [
            filter_inner,
            jnp.where(is_first, filter_group, other_filter),
            jnp.where(is_first, other_filter, filter_group),
        ],
        axis=1,
    )
    spans, chips = lax.axis_size("seq"), lax.axis_size("tp") // 2
    weights = spread_weight(output_weight, spans, chips)
    tail = tail_of_previous(normed[rows - 8 :])
    pad_heads = ((0, 0), (0, LANES - heads_dev))
    matrix = jnp.concatenate(
        (inner_weight[:, 1, :],)
        + group_cols
        + (inner_weight[:, 0, :], jnp.pad(step_weight, pad_heads)),
        axis=1,
    )
    conv_dim = inner_dev + 2 * state_dim
    before = jnp.dot(tail, matrix[:, :conv_dim], preferred_element_type=jnp.float32)
    seg_pad = jnp.concatenate([jnp.full((taps - 1,), -1, jnp.int32), segment_ids])
    seg_ext = lax.dynamic_slice_in_dim(seg_pad, first_row, length + taps - 1)
    seg = seg_ext[taps - 1 :]
    span_before = seg_ext[taps - 2]
    chunked = seg.reshape(-1, STRETCH)
    chunk_before = jnp.concatenate([span_before[None], chunked[:-1, -1]])
    columns = [seg]
    columns += [seg == seg_ext[taps - 1 - back : taps - 1 - back + length] for back in range(1, taps)]
    columns += [
        (chunked == chunk_before[:, None]).reshape(-1),
        (chunked == chunked[:, -1:]).reshape(-1),
        seg == span_before,
    ]
    columns += [jnp.zeros_like(seg)] * (8 - len(columns))
    row_form = jnp.stack([column.astype(jnp.float32) for column in columns])
    row_seg = row_form
    aux = row_form.T
    bias = jnp.pad(step_bias[None], pad_heads)
    rate = jnp.pad(decay_rate[None], pad_heads)
    skip = jnp.repeat(skip_gain, head_dim)[None]
    matrix, before, aux, row_seg = lax.optimization_barrier((matrix, before, aux, row_seg))
    piece = lax.all_gather(normed, "tp", axis=0, tiled=True)
    piece, near = lax.optimization_barrier((piece, weights[:3]))
    projected = jnp.dot(piece, matrix, preferred_element_type=jnp.float32)
    y, c_map, w_span, packed = local_scan(
        heads_dev, state_dim, projected, before, aux, row_seg, filters.astype(jnp.float32),
        bias, rate, skip,
    )
    incoming = entering_state(packed, state_dim)
    gated, squares = gate_all(
        heads_dev, y, c_map, w_span, projected, conv_dim // inner_dev, incoming
    )
    gated, far = lax.optimization_barrier((gated, weights[3:]))
    weights = near + far
    own_squares = squares[:, 0]
    other_squares = swapped(own_squares, "tp", 0)
    group_mean = (own_squares + other_squares) / (2 * inner_dev)
    mixed = (gated * lax.rsqrt(group_mean + EPS)[:, None] * mixer_gain).astype(jnp.bfloat16)
    return project_out(hidden, mixed, weights)


def solution(mesh):
    in_specs = (
        P(("seq", "tp"), None),
        P(),
        P(None, None, "tp"),
        P(None, "tp"),
        P(None, "tp"),
        P("tp"),
        P("tp"),
        P(None, "tp"),
        P(None, "tp"),
        P("tp"),
        P("tp"),
        P("tp", None),
        P(),
    )
    out_specs = P(("seq", "tp"), None)
    return jax.shard_map(body, mesh=mesh, in_specs=in_specs, out_specs=out_specs, check_vma=False)
```

time: 294 us -> 286 us (0.973)
  waiting for transfers between devices: 115 us -> 152 us
  other arithmetic: 36.4 us -> 11.2 us
  blocking collectives: 19.7 us -> 0 us
  Pallas kernels: 0 us -> 12.3 us
  local copies, waits for them, and re-layouts: 30 us -> 23.1 us
  matrix products: 35.1 us -> 29.4 us
    ppermute x22, waiting for transfers between devices: 60.6 us -> 119 us  [crossed(): lax.ppermute(block, axis, [(i, i ^ mask) for i in range(lax.axis_size(axi...]
    all_gather x1, waiting for transfers between devices: 54.6 us -> 0.01 us  [body(): piece = lax.all_gather(normed, 'tp', axis=0, tiled=True)]
    ppermute x0 -> x3, waiting for transfers between devices: none -> 32.6 us  [entering_state(): lax.ppermute(packed, 'seq', [(i, i + e) for i in range(spans - e)])]
    dot_general x5 -> x1, matrix products: 13.1 us -> 0.65 us  [body(): jnp.dot(tail, matrix[:, :conv_dim], preferred_element_type=jnp.float32)]
    pallas_call x0 -> x2, Pallas kernels: none -> 12.3 us  [the longest x1 10.9 us: local_scan(): pl.pallas_call(lambda *refs: scan_kernel(heads, *refs), grid=(length // S...]
    all_gather x1 -> x0, blocking collectives: 10.6 us -> none  [entering_2(): pieces = jax.tree.map(lambda part: lax.all_gather(part, axis), value)]
    unnamed x1 -> x0, blocking collectives: 9.13 us -> none
    dot_general x16, matrix products: 7.96 us -> 16.4 us  [project_out(): jnp.dot(m, w, preferred_element_type=jnp.float32)]
  transfers between devices with their start and end apart: 34 -> 37, of which waited for: 11 -> 11; matrix products, arithmetic and copies ran while one was open for 11% -> 14% of each run, Pallas kernels for 0% -> 0%
where the time goes in v2:
time: 286 us; the launch traced here: 285 us
  waiting for transfers between devices  152 us (53%)
  starting transfers between devices  42.8 us (15%)
  matrix products  29.4 us (10%)
  local copies, waits for them, and re-layouts  23.1 us (8%)
  between operations  14.2 us (5%)
  Pallas kernels  12.3 us (4%)
  other arithmetic  11.2 us (4%)
    ppermute x22, waiting for transfers between devices, crossed(): lax.ppermute(block, axis, [(i, i ^ mask) for i in range(lax.axis_size(axi...  119 us
    ppermute x3, waiting for transfers between devices, entering_state(): lax.ppermute(packed, 'seq', [(i, i + e) for i in range(spans - e)])  32.6 us
    ppermute x22, starting transfers between devices, crossed(): lax.ppermute(block, axis, [(i, i ^ mask) for i in range(lax.axis_size(axi...  29.3 us
    dot_general x16, matrix products, project_out(): jnp.dot(m, w, preferred_element_type=jnp.float32)  16.4 us
    dot_general x1, matrix products, body(): projected = jnp.dot(piece, matrix, preferred_element_type=jnp.float32)  12.3 us
    pallas_call x1, Pallas kernels, local_scan(): pl.pallas_call(lambda *refs: scan_kernel(heads, *refs), grid=(length // S...  10.9 us
    slice x1, local copies, waits for them, and re-layouts, body(): inner_weight[:, 0, :]  10.1 us
    unnamed x51, local copies, waits for them, and re-layouts  8.16 us
  transfers between devices with their start and end apart: 37, of which 11 were waited for; matrix products, arithmetic and copies ran while one was open for 14% of the time, Pallas kernels for 0%

profile of v2, /device:TPU:0, one launch (start us, length us, event | category | flops | bytes accessed | tf_op | source)
XLA Modules:
  0.0 284.9 jit_solution(13426110103279931357)
XLA Ops:
  6.6 1.7 fusion.6
  8.3 2.5 fusion.8
  10.8 0.8 slice.66
  14.3 1.4 copy.23
  17.7 0.9 constant_dynamic-slice_fusion.3
  19.3 10.1 %fusion.52 = (bf16[4096,1,256]{2,1,0:T(2,128)(2,1)}, bf16[4096,1,256]{2,1,0:T(2,128)(2,1)S(1)}) fusion(bf16[4096,2,256]{2,1,0:T(2,128)(2,1)} %param.15), kind=kLoop, calls=%fused_computation.97 | loop fusion | bytes 8388608 | tf_op jit(solution)/shard_map/slice | solution.py:296
  29.5 2.5 constant_dynamic-update-slice_fusion.2
  33.7 1.3 constant_dynamic-update-slice_fusion.1
  37.2 8.5 %collective-permute-start.2 = (bf16[256,1024]{1,0:T(8,128)(2,1)S(1)}, bf16[256,1024]{1,0:T(8,128)(2,1)}, u32[]{:S(2)}, u32[]{:S(2)}) collective-permute-start(bf16[256,1024]{1,0:T(8,128)(2,1)S(1)} %copy-done.6), channel_id=1, source_target_pairs={{0,6},{1,7},{2,4},{3,5},{4,2},{5,3},{6,0},{7,1},{8,14},{9,15},{10,... | collective-permute-start | bytes 1572872 | tf_op jit(solution)/shard_map/ppermute | solution.py:29
  45.7 2.6 constant_dynamic-update-slice_fusion
  48.9 2.1 collective-permute-start.3
  51.1 17.7 %collective-permute-done.2 = bf16[256,1024]{1,0:T(8,128)(2,1)} collective-permute-done((bf16[256,1024]{1,0:T(8,128)(2,1)S(1)}, bf16[256,1024]{1,0:T(8,128)(2,1)}, u32[]{:S(2)}, u32[]{:S(2)}) %collective-permute-start.2) | collective-permute-done | bytes 524320 | tf_op jit(solution)/shard_map/ppermute | solution.py:29
  68.8 2.7 collective-permute-start.10
  71.5 1.8 fusion.9
  73.3 22.9 %collective-permute-done = bf16[256,1024]{1,0:T(8,128)(2,1)} collective-permute-done((bf16[256,1024]{1,0:T(8,128)(2,1)S(1)}, bf16[256,1024]{1,0:T(8,128)(2,1)}, u32[]{:S(2)}, u32[]{:S(2)}) %collective-permute-start) | collective-permute-done | bytes 524320 | tf_op jit(solution)/shard_map/ppermute | solution.py:29
  96.2 2.6 collective-permute-start.6
  98.7 37.9 %collective-permute-done.1 = bf16[256,1024]{1,0:T(8,128)(2,1)} collective-permute-done((bf16[256,1024]{1,0:T(8,128)(2,1)S(1)}, bf16[256,1024]{1,0:T(8,128)(2,1)}, u32[]{:S(2)}, u32[]{:S(2)}) %collective-permute-start.1) | collective-permute-done | bytes 524320 | tf_op jit(solution)/shard_map/ppermute | solution.py:29
  136.7 1.5 collective-permute-start.4
  138.1 1.2 collective-permute-start.8
  142.0 1.3 pad_dynamic-update-slice_fusion
  143.5 8.3 %collective-permute-done.4 = bf16[256,1024]{1,0:T(8,128)(2,1)} collective-permute-done((bf16[256,1024]{1,0:T(8,128)(2,1)}, bf16[256,1024]{1,0:T(8,128)(2,1)}, u32[]{:S(2)}, u32[]{:S(2)}) %collective-permute-start.4) | collective-permute-done | bytes 524320 | tf_op jit(solution)/shard_map/ppermute | solution.py:29
  151.8 11.0 %collective-permute-done.5 = bf16[256,1024]{1,0:T(8,128)(2,1)} collective-permute-done((bf16[256,1024]{1,0:T(8,128)(2,1)}, bf16[256,1024]{1,0:T(8,128)(2,1)}, u32[]{:S(2)}, u32[]{:S(2)}) %collective-permute-start.5) | collective-permute-done | bytes 524320 | tf_op jit(solution)/shard_map/ppermute | solution.py:29
  162.8 1.4 collective-permute-done.9
  164.9 12.3 %fusion.53.refs_0_.refs_3_ = f32[1024,896]{1,0:T(8,128)S(1)} fusion(bf16[1024,4096]{1,0:T(8,128)(2,1)} %all-gather.2.cloned.1.call-done, bf16[4096,896]{1,0:T(8,128)(2,1)} %pad_dynamic-update-slice_fusion), kind=kOutput, calls=%fused_computation.98 | convolution fusion | flops 7516192768 | bytes 19398656 | tf_op jit(solution)/shard_map/dot_general | solution.py:324
  177.3 10.9 %local_scan.1 = (f32[1024,256]{1,0:T(8,128)S(1)}, bf16[1024,128]{1,0:T(8,128)(2,1)S(1)}, f32[1024,128]{1,0:T(8,128)S(1)}, f32[136,256]{1,0:T(8,128)S(1)}) custom-call(f32[1024,896]{1,0:T(8,128)S(1)} %fusion.53.refs_0_.refs_3_, f32[8,512]{1,0:T(8,128)S(1)} %fusion.refs_1_, f32[1024,8]{1,0:T(8,128)S(1)} %copy.24.refs_2_, f32[8,1024]{1,0:T(8,128)S(1)} %stack.59.refs_3_, ...), custom_call_target="tpu_custom_call" | custom-call | flops 12000000000 | bytes 8000000 | tf_op jit(solution)/shard_map/local_scan/pallas_call | solution.py:139
  188.1 2.7 collective-permute-start.21
  190.9 3.1 %collective-permute-start.22 = (f32[136,256]{1,0:T(8,128)S(1)}, f32[136,256]{1,0:T(8,128)S(1)}, u32[]{:S(2)}, u32[]{:S(2)}) collective-permute-start(f32[136,256]{1,0:T(8,128)S(1)} %get-tuple-element.41), channel_id=1, source_target_pairs={{0,16},{8,24},{1,17},{9,25},{2,18},{10,26},{3,19},{11,27},{4,20},{... | collective-permute-start | bytes 417800 | tf_op jit(solution)/shard_map/ppermute | solution.py:212
  194.0 1.5 collective-permute-start.23
  195.5 2.9 %collective-permute-start.25 = (bf16[256,1024]{1,0:T(8,128)(2,1)}, bf16[256,1024]{1,0:T(8,128)(2,1)}, u32[]{:S(2)}, u32[]{:S(2)}) collective-permute-start(bf16[256,1024]{1,0:T(8,128)(2,1)} %collective-permute-done), channel_id=1, source_target_pairs={{0,24},{8,16},{16,8},{24,0},{1,25},{9,17},{17,9},{25,1},{2,26},{10... | collective-permute-start | bytes 1572872 | tf_op jit(solution)/shard_map/ppermute | solution.py:29
  198.5 32.5 %collective-permute-done.22 = f32[136,256]{1,0:T(8,128)S(1)} collective-permute-done((f32[136,256]{1,0:T(8,128)S(1)}, f32[136,256]{1,0:T(8,128)S(1)}, u32[]{:S(2)}, u32[]{:S(2)}) %collective-permute-start.22) | collective-permute-done | bytes 139296 | tf_op jit(solution)/shard_map/ppermute | solution.py:212
  231.2 1.4 gate_all.1
  232.9 12.7 %collective-permute-done.27 = bf16[256,1024]{1,0:T(8,128)(2,1)} collective-permute-done((bf16[256,1024]{1,0:T(8,128)(2,1)}, bf16[256,1024]{1,0:T(8,128)(2,1)}, u32[]{:S(2)}, u32[]{:S(2)}) %collective-permute-start.27) | collective-permute-done | bytes 524320 | tf_op jit(solution)/shard_map/ppermute | solution.py:29
  246.0 2.8 collective-permute-start.30
  248.8 1.5 collective-permute-start.31
  250.3 1.2 collective-permute-done.29
  251.5 1.3 fusion.63
  252.9 5.4 %collective-permute-done.30 = bf16[256,256]{1,0:T(8,128)(2,1)S(1)} collective-permute-done((bf16[256,256]{1,0:T(8,128)(2,1)S(1)}, bf16[256,256]{1,0:T(8,128)(2,1)S(1)}, u32[]{:S(2)}, u32[]{:S(2)}) %collective-permute-start.30) | collective-permute-done | bytes 131104 | tf_op jit(solution)/shard_map/ppermute | solution.py:29
  258.3 1.3 fusion.64
  259.7 1.3 fusion.65
  261.0 1.4 fusion.11
  262.6 1.3 fusion.57
  263.9 1.3 fusion.58
  265.3 1.3 fusion.59
  267.5 1.3 fusion.54
  268.9 1.3 fusion.55
  270.2 1.4 fusion.56
  272.1 1.3 fusion.60
  276.3 0.9 copy-done.9
  (139 shorter events, 19.2 us)
Async XLA Ops:
  6.5 11.1 %copy-start = (bf16[256,4096]{1,0:T(8,128)(2,1)S(1)}, bf16[256,4096]{1,0:T(8,128)(2,1)}, u32[]{:S(2)}) copy-start(bf16[256,4096]{1,0:T(8,128)(2,1)} %param.24) | copy-start | bytes 6291460
  6.5 7.2 %copy-start.4 = (bf16[4096,128]{1,0:T(8,128)(2,1)S(1)}, bf16[4096,128]{1,0:T(8,128)(2,1)}, u32[]{:S(2)}) copy-start(bf16[4096,128]{1,0:T(8,128)(2,1)} %param.16) | copy-start | bytes 3145732
  6.5 7.7 %copy-start.19 = (bf16[4,128]{1,0:T(4,128)(2,1)S(1)}, bf16[4,128]{1,0:T(4,128)(2,1)}, u32[]{:S(2)}) copy-start(bf16[4,128]{1,0:T(4,128)(2,1)} %param.21) | copy-start | bytes 3076
  6.5 7.8 %copy-start.17 = (bf16[4096,4]{0,1:T(4,128)(2,1)S(1)}, bf16[4096,4]{0,1:T(4,128)(2,1)}, u32[]{:S(2)}) copy-start(bf16[4096,4]{0,1:T(4,128)(2,1)} %param.17) | copy-start | bytes 98308
  6.5 9.2 %copy-start.21 = (f32[4]{0:T(128)S(1)}, f32[4]{0:T(128)}, u32[]{:S(2)}) copy-start(f32[4]{0:T(128)} %param.22) | copy-start | bytes 52
  6.5 9.3 %copy-start.16 = (s32[4096]{0:T(1024)S(1)}, s32[4096]{0:T(1024)}, u32[]{:S(2)}) copy-start(s32[4096]{0:T(1024)} %param.25) | copy-start | bytes 49156
  6.6 157.6 %all-gather.2.cloned.1.call-start = ((), (), s32[]{:S(2)}) async-start(), calls=%async_computation | async-start | bytes 9437184 | tf_op jit(solution)/shard_map/all_gather | solution.py:322
  11.7 23.3 %collective-permute-start.12 = (bf16[8,4096]{1,0:T(8,128)(2,1)S(1)}, bf16[8,4096]{1,0:T(8,128)(2,1)S(1)}, u32[]{:S(2)}, u32[]{:S(2)}) collective-permute-start(bf16[8,4096]{1,0:T(8,128)(2,1)S(1)} %slice.66), channel_id=1, source_target_pairs={{7,8},{15,16},{23,24}} | collective-permute-start | bytes 196616 | tf_op jit(solution)/shard_map/ppermute | solution.py:37
  12.3 23.4 %collective-permute-start.13 = (bf16[8,4096]{1,0:T(8,128)(2,1)S(1)}, bf16[8,4096]{1,0:T(8,128)(2,1)S(1)}, u32[]{:S(2)}, u32[]{:S(2)}) collective-permute-start(bf16[8,4096]{1,0:T(8,128)(2,1)S(1)} %slice.66), channel_id=1, source_target_pairs={{7,9},{15,17},{23,25}} | collective-permute-start | bytes 196616 | tf_op jit(solution)/shard_map/ppermute | solution.py:37
  13.0 23.5 %collective-permute-start.14 = (bf16[8,4096]{1,0:T(8,128)(2,1)S(1)}, bf16[8,4096]{1,0:T(8,128)(2,1)S(1)}, u32[]{:S(2)}, u32[]{:S(2)}) collective-permute-start(bf16[8,4096]{1,0:T(8,128)(2,1)S(1)} %slice.66), channel_id=1, source_target_pairs={{7,10},{15,18},{23,26}} | collective-permute-start | bytes 196616 | tf_op jit(solution)/shard_map/ppermute | solution.py:37
  13.7 19.3 %collective-permute-start.11 = (bf16[4096,128]{1,0:T(8,128)(2,1)S(1)}, bf16[4096,128]{1,0:T(8,128)(2,1)}, u32[]{:S(2)}, u32[]{:S(2)}) collective-permute-start(bf16[4096,128]{1,0:T(8,128)(2,1)S(1)} %copy-done.4), channel_id=1, source_target_pairs={{0,1},{1,0},{2,3},{3,2},{4,5},{5,4},{6,7},{7,6},{8,9},{9,8},{10,11... | collective-permute-start | bytes 3145736 | tf_op jit(solution)/shard_map/ppermute | solution.py:23
  14.2 17.9 %collective-permute-start.20 = (bf16[4,128]{1,0:T(4,128)(2,1)S(1)}, bf16[4,128]{1,0:T(4,128)(2,1)S(1)}, u32[]{:S(2)}, u32[]{:S(2)}) collective-permute-start(bf16[4,128]{1,0:T(4,128)(2,1)S(1)} %copy-done.19), channel_id=1, source_target_pairs={{0,1},{1,0},{2,3},{3,2},{4,5},{5,4},{6,7},{7,6},{8,9},{9,8},{10,11... | collective-permute-start | bytes 3080 | tf_op jit(solution)/shard_map/ppermute | solution.py:23
  32.2 5.0 %collective-permute-start.15 = (bf16[8,4096]{1,0:T(8,128)(2,1)S(1)}, bf16[8,4096]{1,0:T(8,128)(2,1)S(1)}, u32[]{:S(2)}, u32[]{:S(2)}) collective-permute-start(bf16[8,4096]{1,0:T(8,128)(2,1)S(1)} %slice.66), channel_id=1, source_target_pairs={{7,11},{15,19},{23,27}} | collective-permute-start | bytes 196616 | tf_op jit(solution)/shard_map/ppermute | solution.py:37
  33.0 15.3 %collective-permute-start.16 = (bf16[8,4096]{1,0:T(8,128)(2,1)S(1)}, bf16[8,4096]{1,0:T(8,128)(2,1)S(1)}, u32[]{:S(2)}, u32[]{:S(2)}) collective-permute-start(bf16[8,4096]{1,0:T(8,128)(2,1)S(1)} %slice.66), channel_id=1, source_target_pairs={{7,12},{15,20},{23,28}} | collective-permute-start | bytes 196616 | tf_op jit(solution)/shard_map/ppermute | solution.py:37
  33.7 37.8 %copy-start.2 = (bf16[4096,1,256]{2,1,0:T(2,128)(2,1)S(1)}, bf16[4096,1,256]{2,1,0:T(2,128)(2,1)}, u32[]{:S(2)}) copy-start(bf16[4096,1,256]{2,1,0:T(2,128)(2,1)} %get-tuple-element.67) | copy-start | bytes 6291460
  35.0 13.3 %collective-permute-start.17 = (bf16[8,4096]{1,0:T(8,128)(2,1)S(1)}, bf16[8,4096]{1,0:T(8,128)(2,1)S(1)}, u32[]{:S(2)}, u32[]{:S(2)}) collective-permute-start(bf16[8,4096]{1,0:T(8,128)(2,1)S(1)} %slice.66), channel_id=1, source_target_pairs={{7,13},{15,21},{23,29}} | collective-permute-start | bytes 196616 | tf_op jit(solution)/shard_map/ppermute | solution.py:37
  35.8 13.1 %collective-permute-start.18 = (bf16[8,4096]{1,0:T(8,128)(2,1)S(1)}, bf16[8,4096]{1,0:T(8,128)(2,1)S(1)}, u32[]{:S(2)}, u32[]{:S(2)}) collective-permute-start(bf16[8,4096]{1,0:T(8,128)(2,1)S(1)} %slice.66), channel_id=1, source_target_pairs={{7,14},{15,22},{23,30}} | collective-permute-start | bytes 196616 | tf_op jit(solution)/shard_map/ppermute | solution.py:37
  36.5 14.5 %collective-permute-start.19 = (bf16[8,4096]{1,0:T(8,128)(2,1)S(1)}, bf16[8,4096]{1,0:T(8,128)(2,1)S(1)}, u32[]{:S(2)}, u32[]{:S(2)}) collective-permute-start(bf16[8,4096]{1,0:T(8,128)(2,1)S(1)} %slice.66), channel_id=1, source_target_pairs={{7,15},{15,23},{23,31}} | collective-permute-start | bytes 196616 | tf_op jit(solution)/shard_map/ppermute | solution.py:37
  37.2 31.6 %collective-permute-start.2 = (bf16[256,1024]{1,0:T(8,128)(2,1)S(1)}, bf16[256,1024]{1,0:T(8,128)(2,1)}, u32[]{:S(2)}, u32[]{:S(2)}) collective-permute-start(bf16[256,1024]{1,0:T(8,128)(2,1)S(1)} %copy-done.6), channel_id=1, source_target_pairs={{0,6},{1,7},{2,4},{3,5},{4,2},{5,3},{6,0},{7,1},{8,14},{9,15},{10,... | collective-permute-start | bytes 1572872 | tf_op jit(solution)/shard_map/ppermute | solution.py:29
  48.3 92.4 %copy-start.8 = (bf16[4096,256]{1,0:T(8,128)(2,1)S(1)}, bf16[4096,256]{1,0:T(8,128)(2,1)}, u32[]{:S(2)}) copy-start(bf16[4096,256]{1,0:T(8,128)(2,1)} %get-tuple-element.66) | copy-start | bytes 6291460
  48.3 47.9 %collective-permute-start = (bf16[256,1024]{1,0:T(8,128)(2,1)S(1)}, bf16[256,1024]{1,0:T(8,128)(2,1)}, u32[]{:S(2)}, u32[]{:S(2)}) collective-permute-start(bf16[256,1024]{1,0:T(8,128)(2,1)S(1)} %copy-done.6), channel_id=1, source_target_pairs={{0,2},{1,3},{2,0},{3,1},{4,6},{5,7},{6,4},{7,5},{8,10},{9,11},{10,... | collective-permute-start | bytes 1572872 | tf_op jit(solution)/shard_map/ppermute | solution.py:29
  48.3 88.3 %collective-permute-start.1 = (bf16[256,1024]{1,0:T(8,128)(2,1)S(1)}, bf16[256,1024]{1,0:T(8,128)(2,1)}, u32[]{:S(2)}, u32[]{:S(2)}) collective-permute-start(bf16[256,1024]{1,0:T(8,128)(2,1)S(1)} %copy-done.6), channel_id=1, source_target_pairs={{0,4},{1,5},{2,6},{3,7},{4,0},{5,1},{6,2},{7,3},{8,12},{9,13},{10,... | collective-permute-start | bytes 1572872 | tf_op jit(solution)/shard_map/ppermute | solution.py:29
  48.9 89.2 %collective-permute-start.3 = (bf16[256,1024]{1,0:T(8,128)(2,1)S(1)}, bf16[256,1024]{1,0:T(8,128)(2,1)S(1)}, u32[]{:S(2)}, u32[]{:S(2)}) collective-permute-start(bf16[256,1024]{1,0:T(8,128)(2,1)S(1)} %copy-done.6), channel_id=1, source_target_pairs={{0,8},{8,0},{16,24},{24,16},{1,9},{9,1},{17,25},{25,17},{2,10},{10... | collective-permute-start | bytes 1572872 | tf_op jit(solution)/shard_map/ppermute | solution.py:29
  51.0 88.3 %collective-permute-start.7 = (bf16[256,1024]{1,0:T(8,128)(2,1)S(1)}, bf16[256,1024]{1,0:T(8,128)(2,1)S(1)}, u32[]{:S(2)}, u32[]{:S(2)}) collective-permute-start(bf16[256,1024]{1,0:T(8,128)(2,1)S(1)} %copy-done.6), channel_id=1, source_target_pairs={{0,16},{8,24},{16,0},{24,8},{1,17},{9,25},{17,1},{25,9},{2,18},{10... | collective-permute-start | bytes 1572872 | tf_op jit(solution)/shard_map/ppermute | solution.py:29
  68.8 71.2 %collective-permute-start.10 = (bf16[256,1024]{1,0:T(8,128)(2,1)}, bf16[256,1024]{1,0:T(8,128)(2,1)S(1)}, u32[]{:S(2)}, u32[]{:S(2)}) collective-permute-start(bf16[256,1024]{1,0:T(8,128)(2,1)} %collective-permute-done.2), channel_id=1, source_target_pairs={{0,16},{8,24},{16,0},{24,8},{1,17},{9,25},{17,1},{25,9},{2,18},{10... | collective-permute-start | bytes 1572872 | tf_op jit(solution)/shard_map/ppermute | solution.py:29
  96.2 66.6 %collective-permute-start.6 = (bf16[256,1024]{1,0:T(8,128)(2,1)}, bf16[256,1024]{1,0:T(8,128)(2,1)}, u32[]{:S(2)}, u32[]{:S(2)}) collective-permute-start(bf16[256,1024]{1,0:T(8,128)(2,1)} %collective-permute-done.2), channel_id=1, source_target_pairs={{0,8},{8,0},{16,24},{24,16},{1,9},{9,1},{17,25},{25,17},{2,10},{10... | collective-permute-start | bytes 1572872 | tf_op jit(solution)/shard_map/ppermute | solution.py:29
  136.7 15.1 %collective-permute-start.4 = (bf16[256,1024]{1,0:T(8,128)(2,1)}, bf16[256,1024]{1,0:T(8,128)(2,1)}, u32[]{:S(2)}, u32[]{:S(2)}) collective-permute-start(bf16[256,1024]{1,0:T(8,128)(2,1)} %collective-permute-done), channel_id=1, source_target_pairs={{0,8},{8,0},{16,24},{24,16},{1,9},{9,1},{17,25},{25,17},{2,10},{10... | collective-permute-start | bytes 1572872 | tf_op jit(solution)/shard_map/ppermute | solution.py:29
  138.1 24.6 %collective-permute-start.8 = (bf16[256,1024]{1,0:T(8,128)(2,1)}, bf16[256,1024]{1,0:T(8,128)(2,1)}, u32[]{:S(2)}, u32[]{:S(2)}) collective-permute-start(bf16[256,1024]{1,0:T(8,128)(2,1)} %collective-permute-done), channel_id=1, source_target_pairs={{0,16},{8,24},{16,0},{24,8},{1,17},{9,25},{17,1},{25,9},{2,18},{10... | collective-permute-start | bytes 1572872 | tf_op jit(solution)/shard_map/ppermute | solution.py:29
  139.3 23.4 %collective-permute-start.5 = (bf16[256,1024]{1,0:T(8,128)(2,1)}, bf16[256,1024]{1,0:T(8,128)(2,1)}, u32[]{:S(2)}, u32[]{:S(2)}) collective-permute-start(bf16[256,1024]{1,0:T(8,128)(2,1)} %collective-permute-done.1), channel_id=1, source_target_pairs={{0,8},{8,0},{16,24},{24,16},{1,9},{9,1},{17,25},{25,17},{2,10},{10... | collective-permute-start | bytes 1572872 | tf_op jit(solution)/shard_map/ppermute | solution.py:29
  140.0 24.1 %collective-permute-start.9 = (bf16[256,1024]{1,0:T(8,128)(2,1)}, bf16[256,1024]{1,0:T(8,128)(2,1)S(1)}, u32[]{:S(2)}, u32[]{:S(2)}) collective-permute-start(bf16[256,1024]{1,0:T(8,128)(2,1)} %collective-permute-done.1), channel_id=1, source_target_pairs={{0,16},{8,24},{16,0},{24,8},{1,17},{9,25},{17,1},{25,9},{2,18},{10... | collective-permute-start | bytes 1572872 | tf_op jit(solution)/shard_map/ppermute | solution.py:29
  177.2 18.2 %copy-start.7 = (bf16[256,1024]{1,0:T(8,128)(2,1)S(1)}, bf16[256,1024]{1,0:T(8,128)(2,1)}, u32[]{:S(2)}) copy-start(bf16[256,1024]{1,0:T(8,128)(2,1)} %constant_dynamic-slice_fusion.3) | copy-start | bytes 1572868
  188.1 57.5 %copy-start.20 = (f32[256]{0:T(256)S(1)}, f32[256]{0:T(256)}, u32[]{:S(2)}) copy-start(f32[256]{0:T(256)} %param.23) | copy-start | bytes 3076
  188.1 10.3 %collective-permute-start.21 = (f32[136,256]{1,0:T(8,128)S(1)}, f32[136,256]{1,0:T(8,128)S(1)}, u32[]{:S(2)}, u32[]{:S(2)}) collective-permute-start(f32[136,256]{1,0:T(8,128)S(1)} %get-tuple-element.41), channel_id=1, source_target_pairs={{0,8},{8,16},{16,24},{1,9},{9,17},{17,25},{2,10},{10,18},{18,26},{... | collective-permute-start | bytes 417800 | tf_op jit(solution)/shard_map/ppermute | solution.py:212
  190.9 40.2 %collective-permute-start.22 = (f32[136,256]{1,0:T(8,128)S(1)}, f32[136,256]{1,0:T(8,128)S(1)}, u32[]{:S(2)}, u32[]{:S(2)}) collective-permute-start(f32[136,256]{1,0:T(8,128)S(1)} %get-tuple-element.41), channel_id=1, source_target_pairs={{0,16},{8,24},{1,17},{9,25},{2,18},{10,26},{3,19},{11,27},{4,20},{... | collective-permute-start | bytes 417800 | tf_op jit(solution)/shard_map/ppermute | solution.py:212
  194.0 37.1 %collective-permute-start.23 = (f32[136,256]{1,0:T(8,128)S(1)}, f32[136,256]{1,0:T(8,128)S(1)}, u32[]{:S(2)}, u32[]{:S(2)}) collective-permute-start(f32[136,256]{1,0:T(8,128)S(1)} %get-tuple-element.41), channel_id=1, source_target_pairs={{0,24},{1,25},{2,26},{3,27},{4,28},{5,29},{6,30},{7,31}} | collective-permute-start | bytes 417800 | tf_op jit(solution)/shard_map/ppermute | solution.py:212
  195.5 37.4 %collective-permute-start.24 = (bf16[256,1024]{1,0:T(8,128)(2,1)S(1)}, bf16[256,1024]{1,0:T(8,128)(2,1)}, u32[]{:S(2)}, u32[]{:S(2)}) collective-permute-start(bf16[256,1024]{1,0:T(8,128)(2,1)S(1)} %copy-done.7), channel_id=1, source_target_pairs={{0,24},{8,16},{16,8},{24,0},{1,25},{9,17},{17,9},{25,1},{2,26},{10... | collective-permute-start | bytes 1572872 | tf_op jit(solution)/shard_map/ppermute | solution.py:29
  195.5 37.3 %collective-permute-start.25 = (bf16[256,1024]{1,0:T(8,128)(2,1)}, bf16[256,1024]{1,0:T(8,128)(2,1)}, u32[]{:S(2)}, u32[]{:S(2)}) collective-permute-start(bf16[256,1024]{1,0:T(8,128)(2,1)} %collective-permute-done), channel_id=1, source_target_pairs={{0,24},{8,16},{16,8},{24,0},{1,25},{9,17},{17,9},{25,1},{2,26},{10... | collective-permute-start | bytes 1572872 | tf_op jit(solution)/shard_map/ppermute | solution.py:29
  198.5 34.4 %collective-permute-start.26 = (bf16[256,1024]{1,0:T(8,128)(2,1)}, bf16[256,1024]{1,0:T(8,128)(2,1)}, u32[]{:S(2)}, u32[]{:S(2)}) collective-permute-start(bf16[256,1024]{1,0:T(8,128)(2,1)} %collective-permute-done.1), channel_id=1, source_target_pairs={{0,24},{8,16},{16,8},{24,0},{1,25},{9,17},{17,9},{25,1},{2,26},{10... | collective-permute-start | bytes 1572872 | tf_op jit(solution)/shard_map/ppermute | solution.py:29
  231.1 14.5 %collective-permute-start.27 = (bf16[256,1024]{1,0:T(8,128)(2,1)}, bf16[256,1024]{1,0:T(8,128)(2,1)}, u32[]{:S(2)}, u32[]{:S(2)}) collective-permute-start(bf16[256,1024]{1,0:T(8,128)(2,1)} %collective-permute-done.2), channel_id=1, source_target_pairs={{0,24},{8,16},{16,8},{24,0},{1,25},{9,17},{17,9},{25,1},{2,26},{10... | collective-permute-start | bytes 1572872 | tf_op jit(solution)/shard_map/ppermute | solution.py:29
  232.7 12.9 %collective-permute-start.28 = (f32[1024]{0:T(1024)S(1)}, f32[1024]{0:T(1024)S(1)}, u32[]{:S(2)}, u32[]{:S(2)}) collective-permute-start(f32[1024]{0:T(1024)S(1)} %reduce.2), channel_id=1, source_target_pairs={{0,1},{1,0},{2,3},{3,2},{4,5},{5,4},{6,7},{7,6},{8,9},{9,8},{10,11... | collective-permute-start | bytes 12296 | tf_op jit(solution)/shard_map/ppermute | solution.py:23
  245.9 5.6 %collective-permute-start.29 = (bf16[256,256]{1,0:T(8,128)(2,1)S(1)}, bf16[256,256]{1,0:T(8,128)(2,1)S(1)}, u32[]{:S(2)}, u32[]{:S(2)}) collective-permute-start(bf16[256,256]{1,0:T(8,128)(2,1)S(1)} %get-tuple-element.69), channel_id=1, source_target_pairs={{0,2},{1,3},{2,0},{3,1},{4,6},{5,7},{6,4},{7,5},{8,10},{9,11},{10,... | collective-permute-start | bytes 393224 | tf_op jit(solution)/shard_map/ppermute | solution.py:29
  246.0 12.3 %collective-permute-start.30 = (bf16[256,256]{1,0:T(8,128)(2,1)S(1)}, bf16[256,256]{1,0:T(8,128)(2,1)S(1)}, u32[]{:S(2)}, u32[]{:S(2)}) collective-permute-start(bf16[256,256]{1,0:T(8,128)(2,1)S(1)} %get-tuple-element.71), channel_id=1, source_target_pairs={{0,4},{1,5},{2,6},{3,7},{4,0},{5,1},{6,2},{7,3},{8,12},{9,13},{10,... | collective-permute-start | bytes 393224 | tf_op jit(solution)/shard_map/ppermute | solution.py:29
  248.8 10.8 %collective-permute-start.31 = (bf16[256,256]{1,0:T(8,128)(2,1)S(1)}, bf16[256,256]{1,0:T(8,128)(2,1)S(1)}, u32[]{:S(2)}, u32[]{:S(2)}) collective-permute-start(bf16[256,256]{1,0:T(8,128)(2,1)S(1)} %get-tuple-element.70), channel_id=1, source_target_pairs={{0,6},{1,7},{2,4},{3,5},{4,2},{5,3},{6,0},{7,1},{8,14},{9,15},{10,... | collective-permute-start | bytes 393224 | tf_op jit(solution)/shard_map/ppermute | solution.py:29
  261.0 5.6 %copy-start.11 = (bf16[256,1024]{1,0:T(8,128)(2,1)S(1)}, bf16[256,1024]{1,0:T(8,128)(2,1)}, u32[]{:S(2)}) copy-start(bf16[256,1024]{1,0:T(8,128)(2,1)} %copy-done.10) | copy-start | bytes 1572868
  262.5 13.8 %collective-permute-start.35 = (bf16[128,1024]{1,0:T(8,128)(2,1)S(1)}, bf16[128,1024]{1,0:T(8,128)(2,1)S(1)}, u32[]{:S(2)}, u32[]{:S(2)}) collective-permute-start(bf16[128,1024]{1,0:T(8,128)(2,1)S(1)} %dynamic-slice_convert_fusion), channel_id=1, source_target_pairs={{0,1},{1,0},{2,3},{3,2},{4,5},{5,4},{6,7},{7,6},{8,9},{9,8},{10,11... | collective-permute-start | bytes 786440 | tf_op jit(solution)/shard_map/ppermute | solution.py:29
  267.0 8.3 %collective-permute-start.33 = (bf16[128,1024]{1,0:T(8,128)(2,1)S(1)}, bf16[128,1024]{1,0:T(8,128)(2,1)S(1)}, u32[]{:S(2)}, u32[]{:S(2)}) collective-permute-start(bf16[128,1024]{1,0:T(8,128)(2,1)S(1)} %dynamic-slice_convert_fusion.2), channel_id=1, source_target_pairs={{0,1},{1,0},{2,3},{3,2},{4,5},{5,4},{6,7},{7,6},{8,9},{9,8},{10,11... | collective-permute-start | bytes 786440 | tf_op jit(solution)/shard_map/ppermute | solution.py:29
  272.0 3.0 %collective-permute-start.32 = (bf16[128,1024]{1,0:T(8,128)(2,1)S(1)}, bf16[128,1024]{1,0:T(8,128)(2,1)S(1)}, u32[]{:S(2)}, u32[]{:S(2)}) collective-permute-start(bf16[128,1024]{1,0:T(8,128)(2,1)S(1)} %dynamic-slice_convert_fusion.3), channel_id=1, source_target_pairs={{0,1},{1,0},{2,3},{3,2},{4,5},{5,4},{6,7},{7,6},{8,9},{9,8},{10,11... | collective-permute-start | bytes 786440 | tf_op jit(solution)/shard_map/ppermute | solution.py:29
  274.5 1.7 collective-permute-start.34
  (13 other events, 32.1 us)
Sparse Core Ops, SparseCore 0:
  11.0 130.0 all-gather.1

commit v3 on v2

--- a/solution.py
+++ b/solution.py
@@ -39,11 +39,10 @@
     return total
 
 
-def spread_weight(weight, spans, chips):
+def spread_along(weight, spans, chips):
     cols = weight.shape[1] // spans
     own = lax.dynamic_slice_in_dim(weight, lax.axis_index("seq") * cols, cols, axis=1)
-    along = [crossed(own, "tp", 2 * d) for d in range(chips)]
-    return [[crossed(part, "seq", e) for part in along] for e in range(spans)]
+    return [crossed(own, "tp", 2 * d) for d in range(chips)]
 
 
 def silu(v):
@@ -287,7 +286,7 @@
         axis=1,
     )
     spans, chips = lax.axis_size("seq"), lax.axis_size("tp") // 2
-    weights = spread_weight(output_weight, spans, chips)
+    summed = width // 2
     tail = tail_of_previous(normed[rows - 8 :])
     pad_heads = ((0, 0), (0, LANES - heads_dev))
     matrix = jnp.concatenate(
@@ -320,23 +319,31 @@
     skip = jnp.repeat(skip_gain, head_dim)[None]
     matrix, before, aux, row_seg = lax.optimization_barrier((matrix, before, aux, row_seg))
     piece = lax.all_gather(normed, "tp", axis=0, tiled=True)
-    piece, near = lax.optimization_barrier((piece, weights[:3]))
+    piece, moved = lax.optimization_barrier((piece, output_weight[:, summed:]))
+    along = spread_along(moved, spans, chips)
     projected = jnp.dot(piece, matrix, preferred_element_type=jnp.float32)
     y, c_map, w_span, packed = local_scan(
         heads_dev, state_dim, projected, before, aux, row_seg, filters.astype(jnp.float32),
         bias, rate, skip,
     )
+    packed, along = lax.optimization_barrier((packed, along))
     incoming = entering_state(packed, state_dim)
+    incoming, along = lax.optimization_barrier((incoming, along))
+    weights = [[crossed(part, "seq", e) for part in along] for e in range(spans)]
     gated, squares = gate_all(
         heads_dev, y, c_map, w_span, projected, conv_dim // inner_dev, incoming
     )
-    gated, far = lax.optimization_barrier((gated, weights[3:]))
-    weights = near + far
     own_squares = squares[:, 0]
     other_squares = swapped(own_squares, "tp", 0)
     group_mean = (own_squares + other_squares) / (2 * inner_dev)
     mixed = (gated * lax.rsqrt(group_mean + EPS)[:, None] * mixer_gain).astype(jnp.bfloat16)
-    return project_out(hidden, mixed, weights)
+    partial_out = jnp.dot(
+        mixed, output_weight[:, :summed], preferred_element_type=jnp.float32
+    ).astype(jnp.bfloat16)
+    mine = lax.psum_scatter(partial_out, "tp", scatter_dimension=0, tiled=True)
+    right = project_out(hidden[:, summed:], mixed, weights)
+    left = (hidden[:, :summed].astype(jnp.float32) + mine.astype(jnp.float32)).astype(jnp.bfloat16)
+    return jnp.concatenate([left, right], axis=1)
 
 
 def solution(mesh):

time: 286 us -> 224 us (0.78)
  waiting for transfers between devices: 152 us -> 103 us
  matrix products: 29.4 us -> 22 us
  starting transfers between devices: 42.8 us -> 39.9 us
    ppermute x22, waiting for transfers between devices: 119 us -> 45.7 us  [crossed(): lax.ppermute(block, axis, [(i, i ^ mask) for i in range(lax.axis_size(axi...]
    all_gather x1, waiting for transfers between devices: 0.01 us -> 53.6 us  [body(): piece = lax.all_gather(normed, 'tp', axis=0, tiled=True)]
    ppermute x3, waiting for transfers between devices: 32.6 us -> 2.37 us  [entering_state(): lax.ppermute(packed, 'seq', [(i, i + e) for i in range(spans - e)])]
    dot_general x16, matrix products: 16.4 us -> 4.48 us  [project_out(): jnp.dot(m, w, preferred_element_type=jnp.float32)]
    dot_general x0 -> x1, matrix products: none -> 4.53 us  [body(): jnp.dot(mixed, output_weight[:, :summed], preferred_element_type=jnp.floa...]
    ppermute x22, starting transfers between devices: 29.3 us -> 26.2 us  [crossed(): lax.ppermute(block, axis, [(i, i ^ mask) for i in range(lax.axis_size(axi...]
    unnamed x51 -> x29, local copies, waits for them, and re-layouts: 8.16 us -> 7.32 us
  transfers between devices with their start and end apart: 37 -> 38, of which waited for: 11 -> 14; matrix products, arithmetic and copies ran while one was open for 14% -> 19% of each run, Pallas kernels for 0% -> 5%
where the time goes in v3:
time: 224 us
  waiting for transfers between devices  103 us (46%)
  starting transfers between devices  39.9 us (18%)
  matrix products  22 us (10%)
  local copies, waits for them, and re-layouts  21.2 us (9%)
  between operations  14.2 us (6%)
  Pallas kernels  12.3 us (5%)
  other arithmetic  11.3 us (5%)
    all_gather x1, waiting for transfers between devices, body(): piece = lax.all_gather(normed, 'tp', axis=0, tiled=True)  53.6 us
    ppermute x22, waiting for transfers between devices, crossed(): lax.ppermute(block, axis, [(i, i ^ mask) for i in range(lax.axis_size(axi...  45.7 us
    ppermute x22, starting transfers between devices, crossed(): lax.ppermute(block, axis, [(i, i ^ mask) for i in range(lax.axis_size(axi...  26.2 us
    dot_general x1, matrix products, body(): projected = jnp.dot(piece, matrix, preferred_element_type=jnp.float32)  12.3 us
    pallas_call x1, Pallas kernels, local_scan(): pl.pallas_call(lambda *refs: scan_kernel(heads, *refs), grid=(length // S...  10.9 us
    slice x1, local copies, waits for them, and re-layouts, body(): inner_weight[:, 0, :]  10.1 us
    ppermute x3, starting transfers between devices, entering_state(): lax.ppermute(packed, 'seq', [(i, i + e) for i in range(spans - e)])  7.62 us
    unnamed x29, local copies, waits for them, and re-layouts  7.32 us
  transfers between devices with their start and end apart: 38, of which 14 were waited for; matrix products, arithmetic and copies ran while one was open for 19% of the time, Pallas kernels for 5%

profile of v3, /device:TPU:0, one launch (start us, length us, event | category | flops | bytes accessed | tf_op | source)
XLA Modules:
  0.0 223.6 jit_solution(9308905372686986561)
XLA Ops:
  6.6 1.6 fusion.6
  8.2 2.5 %fusion.8 = bf16[128,4096]{1,0:T(8,128)(2,1)} fusion(bf16[128,4096]{1,0:T(8,128)(2,1)} %param.13, f32[4096]{0:T(1024)} %param.14, f32[128]{0:T(128)S(1)} %add_rsqrt_fusion.1), kind=kLoop, calls=%fused_computation.11 | loop fusion | flops 2097152 | bytes 2114048 | tf_op jit(solution)/shard_map/convert_element_type | solution.py:274
  10.8 0.8 slice.82
  12.3 0.7 collective-permute-start.2
  14.3 1.4 copy.23
  16.8 0.7 pad_add_fusion
  17.6 0.7 compare_convert_fusion
  18.4 10.1 %fusion.53 = (bf16[4096,1,256]{2,1,0:T(2,128)(2,1)}, bf16[4096,1,256]{2,1,0:T(2,128)(2,1)S(1)}) fusion(bf16[4096,2,256]{2,1,0:T(2,128)(2,1)} %param.15), kind=kLoop, calls=%fused_computation.102 | loop fusion | bytes 8388608 | tf_op jit(solution)/shard_map/slice | solution.py:295
  28.5 2.5 %constant_dynamic-update-slice_fusion.2 = (bf16[4096,896]{1,0:T(8,128)(2,1)}, bf16[4096,256]{1,0:T(8,128)(2,1)}) fusion(bf16[4096,1,256]{2,1,0:T(2,128)(2,1)S(1)} %get-tuple-element.56), kind=kLoop, calls=%fused_computation.70 | loop fusion | bytes 6291456
  32.5 1.4 constant_dynamic-update-slice_fusion.1
  35.9 1.3 constant_dynamic-update-slice_fusion
  38.0 1.6 copy-done
  39.6 1.7 fusion.9
  41.3 1.2 pad_dynamic-update-slice_fusion
  42.8 53.6 %all-gather.2.cloned.1.call-done = bf16[1024,4096]{1,0:T(8,128)(2,1)} async-done(((bf16[128,4096]{1,0:T(8,128)(2,1)}), bf16[1024,4096]{1,0:T(8,128)(2,1)}) %all-gather.2.cloned.1.call-update) | async-done | bytes 8388624 | tf_op jit(solution)/shard_map/all_gather | solution.py:321
  96.4 2.4 %collective-permute-start.11 = (bf16[256,512]{1,0:T(8,128)(2,1)S(1)}, bf16[256,512]{1,0:T(8,128)(2,1)S(1)}, u32[]{:S(2)}, u32[]{:S(2)}) collective-permute-start(bf16[256,512]{1,0:T(8,128)(2,1)S(1)} %constant_dynamic-slice_fusion.3), channel_id=1, source_target_pairs={{0,4},{1,5},{2,6},{3,7},{4,0},{5,1},{6,2},{7,3},{8,12},{9,13},{10,... | collective-permute-start | bytes 786440 | tf_op jit(solution)/shard_map/ppermute | solution.py:29
  98.9 2.0 collective-permute-start.12
  100.8 12.3 %fusion.54.refs_0_.refs_3_ = f32[1024,896]{1,0:T(8,128)S(1)} fusion(bf16[1024,4096]{1,0:T(8,128)(2,1)} %all-gather.2.cloned.1.call-done, bf16[4096,896]{1,0:T(8,128)(2,1)} %pad_dynamic-update-slice_fusion), kind=kOutput, calls=%fused_computation.103 | convolution fusion | flops 7516192768 | bytes 19398656 | tf_op jit(solution)/shard_map/dot_general | solution.py:324
  113.1 10.9 %local_scan.1 = (f32[1024,256]{1,0:T(8,128)S(1)}, bf16[1024,128]{1,0:T(8,128)(2,1)S(1)}, f32[1024,128]{1,0:T(8,128)S(1)}, f32[136,256]{1,0:T(8,128)S(1)}) custom-call(f32[1024,896]{1,0:T(8,128)S(1)} %fusion.54.refs_0_.refs_3_, f32[8,512]{1,0:T(8,128)S(1)} %fusion.refs_1_, f32[1024,8]{1,0:T(8,128)S(1)} %copy.24.refs_2_, f32[8,1024]{1,0:T(8,128)S(1)} %stack.59.refs_3_, ...), custom_call_target="tpu_custom_call" | custom-call | flops 12000000000 | bytes 8000000 | tf_op jit(solution)/shard_map/local_scan/pallas_call | solution.py:138
  124.1 3.4 %collective-permute-start.13 = (f32[136,256]{1,0:T(8,128)S(1)}, f32[136,256]{1,0:T(8,128)S(1)}, u32[]{:S(2)}, u32[]{:S(2)}) collective-permute-start(f32[136,256]{1,0:T(8,128)S(1)} %get-tuple-element.37), channel_id=1, source_target_pairs={{0,8},{8,16},{16,24},{1,9},{9,17},{17,25},{2,10},{10,18},{18,26},{... | collective-permute-start | bytes 417800 | tf_op jit(solution)/shard_map/ppermute | solution.py:211
  127.5 2.8 %collective-permute-start.14 = (f32[136,256]{1,0:T(8,128)S(1)}, f32[136,256]{1,0:T(8,128)S(1)}, u32[]{:S(2)}, u32[]{:S(2)}) collective-permute-start(f32[136,256]{1,0:T(8,128)S(1)} %get-tuple-element.37), channel_id=1, source_target_pairs={{0,16},{8,24},{1,17},{9,25},{2,18},{10,26},{3,19},{11,27},{4,20},{... | collective-permute-start | bytes 417800 | tf_op jit(solution)/shard_map/ppermute | solution.py:211
  130.2 1.5 collective-permute-start.15
  131.7 2.2 collective-permute-done.14
  134.2 1.4 gate_all.1
  135.8 1.2 collective-permute-done.16
  137.2 4.5 %convolution_convert_fusion = bf16[1024,2048]{1,0:T(8,128)(2,1)} fusion(bf16[1024,256]{1,0:T(8,128)(2,1)S(1)} %multiply_convert_fusion, bf16[256,4096]{1,0:T(8,128)(2,1)} %param.24), kind=kOutput, calls=%fused_computation.6 | convolution fusion | flops 1075838976 | bytes 5767168 | tf_op jit(solution)/shard_map/dot_general | solution.py:340
  141.9 3.6 %collective-permute-start.32 = (bf16[256,512]{1,0:T(8,128)(2,1)}, bf16[256,512]{1,0:T(8,128)(2,1)S(1)}, u32[]{:S(2)}, u32[]{:S(2)}) collective-permute-start(bf16[256,512]{1,0:T(8,128)(2,1)} %collective-permute-done.10), channel_id=1, source_target_pairs={{0,24},{8,16},{16,8},{24,0},{1,25},{9,17},{17,9},{25,1},{2,26},{10... | collective-permute-start | bytes 786440 | tf_op jit(solution)/shard_map/ppermute | solution.py:29
  145.6 1.6 collective-permute-start.34
  147.2 1.3 collective-permute-start.31
  149.0 7.4 %collective-permute-done.17 = bf16[256,256]{1,0:T(8,128)(2,1)S(1)} collective-permute-done((bf16[256,256]{1,0:T(8,128)(2,1)S(1)}, bf16[256,256]{1,0:T(8,128)(2,1)S(1)}, u32[]{:S(2)}, u32[]{:S(2)}) %collective-permute-start.17) | collective-permute-done | bytes 131104 | tf_op jit(solution)/shard_map/ppermute | solution.py:29
  156.4 2.4 %collective-permute-start.19 = (bf16[256,256]{1,0:T(8,128)(2,1)S(1)}, bf16[256,256]{1,0:T(8,128)(2,1)S(1)}, u32[]{:S(2)}, u32[]{:S(2)}) collective-permute-start(bf16[256,256]{1,0:T(8,128)(2,1)S(1)} %get-tuple-element.58), channel_id=1, source_target_pairs={{0,6},{1,7},{2,4},{3,5},{4,2},{5,3},{6,0},{7,1},{8,14},{9,15},{10,... | collective-permute-start | bytes 393224 | tf_op jit(solution)/shard_map/ppermute | solution.py:29
  158.8 1.2 convolution_add_fusion.4
  160.0 6.3 %collective-permute-done.19 = bf16[256,256]{1,0:T(8,128)(2,1)S(1)} collective-permute-done((bf16[256,256]{1,0:T(8,128)(2,1)S(1)}, bf16[256,256]{1,0:T(8,128)(2,1)S(1)}, u32[]{:S(2)}, u32[]{:S(2)}) %collective-permute-start.19) | collective-permute-done | bytes 131104 | tf_op jit(solution)/shard_map/ppermute | solution.py:29
  166.2 4.6 %collective-permute-start.18 = (bf16[256,256]{1,0:T(8,128)(2,1)S(1)}, bf16[256,256]{1,0:T(8,128)(2,1)S(1)}, u32[]{:S(2)}, u32[]{:S(2)}) collective-permute-start(bf16[256,256]{1,0:T(8,128)(2,1)S(1)} %get-tuple-element.57), channel_id=1, source_target_pairs={{0,4},{1,5},{2,6},{3,7},{4,0},{5,1},{6,2},{7,3},{8,12},{9,13},{10,... | collective-permute-start | bytes 393224 | tf_op jit(solution)/shard_map/ppermute | solution.py:29
  171.0 11.1 %collective-permute-done.18 = bf16[256,256]{1,0:T(8,128)(2,1)S(1)} collective-permute-done((bf16[256,256]{1,0:T(8,128)(2,1)S(1)}, bf16[256,256]{1,0:T(8,128)(2,1)S(1)}, u32[]{:S(2)}, u32[]{:S(2)}) %collective-permute-start.18) | collective-permute-done | bytes 131104 | tf_op jit(solution)/shard_map/ppermute | solution.py:29
  182.4 1.7 collective-permute-start.28
  184.3 5.2 %collective-permute-done.33 = bf16[256,512]{1,0:T(8,128)(2,1)S(1)} collective-permute-done((bf16[256,512]{1,0:T(8,128)(2,1)S(1)}, bf16[256,512]{1,0:T(8,128)(2,1)S(1)}, u32[]{:S(2)}, u32[]{:S(2)}) %collective-permute-start.33) | collective-permute-done | bytes 262176 | tf_op jit(solution)/shard_map/ppermute | solution.py:29
  189.5 1.6 collective-permute-start.29
  192.5 1.9 collective-permute-start.23
  195.5 4.6 %collective-permute-done.29 = bf16[256,512]{1,0:T(8,128)(2,1)S(1)} collective-permute-done((bf16[256,512]{1,0:T(8,128)(2,1)S(1)}, bf16[256,512]{1,0:T(8,128)(2,1)S(1)}, u32[]{:S(2)}, u32[]{:S(2)}) %collective-permute-start.29) | collective-permute-done | bytes 262176 | tf_op jit(solution)/shard_map/ppermute | solution.py:29
  200.1 0.8 collective-permute-start.21
  201.1 3.0 %collective-permute-done.26 = bf16[256,512]{1,0:T(8,128)(2,1)S(1)} collective-permute-done((bf16[256,512]{1,0:T(8,128)(2,1)S(1)}, bf16[256,512]{1,0:T(8,128)(2,1)S(1)}, u32[]{:S(2)}, u32[]{:S(2)}) %collective-permute-start.26) | collective-permute-done | bytes 262176 | tf_op jit(solution)/shard_map/ppermute | solution.py:29
  205.2 1.8 collective-permute-done.23
  207.3 2.6 %collective-permute-done.24 = bf16[256,512]{1,0:T(8,128)(2,1)S(1)} collective-permute-done((bf16[256,512]{1,0:T(8,128)(2,1)S(1)}, bf16[256,512]{1,0:T(8,128)(2,1)S(1)}, u32[]{:S(2)}, u32[]{:S(2)}) %collective-permute-start.24) | collective-permute-done | bytes 262176 | tf_op jit(solution)/shard_map/ppermute | solution.py:29
  210.1 2.6 %collective-permute-done.21 = bf16[256,512]{1,0:T(8,128)(2,1)S(1)} collective-permute-done((bf16[256,512]{1,0:T(8,128)(2,1)S(1)}, bf16[256,512]{1,0:T(8,128)(2,1)S(1)}, u32[]{:S(2)}, u32[]{:S(2)}) %collective-permute-start.21) | collective-permute-done | bytes 262176 | tf_op jit(solution)/shard_map/ppermute | solution.py:29
  213.1 1.2 collective-permute-done.25
  214.6 1.2 add_convert_fusion
  215.8 1.1 pad_maximum_fusion
  (126 shorter events, 14.5 us)
Async XLA Ops:
  6.5 7.1 %copy-start.2 = (bf16[4096,128]{1,0:T(8,128)(2,1)S(1)}, bf16[4096,128]{1,0:T(8,128)(2,1)}, u32[]{:S(2)}) copy-start(bf16[4096,128]{1,0:T(8,128)(2,1)} %param.16) | copy-start | bytes 3145732
  6.5 7.7 %copy-start.8 = (bf16[4,128]{1,0:T(4,128)(2,1)S(1)}, bf16[4,128]{1,0:T(4,128)(2,1)}, u32[]{:S(2)}) copy-start(bf16[4,128]{1,0:T(4,128)(2,1)} %param.21) | copy-start | bytes 3076
  6.5 7.8 %copy-start.6 = (bf16[4096,4]{0,1:T(4,128)(2,1)S(1)}, bf16[4096,4]{0,1:T(4,128)(2,1)}, u32[]{:S(2)}) copy-start(bf16[4096,4]{0,1:T(4,128)(2,1)} %param.17) | copy-start | bytes 98308
  6.5 9.2 %copy-start.10 = (f32[4]{0:T(128)S(1)}, f32[4]{0:T(128)}, u32[]{:S(2)}) copy-start(f32[4]{0:T(128)} %param.22) | copy-start | bytes 52
  6.5 9.3 %copy-start.11 = (f32[4]{0:T(128)S(1)}, f32[4]{0:T(128)}, u32[]{:S(2)}) copy-start(f32[4]{0:T(128)} %param.18) | copy-start | bytes 52
  6.5 9.3 %copy-start.12 = (f32[4]{0:T(128)S(1)}, f32[4]{0:T(128)}, u32[]{:S(2)}) copy-start(f32[4]{0:T(128)} %param.19) | copy-start | bytes 52
  6.6 9.3 %copy-start.5 = (s32[4096]{0:T(1024)S(1)}, s32[4096]{0:T(1024)}, u32[]{:S(2)}) copy-start(s32[4096]{0:T(1024)} %param.25) | copy-start | bytes 49156
  6.6 89.8 %all-gather.2.cloned.1.call-start = ((), (), s32[]{:S(2)}) async-start(), calls=%async_computation.1 | async-start | bytes 9437184 | tf_op jit(solution)/shard_map/all_gather | solution.py:321
  10.8 203.8 %reduce-scatter.2.cloned.1.call-start = ((), (), s32[]{:S(2)}) async-start(), calls=%async_computation.2 | async-start | bytes 4718592 | tf_op jit(solution)/shard_map/reduce_scatter | solution.py:343
  11.7 22.2 %collective-permute-start.1 = (bf16[8,4096]{1,0:T(8,128)(2,1)S(1)}, bf16[8,4096]{1,0:T(8,128)(2,1)S(1)}, u32[]{:S(2)}, u32[]{:S(2)}) collective-permute-start(bf16[8,4096]{1,0:T(8,128)(2,1)S(1)} %slice.82), channel_id=1, source_target_pairs={{7,8},{15,16},{23,24}} | collective-permute-start | bytes 196616 | tf_op jit(solution)/shard_map/ppermute | solution.py:37
  12.3 22.2 %collective-permute-start.2 = (bf16[8,4096]{1,0:T(8,128)(2,1)S(1)}, bf16[8,4096]{1,0:T(8,128)(2,1)S(1)}, u32[]{:S(2)}, u32[]{:S(2)}) collective-permute-start(bf16[8,4096]{1,0:T(8,128)(2,1)S(1)} %slice.82), channel_id=1, source_target_pairs={{7,9},{15,17},{23,25}} | collective-permute-start | bytes 196616 | tf_op jit(solution)/shard_map/ppermute | solution.py:37
  13.0 22.2 %collective-permute-start.3 = (bf16[8,4096]{1,0:T(8,128)(2,1)S(1)}, bf16[8,4096]{1,0:T(8,128)(2,1)S(1)}, u32[]{:S(2)}, u32[]{:S(2)}) collective-permute-start(bf16[8,4096]{1,0:T(8,128)(2,1)S(1)} %slice.82), channel_id=1, source_target_pairs={{7,10},{15,18},{23,26}} | collective-permute-start | bytes 196616 | tf_op jit(solution)/shard_map/ppermute | solution.py:37
  13.7 18.2 %collective-permute-start = (bf16[4096,128]{1,0:T(8,128)(2,1)S(1)}, bf16[4096,128]{1,0:T(8,128)(2,1)S(1)}, u32[]{:S(2)}, u32[]{:S(2)}) collective-permute-start(bf16[4096,128]{1,0:T(8,128)(2,1)S(1)} %copy-done.2), channel_id=1, source_target_pairs={{0,1},{1,0},{2,3},{3,2},{4,5},{5,4},{6,7},{7,6},{8,9},{9,8},{10,11... | collective-permute-start | bytes 3145736 | tf_op jit(solution)/shard_map/ppermute | solution.py:23
  14.2 16.9 %collective-permute-start.9 = (bf16[4,128]{1,0:T(4,128)(2,1)S(1)}, bf16[4,128]{1,0:T(4,128)(2,1)S(1)}, u32[]{:S(2)}, u32[]{:S(2)}) collective-permute-start(bf16[4,128]{1,0:T(4,128)(2,1)S(1)} %copy-done.8), channel_id=1, source_target_pairs={{0,1},{1,0},{2,3},{3,2},{4,5},{5,4},{6,7},{7,6},{8,9},{9,8},{10,11... | collective-permute-start | bytes 3080 | tf_op jit(solution)/shard_map/ppermute | solution.py:23
  31.1 6.1 %collective-permute-start.4 = (bf16[8,4096]{1,0:T(8,128)(2,1)S(1)}, bf16[8,4096]{1,0:T(8,128)(2,1)S(1)}, u32[]{:S(2)}, u32[]{:S(2)}) collective-permute-start(bf16[8,4096]{1,0:T(8,128)(2,1)S(1)} %slice.82), channel_id=1, source_target_pairs={{7,11},{15,19},{23,27}} | collective-permute-start | bytes 196616 | tf_op jit(solution)/shard_map/ppermute | solution.py:37
  31.9 5.4 %collective-permute-start.5 = (bf16[8,4096]{1,0:T(8,128)(2,1)S(1)}, bf16[8,4096]{1,0:T(8,128)(2,1)S(1)}, u32[]{:S(2)}, u32[]{:S(2)}) collective-permute-start(bf16[8,4096]{1,0:T(8,128)(2,1)S(1)} %slice.82), channel_id=1, source_target_pairs={{7,12},{15,20},{23,28}} | collective-permute-start | bytes 196616 | tf_op jit(solution)/shard_map/ppermute | solution.py:37
  32.5 4.8 %copy-start.4 = (bf16[4096,256]{1,0:T(8,128)(2,1)S(1)}, bf16[4096,256]{1,0:T(8,128)(2,1)}, u32[]{:S(2)}) copy-start(bf16[4096,256]{1,0:T(8,128)(2,1)} %get-tuple-element.54) | copy-start | bytes 6291460
  33.9 3.4 %collective-permute-start.6 = (bf16[8,4096]{1,0:T(8,128)(2,1)S(1)}, bf16[8,4096]{1,0:T(8,128)(2,1)S(1)}, u32[]{:S(2)}, u32[]{:S(2)}) collective-permute-start(bf16[8,4096]{1,0:T(8,128)(2,1)S(1)} %slice.82), channel_id=1, source_target_pairs={{7,13},{15,21},{23,29}} | collective-permute-start | bytes 196616 | tf_op jit(solution)/shard_map/ppermute | solution.py:37
  34.6 2.7 %collective-permute-start.7 = (bf16[8,4096]{1,0:T(8,128)(2,1)S(1)}, bf16[8,4096]{1,0:T(8,128)(2,1)S(1)}, u32[]{:S(2)}, u32[]{:S(2)}) collective-permute-start(bf16[8,4096]{1,0:T(8,128)(2,1)S(1)} %slice.82), channel_id=1, source_target_pairs={{7,14},{15,22},{23,30}} | collective-permute-start | bytes 196616 | tf_op jit(solution)/shard_map/ppermute | solution.py:37
  35.3 2.0 collective-permute-start.8
  39.6 56.8 %slice-start = ((bf16[256,4096]{1,0:T(8,128)(2,1)}), bf16[256,2048]{1,0:T(8,128)(2,1)S(1)}, s32[]{:S(2)}) async-start(bf16[256,4096]{1,0:T(8,128)(2,1)} %param.24), calls=%async_computation.3 | async-start | bytes 2097152 | tf_op jit(solution)/shard_map/slice | solution.py:322
  96.4 27.7 %collective-permute-start.10 = (bf16[256,512]{1,0:T(8,128)(2,1)S(1)}, bf16[256,512]{1,0:T(8,128)(2,1)}, u32[]{:S(2)}, u32[]{:S(2)}) collective-permute-start(bf16[256,512]{1,0:T(8,128)(2,1)S(1)} %constant_dynamic-slice_fusion.3), channel_id=1, source_target_pairs={{0,2},{1,3},{2,0},{3,1},{4,6},{5,7},{6,4},{7,5},{8,10},{9,11},{10,... | collective-permute-start | bytes 786440 | tf_op jit(solution)/shard_map/ppermute | solution.py:29
  96.4 27.6 %collective-permute-start.11 = (bf16[256,512]{1,0:T(8,128)(2,1)S(1)}, bf16[256,512]{1,0:T(8,128)(2,1)S(1)}, u32[]{:S(2)}, u32[]{:S(2)}) collective-permute-start(bf16[256,512]{1,0:T(8,128)(2,1)S(1)} %constant_dynamic-slice_fusion.3), channel_id=1, source_target_pairs={{0,4},{1,5},{2,6},{3,7},{4,0},{5,1},{6,2},{7,3},{8,12},{9,13},{10,... | collective-permute-start | bytes 786440 | tf_op jit(solution)/shard_map/ppermute | solution.py:29
  98.9 25.2 %collective-permute-start.12 = (bf16[256,512]{1,0:T(8,128)(2,1)S(1)}, bf16[256,512]{1,0:T(8,128)(2,1)S(1)}, u32[]{:S(2)}, u32[]{:S(2)}) collective-permute-start(bf16[256,512]{1,0:T(8,128)(2,1)S(1)} %constant_dynamic-slice_fusion.3), channel_id=1, source_target_pairs={{0,6},{1,7},{2,4},{3,5},{4,2},{5,3},{6,0},{7,1},{8,14},{9,15},{10,... | collective-permute-start | bytes 786440 | tf_op jit(solution)/shard_map/ppermute | solution.py:29
  124.0 13.0 %copy-start.9 = (f32[256]{0:T(256)S(1)}, f32[256]{0:T(256)}, u32[]{:S(2)}) copy-start(f32[256]{0:T(256)} %param.23) | copy-start | bytes 3076
  124.1 7.7 %collective-permute-start.13 = (f32[136,256]{1,0:T(8,128)S(1)}, f32[136,256]{1,0:T(8,128)S(1)}, u32[]{:S(2)}, u32[]{:S(2)}) collective-permute-start(f32[136,256]{1,0:T(8,128)S(1)} %get-tuple-element.37), channel_id=1, source_target_pairs={{0,8},{8,16},{16,24},{1,9},{9,17},{17,25},{2,10},{10,18},{18,26},{... | collective-permute-start | bytes 417800 | tf_op jit(solution)/shard_map/ppermute | solution.py:211
  127.5 6.4 %collective-permute-start.14 = (f32[136,256]{1,0:T(8,128)S(1)}, f32[136,256]{1,0:T(8,128)S(1)}, u32[]{:S(2)}, u32[]{:S(2)}) collective-permute-start(f32[136,256]{1,0:T(8,128)S(1)} %get-tuple-element.37), channel_id=1, source_target_pairs={{0,16},{8,24},{1,17},{9,25},{2,18},{10,26},{3,19},{11,27},{4,20},{... | collective-permute-start | bytes 417800 | tf_op jit(solution)/shard_map/ppermute | solution.py:211
  130.2 3.9 %collective-permute-start.15 = (f32[136,256]{1,0:T(8,128)S(1)}, f32[136,256]{1,0:T(8,128)S(1)}, u32[]{:S(2)}, u32[]{:S(2)}) collective-permute-start(f32[136,256]{1,0:T(8,128)S(1)} %get-tuple-element.37), channel_id=1, source_target_pairs={{0,24},{1,25},{2,26},{3,27},{4,28},{5,29},{6,30},{7,31}} | collective-permute-start | bytes 417800 | tf_op jit(solution)/shard_map/ppermute | solution.py:211
  135.7 1.2 collective-permute-start.16
  141.9 40.4 %collective-permute-start.32 = (bf16[256,512]{1,0:T(8,128)(2,1)}, bf16[256,512]{1,0:T(8,128)(2,1)S(1)}, u32[]{:S(2)}, u32[]{:S(2)}) collective-permute-start(bf16[256,512]{1,0:T(8,128)(2,1)} %collective-permute-done.10), channel_id=1, source_target_pairs={{0,24},{8,16},{16,8},{24,0},{1,25},{9,17},{17,9},{25,1},{2,26},{10... | collective-permute-start | bytes 786440 | tf_op jit(solution)/shard_map/ppermute | solution.py:29
  145.6 46.9 %collective-permute-start.27 = (bf16[256,512]{1,0:T(8,128)(2,1)}, bf16[256,512]{1,0:T(8,128)(2,1)S(1)}, u32[]{:S(2)}, u32[]{:S(2)}) collective-permute-start(bf16[256,512]{1,0:T(8,128)(2,1)} %collective-permute-done.10), channel_id=1, source_target_pairs={{0,16},{8,24},{16,0},{24,8},{1,17},{9,25},{17,1},{25,9},{2,18},{10... | collective-permute-start | bytes 786440 | tf_op jit(solution)/shard_map/ppermute | solution.py:29
  145.6 45.7 %collective-permute-start.34 = (bf16[256,512]{1,0:T(8,128)(2,1)S(1)}, bf16[256,512]{1,0:T(8,128)(2,1)S(1)}, u32[]{:S(2)}, u32[]{:S(2)}) collective-permute-start(bf16[256,512]{1,0:T(8,128)(2,1)S(1)} %collective-permute-done.12), channel_id=1, source_target_pairs={{0,24},{8,16},{16,8},{24,0},{1,25},{9,17},{17,9},{25,1},{2,26},{10... | collective-permute-start | bytes 786440 | tf_op jit(solution)/shard_map/ppermute | solution.py:29
  147.2 44.8 %collective-permute-start.31 = (bf16[256,512]{1,0:T(8,128)(2,1)S(1)}, bf16[256,512]{1,0:T(8,128)(2,1)S(1)}, u32[]{:S(2)}, u32[]{:S(2)}) collective-permute-start(bf16[256,512]{1,0:T(8,128)(2,1)S(1)} %constant_dynamic-slice_fusion.3), channel_id=1, source_target_pairs={{0,24},{8,16},{16,8},{24,0},{1,25},{9,17},{17,9},{25,1},{2,26},{10... | collective-permute-start | bytes 786440 | tf_op jit(solution)/shard_map/ppermute | solution.py:29
  148.5 7.8 %collective-permute-start.17 = (bf16[256,256]{1,0:T(8,128)(2,1)S(1)}, bf16[256,256]{1,0:T(8,128)(2,1)S(1)}, u32[]{:S(2)}, u32[]{:S(2)}) collective-permute-start(bf16[256,256]{1,0:T(8,128)(2,1)S(1)} %get-tuple-element.59), channel_id=1, source_target_pairs={{0,2},{1,3},{2,0},{3,1},{4,6},{5,7},{6,4},{7,5},{8,10},{9,11},{10,... | collective-permute-start | bytes 393224 | tf_op jit(solution)/shard_map/ppermute | solution.py:29
  156.4 9.9 %collective-permute-start.19 = (bf16[256,256]{1,0:T(8,128)(2,1)S(1)}, bf16[256,256]{1,0:T(8,128)(2,1)S(1)}, u32[]{:S(2)}, u32[]{:S(2)}) collective-permute-start(bf16[256,256]{1,0:T(8,128)(2,1)S(1)} %get-tuple-element.58), channel_id=1, source_target_pairs={{0,6},{1,7},{2,4},{3,5},{4,2},{5,3},{6,0},{7,1},{8,14},{9,15},{10,... | collective-permute-start | bytes 393224 | tf_op jit(solution)/shard_map/ppermute | solution.py:29
  166.2 15.9 %collective-permute-start.18 = (bf16[256,256]{1,0:T(8,128)(2,1)S(1)}, bf16[256,256]{1,0:T(8,128)(2,1)S(1)}, u32[]{:S(2)}, u32[]{:S(2)}) collective-permute-start(bf16[256,256]{1,0:T(8,128)(2,1)S(1)} %get-tuple-element.57), channel_id=1, source_target_pairs={{0,4},{1,5},{2,6},{3,7},{4,0},{5,1},{6,2},{7,3},{8,12},{9,13},{10,... | collective-permute-start | bytes 393224 | tf_op jit(solution)/shard_map/ppermute | solution.py:29
  182.1 7.4 %collective-permute-start.33 = (bf16[256,512]{1,0:T(8,128)(2,1)S(1)}, bf16[256,512]{1,0:T(8,128)(2,1)S(1)}, u32[]{:S(2)}, u32[]{:S(2)}) collective-permute-start(bf16[256,512]{1,0:T(8,128)(2,1)S(1)} %collective-permute-done.11), channel_id=1, source_target_pairs={{0,24},{8,16},{16,8},{24,0},{1,25},{9,17},{17,9},{25,1},{2,26},{10... | collective-permute-start | bytes 786440 | tf_op jit(solution)/shard_map/ppermute | solution.py:29
  182.4 12.3 %collective-permute-start.28 = (bf16[256,512]{1,0:T(8,128)(2,1)S(1)}, bf16[256,512]{1,0:T(8,128)(2,1)S(1)}, u32[]{:S(2)}, u32[]{:S(2)}) collective-permute-start(bf16[256,512]{1,0:T(8,128)(2,1)S(1)} %collective-permute-done.11), channel_id=1, source_target_pairs={{0,16},{8,24},{16,0},{24,8},{1,17},{9,25},{17,1},{25,9},{2,18},{10... | collective-permute-start | bytes 786440 | tf_op jit(solution)/shard_map/ppermute | solution.py:29
  189.5 10.6 %collective-permute-start.29 = (bf16[256,512]{1,0:T(8,128)(2,1)S(1)}, bf16[256,512]{1,0:T(8,128)(2,1)S(1)}, u32[]{:S(2)}, u32[]{:S(2)}) collective-permute-start(bf16[256,512]{1,0:T(8,128)(2,1)S(1)} %collective-permute-done.12), channel_id=1, source_target_pairs={{0,16},{8,24},{16,0},{24,8},{1,17},{9,25},{17,1},{25,9},{2,18},{10... | collective-permute-start | bytes 786440 | tf_op jit(solution)/shard_map/ppermute | solution.py:29
  191.3 12.9 %collective-permute-start.26 = (bf16[256,512]{1,0:T(8,128)(2,1)S(1)}, bf16[256,512]{1,0:T(8,128)(2,1)S(1)}, u32[]{:S(2)}, u32[]{:S(2)}) collective-permute-start(bf16[256,512]{1,0:T(8,128)(2,1)S(1)} %constant_dynamic-slice_fusion.3), channel_id=1, source_target_pairs={{0,16},{8,24},{16,0},{24,8},{1,17},{9,25},{17,1},{25,9},{2,18},{10... | collective-permute-start | bytes 786440 | tf_op jit(solution)/shard_map/ppermute | solution.py:29
  192.0 12.4 %collective-permute-start.22 = (bf16[256,512]{1,0:T(8,128)(2,1)}, bf16[256,512]{1,0:T(8,128)(2,1)S(1)}, u32[]{:S(2)}, u32[]{:S(2)}) collective-permute-start(bf16[256,512]{1,0:T(8,128)(2,1)} %collective-permute-done.10), channel_id=1, source_target_pairs={{0,8},{8,0},{16,24},{24,16},{1,9},{9,1},{17,25},{25,17},{2,10},{10... | collective-permute-start | bytes 786440 | tf_op jit(solution)/shard_map/ppermute | solution.py:29
  192.5 14.6 %collective-permute-start.23 = (bf16[256,512]{1,0:T(8,128)(2,1)S(1)}, bf16[256,512]{1,0:T(8,128)(2,1)S(1)}, u32[]{:S(2)}, u32[]{:S(2)}) collective-permute-start(bf16[256,512]{1,0:T(8,128)(2,1)S(1)} %collective-permute-done.11), channel_id=1, source_target_pairs={{0,8},{8,0},{16,24},{24,16},{1,9},{9,1},{17,25},{25,17},{2,10},{10... | collective-permute-start | bytes 786440 | tf_op jit(solution)/shard_map/ppermute | solution.py:29
  194.7 15.2 %collective-permute-start.24 = (bf16[256,512]{1,0:T(8,128)(2,1)S(1)}, bf16[256,512]{1,0:T(8,128)(2,1)S(1)}, u32[]{:S(2)}, u32[]{:S(2)}) collective-permute-start(bf16[256,512]{1,0:T(8,128)(2,1)S(1)} %collective-permute-done.12), channel_id=1, source_target_pairs={{0,8},{8,0},{16,24},{24,16},{1,9},{9,1},{17,25},{25,17},{2,10},{10... | collective-permute-start | bytes 786440 | tf_op jit(solution)/shard_map/ppermute | solution.py:29
  200.1 12.5 %collective-permute-start.21 = (bf16[256,512]{1,0:T(8,128)(2,1)S(1)}, bf16[256,512]{1,0:T(8,128)(2,1)S(1)}, u32[]{:S(2)}, u32[]{:S(2)}) collective-permute-start(bf16[256,512]{1,0:T(8,128)(2,1)S(1)} %constant_dynamic-slice_fusion.3), channel_id=1, source_target_pairs={{0,8},{8,0},{16,24},{24,16},{1,9},{9,1},{17,25},{25,17},{2,10},{10... | collective-permute-start | bytes 786440 | tf_op jit(solution)/shard_map/ppermute | solution.py:29
  204.2 8.8 %collective-permute-start.20 = (bf16[128,512]{1,0:T(8,128)(2,1)S(1)}, bf16[128,512]{1,0:T(8,128)(2,1)S(1)}, u32[]{:S(2)}, u32[]{:S(2)}) collective-permute-start(bf16[128,512]{1,0:T(8,128)(2,1)S(1)} %dynamic-slice_convert_fusion.3), channel_id=1, source_target_pairs={{0,1},{1,0},{2,3},{3,2},{4,5},{5,4},{6,7},{7,6},{8,9},{9,8},{10,11... | collective-permute-start | bytes 393224 | tf_op jit(solution)/shard_map/ppermute | solution.py:29
  204.4 10.1 %collective-permute-start.35 = (bf16[128,512]{1,0:T(8,128)(2,1)S(1)}, bf16[128,512]{1,0:T(8,128)(2,1)S(1)}, u32[]{:S(2)}, u32[]{:S(2)}) collective-permute-start(bf16[128,512]{1,0:T(8,128)(2,1)S(1)} %dynamic-slice_convert_fusion), channel_id=1, source_target_pairs={{0,1},{1,0},{2,3},{3,2},{4,5},{5,4},{6,7},{7,6},{8,9},{9,8},{10,11... | collective-permute-start | bytes 393224 | tf_op jit(solution)/shard_map/ppermute | solution.py:29
  207.0 7.4 %collective-permute-start.30 = (bf16[128,512]{1,0:T(8,128)(2,1)S(1)}, bf16[128,512]{1,0:T(8,128)(2,1)S(1)}, u32[]{:S(2)}, u32[]{:S(2)}) collective-permute-start(bf16[128,512]{1,0:T(8,128)(2,1)S(1)} %dynamic-slice_convert_fusion.1), channel_id=1, source_target_pairs={{0,1},{1,0},{2,3},{3,2},{4,5},{5,4},{6,7},{7,6},{8,9},{9,8},{10,11... | collective-permute-start | bytes 393224 | tf_op jit(solution)/shard_map/ppermute | solution.py:29
  212.9 1.4 collective-permute-start.25
  (4 other events, 13.5 us)
Sparse Core Ops, SparseCore 0:
  10.9 85.4 all-gather.1
  141.9 58.2 reduce-scatter.1

commit v4 on v3

--- a/solution.py
+++ b/solution.py
@@ -39,10 +39,9 @@
     return total
 
 
-def spread_along(weight, spans, chips):
+def own_columns(weight, spans):
     cols = weight.shape[1] // spans
-    own = lax.dynamic_slice_in_dim(weight, lax.axis_index("seq") * cols, cols, axis=1)
-    return [crossed(own, "tp", 2 * d) for d in range(chips)]
+    return lax.dynamic_slice_in_dim(weight, lax.axis_index("seq") * cols, cols, axis=1)
 
 
 def silu(v):
@@ -218,7 +217,7 @@
 
 
 def project_out(hidden, mixed, weights):
-    rows, spans, chips = hidden.shape[0], len(weights), len(weights[0])
+    rows, spans, chips = hidden.shape[0], len(weights), lax.axis_size("tp") // 2
     chip, core = lax.axis_index("tp") // 2, lax.axis_index("tp") % 2
     span = lax.axis_index("seq")
     cols = hidden.shape[1] // spans
@@ -226,6 +225,7 @@
     for d in range(chips):
         block = lax.dynamic_slice_in_dim(mixed, (chip ^ d) * 2 * rows, 2 * rows, axis=0)
         taken.append(crossed(block, "tp", 2 * d))
+    taken = (taken[0], jnp.concatenate(taken[1:], axis=1))
     out = jnp.zeros(hidden.shape, jnp.bfloat16)
     for e in range(spans):
         part = sum(
@@ -286,7 +286,9 @@
         axis=1,
     )
     spans, chips = lax.axis_size("seq"), lax.axis_size("tp") // 2
-    summed = width // 2
+    summed = width - 3 * width // 8
+    own = own_columns(output_weight[:, summed:], spans)
+    first = [crossed(own, "seq", e) for e in range(spans)]
     tail = tail_of_previous(normed[rows - 8 :])
     pad_heads = ((0, 0), (0, LANES - heads_dev))
     matrix = jnp.concatenate(
@@ -319,17 +321,17 @@
     skip = jnp.repeat(skip_gain, head_dim)[None]
     matrix, before, aux, row_seg = lax.optimization_barrier((matrix, before, aux, row_seg))
     piece = lax.all_gather(normed, "tp", axis=0, tiled=True)
-    piece, moved = lax.optimization_barrier((piece, output_weight[:, summed:]))
-    along = spread_along(moved, spans, chips)
+    piece, first, own = lax.optimization_barrier((piece, first, own))
+    along = [crossed(own, "tp", 2 * d) for d in range(1, chips)]
     projected = jnp.dot(piece, matrix, preferred_element_type=jnp.float32)
     y, c_map, w_span, packed = local_scan(
         heads_dev, state_dim, projected, before, aux, row_seg, filters.astype(jnp.float32),
         bias, rate, skip,
     )
-    packed, along = lax.optimization_barrier((packed, along))
+    packed, along = lax.optimization_barrier((packed, jnp.concatenate(along, axis=0)))
     incoming = entering_state(packed, state_dim)
     incoming, along = lax.optimization_barrier((incoming, along))
-    weights = [[crossed(part, "seq", e) for part in along] for e in range(spans)]
+    weights = [(first[e], crossed(along, "seq", e)) for e in range(spans)]
     gated, squares = gate_all(
         heads_dev, y, c_map, w_span, projected, conv_dim // inner_dev, incoming
     )

time: 224 us -> 219 us (0.978); the launches traced: 224 us -> 216 us
  waiting for transfers between devices: 103 us -> 96.6 us
  starting transfers between devices: 39.9 us -> 35 us
  matrix products: 22 us -> 24.4 us
    reduce_scatter x1, waiting for transfers between devices: 0.02 us -> 23.3 us  [body(): mine = lax.psum_scatter(partial_out, 'tp', scatter_dimension=0, tiled=True)]
    ppermute x22 -> x16, waiting for transfers between devices: 45.7 us -> 26 us  [crossed(): lax.ppermute(block, axis, [(i, i ^ mask) for i in range(lax.axis_size(axi...]
    all_gather x1, waiting for transfers between devices: 53.6 us -> 43.2 us  [body(): piece = lax.all_gather(normed, 'tp', axis=0, tiled=True)]
    ppermute x22 -> x16, starting transfers between devices: 26.2 us -> 22.3 us  [crossed(): lax.ppermute(block, axis, [(i, i ^ mask) for i in range(lax.axis_size(axi...]
    dot_general x16 -> x8, matrix products: 4.48 us -> 6.2 us  [project_out(): jnp.dot(m, w, preferred_element_type=jnp.float32)]
    unnamed x29 -> x37, local copies, waits for them, and re-layouts: 7.32 us -> 6.85 us
  transfers between devices with their start and end apart: 38 -> 32, of which waited for: 14 -> 12; matrix products, arithmetic and copies ran while one was open for 19% -> 21% of each run, Pallas kernels for 5% -> 5%
where the time goes in v4:
time: 219 us; the launch traced here: 216 us
  waiting for transfers between devices  96.6 us (44%)
  starting transfers between devices  35 us (16%)
  matrix products  24.4 us (11%)
  local copies, waits for them, and re-layouts  21.5 us (10%)
  between operations  14 us (6%)
  other arithmetic  12.5 us (6%)
  Pallas kernels  12.2 us (6%)
    all_gather x1, waiting for transfers between devices, body(): piece = lax.all_gather(normed, 'tp', axis=0, tiled=True)  43.2 us
    ppermute x16, waiting for transfers between devices, crossed(): lax.ppermute(block, axis, [(i, i ^ mask) for i in range(lax.axis_size(axi...  26 us
    reduce_scatter x1, waiting for transfers between devices, body(): mine = lax.psum_scatter(partial_out, 'tp', scatter_dimension=0, tiled=True)  23.3 us
    ppermute x16, starting transfers between devices, crossed(): lax.ppermute(block, axis, [(i, i ^ mask) for i in range(lax.axis_size(axi...  22.3 us
    dot_general x1, matrix products, body(): projected = jnp.dot(piece, matrix, preferred_element_type=jnp.float32)  12.3 us
    pallas_call x1, Pallas kernels, local_scan(): pl.pallas_call(lambda *refs: scan_kernel(heads, *refs), grid=(length // S...  10.8 us
    slice x1, local copies, waits for them, and re-layouts, body(): inner_weight[:, 0, :]  10.1 us
    unnamed x37, local copies, waits for them, and re-layouts  6.85 us
  transfers between devices with their start and end apart: 32, of which 12 were waited for; matrix products, arithmetic and copies ran while one was open for 21% of the time, Pallas kernels for 5%

profile of v4, /device:TPU:0, one launch (start us, length us, event | category | flops | bytes accessed | tf_op | source)
XLA Modules:
  0.0 216.2 jit_solution(8243479518624400754)
XLA Ops:
  6.6 1.6 fusion.6
  8.3 2.5 %fusion.8 = bf16[128,4096]{1,0:T(8,128)(2,1)} fusion(bf16[128,4096]{1,0:T(8,128)(2,1)} %param.13, f32[4096]{0:T(1024)} %param.14, f32[128]{0:T(128)S(1)} %add_rsqrt_fusion.1), kind=kLoop, calls=%fused_computation.11 | loop fusion | flops 2097152 | bytes 2114048 | tf_op jit(solution)/shard_map/convert_element_type | solution.py:274
  10.9 0.8 slice.82
  14.3 1.4 copy.23
  16.8 0.8 pad_add_fusion
  17.8 0.7 constant_dynamic-slice_fusion.3
  18.5 0.8 compare_convert_fusion
  19.3 10.1 %fusion.45 = (bf16[4096,1,256]{2,1,0:T(2,128)(2,1)}, bf16[4096,1,256]{2,1,0:T(2,128)(2,1)S(1)}) fusion(bf16[4096,2,256]{2,1,0:T(2,128)(2,1)} %param.15), kind=kLoop, calls=%fused_computation.97 | loop fusion | bytes 8388608 | tf_op jit(solution)/shard_map/slice | solution.py:297
  29.4 2.6 %constant_dynamic-update-slice_fusion.2 = (bf16[4096,896]{1,0:T(8,128)(2,1)}, bf16[4096,256]{1,0:T(8,128)(2,1)}) fusion(bf16[4096,1,256]{2,1,0:T(2,128)(2,1)S(1)} %get-tuple-element.52), kind=kLoop, calls=%fused_computation.62 | loop fusion | bytes 6291456
  33.5 1.3 constant_dynamic-update-slice_fusion.1
  34.8 1.3 constant_dynamic-update-slice_fusion
  36.4 1.8 fusion.9
  40.2 1.3 pad_dynamic-update-slice_fusion
  41.5 3.3 %collective-permute-start = (bf16[256,384]{1,0:T(8,128)(2,1)}, bf16[256,384]{1,0:T(8,128)(2,1)S(1)}, u32[]{:S(2)}, u32[]{:S(2)}) collective-permute-start(bf16[256,384]{1,0:T(8,128)(2,1)} %constant_dynamic-slice_fusion.3), channel_id=1, source_target_pairs={{0,8},{8,0},{16,24},{24,16},{1,9},{9,1},{17,25},{25,17},{2,10},{10... | collective-permute-start | bytes 589832 | tf_op jit(solution)/shard_map/ppermute | solution.py:29
  44.9 1.5 collective-permute-start.1
  46.4 0.7 fusion.refs_1_
  47.3 2.0 collective-permute-done
  49.3 1.5 collective-permute-done.1
  50.8 3.8 %collective-permute-done.2 = bf16[256,384]{1,0:T(8,128)(2,1)S(1)} collective-permute-done((bf16[256,384]{1,0:T(8,128)(2,1)}, bf16[256,384]{1,0:T(8,128)(2,1)S(1)}, u32[]{:S(2)}, u32[]{:S(2)}) %collective-permute-start.2) | collective-permute-done | bytes 196640 | tf_op jit(solution)/shard_map/ppermute | solution.py:29
  54.6 43.2 %all-gather.2.cloned.1.call-done = bf16[1024,4096]{1,0:T(8,128)(2,1)} async-done(((bf16[128,4096]{1,0:T(8,128)(2,1)}), bf16[1024,4096]{1,0:T(8,128)(2,1)}) %all-gather.2.cloned.1.call-update) | async-done | bytes 8388624 | tf_op jit(solution)/shard_map/all_gather | solution.py:323
  97.8 2.3 %collective-permute-start.14 = (bf16[256,384]{1,0:T(8,128)(2,1)}, bf16[256,384]{1,0:T(8,128)(2,1)S(1)}, u32[]{:S(2)}, u32[]{:S(2)}) collective-permute-start(bf16[256,384]{1,0:T(8,128)(2,1)} %constant_dynamic-slice_fusion.3), channel_id=1, source_target_pairs={{0,4},{1,5},{2,6},{3,7},{4,0},{5,1},{6,2},{7,3},{8,12},{9,13},{10,... | collective-permute-start | bytes 589832 | tf_op jit(solution)/shard_map/ppermute | solution.py:29
  100.1 2.1 collective-permute-start.15
  102.2 12.3 %fusion.46.refs_0_.refs_3_ = f32[1024,896]{1,0:T(8,128)S(1)} fusion(bf16[1024,4096]{1,0:T(8,128)(2,1)} %all-gather.2.cloned.1.call-done, bf16[4096,896]{1,0:T(8,128)(2,1)} %pad_dynamic-update-slice_fusion), kind=kOutput, calls=%fused_computation.98 | convolution fusion | flops 7516192768 | bytes 19398656 | tf_op jit(solution)/shard_map/dot_general | solution.py:326
  114.5 10.8 %local_scan.1 = (f32[1024,256]{1,0:T(8,128)S(1)}, bf16[1024,128]{1,0:T(8,128)(2,1)S(1)}, f32[1024,128]{1,0:T(8,128)S(1)}, f32[136,256]{1,0:T(8,128)S(1)}) custom-call(f32[1024,896]{1,0:T(8,128)S(1)} %fusion.46.refs_0_.refs_3_, f32[8,512]{1,0:T(8,128)S(1)} %fusion.refs_1_, f32[1024,8]{1,0:T(8,128)S(1)} %copy.24.refs_2_, f32[8,1024]{1,0:T(8,128)S(1)} %stack.59.refs_3_, ...), custom_call_target="tpu_custom_call" | custom-call | flops 12000000000 | bytes 8000000 | tf_op jit(solution)/shard_map/local_scan/pallas_call | solution.py:137
  125.4 3.4 %collective-permute-start.16 = (f32[136,256]{1,0:T(8,128)S(1)}, f32[136,256]{1,0:T(8,128)S(1)}, u32[]{:S(2)}, u32[]{:S(2)}) collective-permute-start(f32[136,256]{1,0:T(8,128)S(1)} %get-tuple-element.35), channel_id=1, source_target_pairs={{0,8},{8,16},{16,24},{1,9},{9,17},{17,25},{2,10},{10,18},{18,26},{... | collective-permute-start | bytes 417800 | tf_op jit(solution)/shard_map/ppermute | solution.py:210
  128.8 1.8 collective-permute-start.17
  130.7 1.5 collective-permute-start.18
  132.2 2.9 %collective-permute-done.17 = f32[136,256]{1,0:T(8,128)S(1)} collective-permute-done((f32[136,256]{1,0:T(8,128)S(1)}, f32[136,256]{1,0:T(8,128)S(1)}, u32[]{:S(2)}, u32[]{:S(2)}) %collective-permute-start.17) | collective-permute-done | bytes 139296 | tf_op jit(solution)/shard_map/ppermute | solution.py:210
  135.2 1.4 gate_all.1
  136.8 1.2 collective-permute-done.19
  138.2 5.2 %convolution_convert_fusion = bf16[1024,2560]{1,0:T(8,128)(2,1)} fusion(bf16[1024,256]{1,0:T(8,128)(2,1)S(1)} %multiply_convert_fusion, bf16[256,4096]{1,0:T(8,128)(2,1)} %param.24), kind=kOutput, calls=%fused_computation | convolution fusion | flops 1344798720 | bytes 7077888 | tf_op jit(solution)/shard_map/dot_general | solution.py:342
  144.0 2.4 %collective-permute-start.21 = (bf16[256,256]{1,0:T(8,128)(2,1)S(1)}, bf16[256,256]{1,0:T(8,128)(2,1)S(1)}, u32[]{:S(2)}, u32[]{:S(2)}) collective-permute-start(bf16[256,256]{1,0:T(8,128)(2,1)S(1)} %get-tuple-element.54), channel_id=1, source_target_pairs={{0,4},{1,5},{2,6},{3,7},{4,0},{5,1},{6,2},{7,3},{8,12},{9,13},{10,... | collective-permute-start | bytes 393224 | tf_op jit(solution)/shard_map/ppermute | solution.py:29
  146.4 3.8 %collective-permute-start.28 = (bf16[768,384]{1,0:T(8,128)(2,1)S(1)}, bf16[768,384]{1,0:T(8,128)(2,1)}, u32[]{:S(2)}, u32[]{:S(2)}) collective-permute-start(bf16[768,384]{1,0:T(8,128)(2,1)S(1)} %pad_maximum_fusion.1), channel_id=1, source_target_pairs={{0,24},{8,16},{16,8},{24,0},{1,25},{9,17},{17,9},{25,1},{2,26},{10... | collective-permute-start | bytes 1769480 | tf_op jit(solution)/shard_map/ppermute | solution.py:29
  150.1 1.7 collective-permute-start.22
  152.0 7.8 %collective-permute-done.22 = bf16[256,256]{1,0:T(8,128)(2,1)S(1)} collective-permute-done((bf16[256,256]{1,0:T(8,128)(2,1)S(1)}, bf16[256,256]{1,0:T(8,128)(2,1)S(1)}, u32[]{:S(2)}, u32[]{:S(2)}) %collective-permute-start.22) | collective-permute-done | bytes 131104 | tf_op jit(solution)/shard_map/ppermute | solution.py:29
  160.1 1.1 convolution_add_fusion.3
  161.3 0.7 copy-done.5
  162.2 1.5 collective-permute-start.26
  163.7 2.4 %collective-permute-start.24 = (bf16[768,384]{1,0:T(8,128)(2,1)S(1)}, bf16[768,384]{1,0:T(8,128)(2,1)S(1)}, u32[]{:S(2)}, u32[]{:S(2)}) collective-permute-start(bf16[768,384]{1,0:T(8,128)(2,1)S(1)} %pad_maximum_fusion.1), channel_id=1, source_target_pairs={{0,8},{8,0},{16,24},{24,16},{1,9},{9,1},{17,25},{25,17},{2,10},{10... | collective-permute-start | bytes 1769480 | tf_op jit(solution)/shard_map/ppermute | solution.py:29
  166.2 1.0 fusion.15
  167.2 1.4 fusion.50
  168.7 1.2 convolution_add_fusion
  169.9 9.9 %collective-permute-done.24 = bf16[768,384]{1,0:T(8,128)(2,1)S(1)} collective-permute-done((bf16[768,384]{1,0:T(8,128)(2,1)S(1)}, bf16[768,384]{1,0:T(8,128)(2,1)S(1)}, u32[]{:S(2)}, u32[]{:S(2)}) %collective-permute-start.24) | collective-permute-done | bytes 589856 | tf_op jit(solution)/shard_map/ppermute | solution.py:29
  180.2 1.2 convolution_add_fusion.2
  182.8 0.8 collective-permute-done.27
  183.7 23.3 %reduce-scatter.2.cloned.1.call-done = bf16[128,2560]{1,0:T(8,128)(2,1)} async-done(((bf16[1024,2560]{1,0:T(8,128)(2,1)}), bf16[128,2560]{1,0:T(8,128)(2,1)}) %reduce-scatter.2.cloned.1.call-update) | async-done | bytes 655376 | tf_op jit(solution)/shard_map/reduce_scatter | solution.py:345
  207.0 1.2 add_convert_fusion
  208.3 1.1 pad_maximum_fusion
  (116 shorter events, 11.8 us)
Async XLA Ops:
  6.5 7.2 %copy-start.2 = (bf16[4096,128]{1,0:T(8,128)(2,1)S(1)}, bf16[4096,128]{1,0:T(8,128)(2,1)}, u32[]{:S(2)}) copy-start(bf16[4096,128]{1,0:T(8,128)(2,1)} %param.16) | copy-start | bytes 3145732
  6.5 7.7 %copy-start.11 = (bf16[4,128]{1,0:T(4,128)(2,1)S(1)}, bf16[4,128]{1,0:T(4,128)(2,1)}, u32[]{:S(2)}) copy-start(bf16[4,128]{1,0:T(4,128)(2,1)} %param.21) | copy-start | bytes 3076
  6.5 7.8 %copy-start.9 = (bf16[4096,4]{0,1:T(4,128)(2,1)S(1)}, bf16[4096,4]{0,1:T(4,128)(2,1)}, u32[]{:S(2)}) copy-start(bf16[4096,4]{0,1:T(4,128)(2,1)} %param.17) | copy-start | bytes 98308
  6.5 11.2 %slice-start = ((bf16[256,4096]{1,0:T(8,128)(2,1)}), bf16[256,1536]{1,0:T(8,128)(2,1)S(1)}, s32[]{:S(2)}) async-start(bf16[256,4096]{1,0:T(8,128)(2,1)} %param.24), calls=%async_computation.3 | async-start | bytes 1572864 | tf_op jit(solution)/shard_map/slice | solution.py:290
  6.5 9.2 %copy-start.13 = (f32[4]{0:T(128)S(1)}, f32[4]{0:T(128)}, u32[]{:S(2)}) copy-start(f32[4]{0:T(128)} %param.22) | copy-start | bytes 52
  6.5 9.3 %copy-start.8 = (s32[4096]{0:T(1024)S(1)}, s32[4096]{0:T(1024)}, u32[]{:S(2)}) copy-start(s32[4096]{0:T(1024)} %param.25) | copy-start | bytes 49156
  6.6 91.2 %all-gather.2.cloned.1.call-start = ((), (), s32[]{:S(2)}) async-start(), calls=%async_computation.1 | async-start | bytes 9437184 | tf_op jit(solution)/shard_map/all_gather | solution.py:323
  10.8 196.2 %reduce-scatter.2.cloned.1.call-start = ((), (), s32[]{:S(2)}) async-start(), calls=%async_computation.2 | async-start | bytes 5898240 | tf_op jit(solution)/shard_map/reduce_scatter | solution.py:345
  11.7 26.5 %collective-permute-start.10 = (bf16[8,4096]{1,0:T(8,128)(2,1)S(1)}, bf16[8,4096]{1,0:T(8,128)(2,1)S(1)}, u32[]{:S(2)}, u32[]{:S(2)}) collective-permute-start(bf16[8,4096]{1,0:T(8,128)(2,1)S(1)} %slice.82), channel_id=1, source_target_pairs={{7,14},{15,22},{23,30}} | collective-permute-start | bytes 196616 | tf_op jit(solution)/shard_map/ppermute | solution.py:37
  12.4 26.5 %collective-permute-start.11 = (bf16[8,4096]{1,0:T(8,128)(2,1)S(1)}, bf16[8,4096]{1,0:T(8,128)(2,1)S(1)}, u32[]{:S(2)}, u32[]{:S(2)}) collective-permute-start(bf16[8,4096]{1,0:T(8,128)(2,1)S(1)} %slice.82), channel_id=1, source_target_pairs={{7,15},{15,23},{23,31}} | collective-permute-start | bytes 196616 | tf_op jit(solution)/shard_map/ppermute | solution.py:37
  13.0 26.5 %collective-permute-start.4 = (bf16[8,4096]{1,0:T(8,128)(2,1)S(1)}, bf16[8,4096]{1,0:T(8,128)(2,1)S(1)}, u32[]{:S(2)}, u32[]{:S(2)}) collective-permute-start(bf16[8,4096]{1,0:T(8,128)(2,1)S(1)} %slice.82), channel_id=1, source_target_pairs={{7,8},{15,16},{23,24}} | collective-permute-start | bytes 196616 | tf_op jit(solution)/shard_map/ppermute | solution.py:37
  13.7 19.1 %collective-permute-start.3 = (bf16[4096,128]{1,0:T(8,128)(2,1)S(1)}, bf16[4096,128]{1,0:T(8,128)(2,1)S(1)}, u32[]{:S(2)}, u32[]{:S(2)}) collective-permute-start(bf16[4096,128]{1,0:T(8,128)(2,1)S(1)} %copy-done.2), channel_id=1, source_target_pairs={{0,1},{1,0},{2,3},{3,2},{4,5},{5,4},{6,7},{7,6},{8,9},{9,8},{10,11... | collective-permute-start | bytes 3145736 | tf_op jit(solution)/shard_map/ppermute | solution.py:23
  14.2 17.9 %collective-permute-start.12 = (bf16[4,128]{1,0:T(4,128)(2,1)S(1)}, bf16[4,128]{1,0:T(4,128)(2,1)S(1)}, u32[]{:S(2)}, u32[]{:S(2)}) collective-permute-start(bf16[4,128]{1,0:T(4,128)(2,1)S(1)} %copy-done.11), channel_id=1, source_target_pairs={{0,1},{1,0},{2,3},{3,2},{4,5},{5,4},{6,7},{7,6},{8,9},{9,8},{10,11... | collective-permute-start | bytes 3080 | tf_op jit(solution)/shard_map/ppermute | solution.py:23
  29.4 2.6 %copy-start.14 = (f32[4]{0:T(128)S(1)}, f32[4]{0:T(128)}, u32[]{:S(2)}) copy-start(f32[4]{0:T(128)} %param.18) | copy-start | bytes 52
  29.4 2.6 %copy-start.15 = (f32[4]{0:T(128)S(1)}, f32[4]{0:T(128)}, u32[]{:S(2)}) copy-start(f32[4]{0:T(128)} %param.19) | copy-start | bytes 52
  29.4 3.4 %copy-start.10 = (bf16[4,256]{1,0:T(4,128)(2,1)S(1)}, bf16[4,256]{1,0:T(4,128)(2,1)}, u32[]{:S(2)}) copy-start(bf16[4,256]{1,0:T(4,128)(2,1)} %param.20) | copy-start | bytes 6148
  32.1 9.4 %collective-permute-start.5 = (bf16[8,4096]{1,0:T(8,128)(2,1)S(1)}, bf16[8,4096]{1,0:T(8,128)(2,1)S(1)}, u32[]{:S(2)}, u32[]{:S(2)}) collective-permute-start(bf16[8,4096]{1,0:T(8,128)(2,1)S(1)} %slice.82), channel_id=1, source_target_pairs={{7,9},{15,17},{23,25}} | collective-permute-start | bytes 196616 | tf_op jit(solution)/shard_map/ppermute | solution.py:37
  32.9 12.0 %collective-permute-start.6 = (bf16[8,4096]{1,0:T(8,128)(2,1)S(1)}, bf16[8,4096]{1,0:T(8,128)(2,1)S(1)}, u32[]{:S(2)}, u32[]{:S(2)}) collective-permute-start(bf16[8,4096]{1,0:T(8,128)(2,1)S(1)} %slice.82), channel_id=1, source_target_pairs={{7,10},{15,18},{23,26}} | collective-permute-start | bytes 196616 | tf_op jit(solution)/shard_map/ppermute | solution.py:37
  33.5 2.9 %copy-start = (bf16[4096,1,256]{2,1,0:T(2,128)(2,1)S(1)}, bf16[4096,1,256]{2,1,0:T(2,128)(2,1)}, u32[]{:S(2)}) copy-start(bf16[4096,1,256]{2,1,0:T(2,128)(2,1)} %get-tuple-element.51) | copy-start | bytes 6291460
  36.1 4.1 %copy-start.3 = (bf16[4096,4]{1,0:T(8,128)(2,1)S(1)}, bf16[4096,4]{1,0:T(8,128)(2,1)}, u32[]{:S(2)}) copy-start(bf16[4096,4]{1,0:T(8,128)(2,1)} %copy.23) | copy-start | bytes 98308
  36.4 10.0 %copy-start.4 = (bf16[4096,256]{1,0:T(8,128)(2,1)S(1)}, bf16[4096,256]{1,0:T(8,128)(2,1)}, u32[]{:S(2)}) copy-start(bf16[4096,256]{1,0:T(8,128)(2,1)} %get-tuple-element.50) | copy-start | bytes 6291460
  38.2 8.1 %collective-permute-start.7 = (bf16[8,4096]{1,0:T(8,128)(2,1)S(1)}, bf16[8,4096]{1,0:T(8,128)(2,1)S(1)}, u32[]{:S(2)}, u32[]{:S(2)}) collective-permute-start(bf16[8,4096]{1,0:T(8,128)(2,1)S(1)} %slice.82), channel_id=1, source_target_pairs={{7,11},{15,19},{23,27}} | collective-permute-start | bytes 196616 | tf_op jit(solution)/shard_map/ppermute | solution.py:37
  38.9 7.5 %collective-permute-start.8 = (bf16[8,4096]{1,0:T(8,128)(2,1)S(1)}, bf16[8,4096]{1,0:T(8,128)(2,1)S(1)}, u32[]{:S(2)}, u32[]{:S(2)}) collective-permute-start(bf16[8,4096]{1,0:T(8,128)(2,1)S(1)} %slice.82), channel_id=1, source_target_pairs={{7,12},{15,20},{23,28}} | collective-permute-start | bytes 196616 | tf_op jit(solution)/shard_map/ppermute | solution.py:37
  39.6 6.8 %collective-permute-start.9 = (bf16[8,4096]{1,0:T(8,128)(2,1)S(1)}, bf16[8,4096]{1,0:T(8,128)(2,1)S(1)}, u32[]{:S(2)}, u32[]{:S(2)}) collective-permute-start(bf16[8,4096]{1,0:T(8,128)(2,1)S(1)} %slice.82), channel_id=1, source_target_pairs={{7,13},{15,21},{23,29}} | collective-permute-start | bytes 196616 | tf_op jit(solution)/shard_map/ppermute | solution.py:37
  41.5 7.7 %collective-permute-start = (bf16[256,384]{1,0:T(8,128)(2,1)}, bf16[256,384]{1,0:T(8,128)(2,1)S(1)}, u32[]{:S(2)}, u32[]{:S(2)}) collective-permute-start(bf16[256,384]{1,0:T(8,128)(2,1)} %constant_dynamic-slice_fusion.3), channel_id=1, source_target_pairs={{0,8},{8,0},{16,24},{24,16},{1,9},{9,1},{17,25},{25,17},{2,10},{10... | collective-permute-start | bytes 589832 | tf_op jit(solution)/shard_map/ppermute | solution.py:29
  44.9 5.9 %collective-permute-start.1 = (bf16[256,384]{1,0:T(8,128)(2,1)}, bf16[256,384]{1,0:T(8,128)(2,1)S(1)}, u32[]{:S(2)}, u32[]{:S(2)}) collective-permute-start(bf16[256,384]{1,0:T(8,128)(2,1)} %constant_dynamic-slice_fusion.3), channel_id=1, source_target_pairs={{0,16},{8,24},{16,0},{24,8},{1,17},{9,25},{17,1},{25,9},{2,18},{10... | collective-permute-start | bytes 589832 | tf_op jit(solution)/shard_map/ppermute | solution.py:29
  46.4 8.2 %collective-permute-start.2 = (bf16[256,384]{1,0:T(8,128)(2,1)}, bf16[256,384]{1,0:T(8,128)(2,1)S(1)}, u32[]{:S(2)}, u32[]{:S(2)}) collective-permute-start(bf16[256,384]{1,0:T(8,128)(2,1)} %constant_dynamic-slice_fusion.3), channel_id=1, source_target_pairs={{0,24},{8,16},{16,8},{24,0},{1,25},{9,17},{17,9},{25,1},{2,26},{10... | collective-permute-start | bytes 589832 | tf_op jit(solution)/shard_map/ppermute | solution.py:29
  49.3 65.2 %copy-start.6 = (bf16[256,384]{1,0:T(8,128)(2,1)}, bf16[256,384]{1,0:T(8,128)(2,1)S(1)}, u32[]{:S(2)}) copy-start(bf16[256,384]{1,0:T(8,128)(2,1)S(1)} %collective-permute-done) | copy-start | bytes 589828
  54.6 59.9 %copy-start.7 = (bf16[256,384]{1,0:T(8,128)(2,1)}, bf16[256,384]{1,0:T(8,128)(2,1)S(1)}, u32[]{:S(2)}) copy-start(bf16[256,384]{1,0:T(8,128)(2,1)S(1)} %collective-permute-done.2) | copy-start | bytes 589828
  97.8 27.6 %collective-permute-start.13 = (bf16[256,384]{1,0:T(8,128)(2,1)}, bf16[256,384]{1,0:T(8,128)(2,1)S(1)}, u32[]{:S(2)}, u32[]{:S(2)}) collective-permute-start(bf16[256,384]{1,0:T(8,128)(2,1)} %constant_dynamic-slice_fusion.3), channel_id=1, source_target_pairs={{0,2},{1,3},{2,0},{3,1},{4,6},{5,7},{6,4},{7,5},{8,10},{9,11},{10,... | collective-permute-start | bytes 589832 | tf_op jit(solution)/shard_map/ppermute | solution.py:29
  97.8 27.6 %collective-permute-start.14 = (bf16[256,384]{1,0:T(8,128)(2,1)}, bf16[256,384]{1,0:T(8,128)(2,1)S(1)}, u32[]{:S(2)}, u32[]{:S(2)}) collective-permute-start(bf16[256,384]{1,0:T(8,128)(2,1)} %constant_dynamic-slice_fusion.3), channel_id=1, source_target_pairs={{0,4},{1,5},{2,6},{3,7},{4,0},{5,1},{6,2},{7,3},{8,12},{9,13},{10,... | collective-permute-start | bytes 589832 | tf_op jit(solution)/shard_map/ppermute | solution.py:29
  100.1 25.3 %collective-permute-start.15 = (bf16[256,384]{1,0:T(8,128)(2,1)}, bf16[256,384]{1,0:T(8,128)(2,1)S(1)}, u32[]{:S(2)}, u32[]{:S(2)}) collective-permute-start(bf16[256,384]{1,0:T(8,128)(2,1)} %constant_dynamic-slice_fusion.3), channel_id=1, source_target_pairs={{0,6},{1,7},{2,4},{3,5},{4,2},{5,3},{6,0},{7,1},{8,14},{9,15},{10,... | collective-permute-start | bytes 589832 | tf_op jit(solution)/shard_map/ppermute | solution.py:29
  125.3 12.7 %copy-start.12 = (f32[256]{0:T(256)S(1)}, f32[256]{0:T(256)}, u32[]{:S(2)}) copy-start(f32[256]{0:T(256)} %param.23) | copy-start | bytes 3076
  125.4 6.7 %collective-permute-start.16 = (f32[136,256]{1,0:T(8,128)S(1)}, f32[136,256]{1,0:T(8,128)S(1)}, u32[]{:S(2)}, u32[]{:S(2)}) collective-permute-start(f32[136,256]{1,0:T(8,128)S(1)} %get-tuple-element.35), channel_id=1, source_target_pairs={{0,8},{8,16},{16,24},{1,9},{9,17},{17,25},{2,10},{10,18},{18,26},{... | collective-permute-start | bytes 417800 | tf_op jit(solution)/shard_map/ppermute | solution.py:210
  128.8 6.3 %collective-permute-start.17 = (f32[136,256]{1,0:T(8,128)S(1)}, f32[136,256]{1,0:T(8,128)S(1)}, u32[]{:S(2)}, u32[]{:S(2)}) collective-permute-start(f32[136,256]{1,0:T(8,128)S(1)} %get-tuple-element.35), channel_id=1, source_target_pairs={{0,16},{8,24},{1,17},{9,25},{2,18},{10,26},{3,19},{11,27},{4,20},{... | collective-permute-start | bytes 417800 | tf_op jit(solution)/shard_map/ppermute | solution.py:210
  130.7 4.4 %collective-permute-start.18 = (f32[136,256]{1,0:T(8,128)S(1)}, f32[136,256]{1,0:T(8,128)S(1)}, u32[]{:S(2)}, u32[]{:S(2)}) collective-permute-start(f32[136,256]{1,0:T(8,128)S(1)} %get-tuple-element.35), channel_id=1, source_target_pairs={{0,24},{1,25},{2,26},{3,27},{4,28},{5,29},{6,30},{7,31}} | collective-permute-start | bytes 417800 | tf_op jit(solution)/shard_map/ppermute | solution.py:210
  136.7 1.2 collective-permute-start.19
  143.4 18.8 %copy-start.1 = (bf16[128,4096]{1,0:T(8,128)(2,1)S(1)}, bf16[128,4096]{1,0:T(8,128)(2,1)}, u32[]{:S(2)}) copy-start(bf16[128,4096]{1,0:T(8,128)(2,1)} %param.13) | copy-start | bytes 3145732
  143.5 8.4 %collective-permute-start.20 = (bf16[256,256]{1,0:T(8,128)(2,1)S(1)}, bf16[256,256]{1,0:T(8,128)(2,1)S(1)}, u32[]{:S(2)}, u32[]{:S(2)}) collective-permute-start(bf16[256,256]{1,0:T(8,128)(2,1)S(1)} %get-tuple-element.55), channel_id=1, source_target_pairs={{0,2},{1,3},{2,0},{3,1},{4,6},{5,7},{6,4},{7,5},{8,10},{9,11},{10,... | collective-permute-start | bytes 393224 | tf_op jit(solution)/shard_map/ppermute | solution.py:29
  144.0 8.0 %collective-permute-start.21 = (bf16[256,256]{1,0:T(8,128)(2,1)S(1)}, bf16[256,256]{1,0:T(8,128)(2,1)S(1)}, u32[]{:S(2)}, u32[]{:S(2)}) collective-permute-start(bf16[256,256]{1,0:T(8,128)(2,1)S(1)} %get-tuple-element.54), channel_id=1, source_target_pairs={{0,4},{1,5},{2,6},{3,7},{4,0},{5,1},{6,2},{7,3},{8,12},{9,13},{10,... | collective-permute-start | bytes 393224 | tf_op jit(solution)/shard_map/ppermute | solution.py:29
  146.4 20.9 %collective-permute-start.28 = (bf16[768,384]{1,0:T(8,128)(2,1)S(1)}, bf16[768,384]{1,0:T(8,128)(2,1)}, u32[]{:S(2)}, u32[]{:S(2)}) collective-permute-start(bf16[768,384]{1,0:T(8,128)(2,1)S(1)} %pad_maximum_fusion.1), channel_id=1, source_target_pairs={{0,24},{8,16},{16,8},{24,0},{1,25},{9,17},{17,9},{25,1},{2,26},{10... | collective-permute-start | bytes 1769480 | tf_op jit(solution)/shard_map/ppermute | solution.py:29
  150.1 9.6 %collective-permute-start.22 = (bf16[256,256]{1,0:T(8,128)(2,1)S(1)}, bf16[256,256]{1,0:T(8,128)(2,1)S(1)}, u32[]{:S(2)}, u32[]{:S(2)}) collective-permute-start(bf16[256,256]{1,0:T(8,128)(2,1)S(1)} %get-tuple-element.53), channel_id=1, source_target_pairs={{0,6},{1,7},{2,4},{3,5},{4,2},{5,3},{6,0},{7,1},{8,14},{9,15},{10,... | collective-permute-start | bytes 393224 | tf_op jit(solution)/shard_map/ppermute | solution.py:29
  162.1 4.1 %collective-permute-start.23 = (bf16[128,384]{1,0:T(8,128)(2,1)S(1)}, bf16[128,384]{1,0:T(8,128)(2,1)}, u32[]{:S(2)}, u32[]{:S(2)}) collective-permute-start(bf16[128,384]{1,0:T(8,128)(2,1)S(1)} %dynamic-slice_convert_fusion.3), channel_id=1, source_target_pairs={{0,1},{1,0},{2,3},{3,2},{4,5},{5,4},{6,7},{7,6},{8,9},{9,8},{10,11... | collective-permute-start | bytes 294920 | tf_op jit(solution)/shard_map/ppermute | solution.py:29
  162.2 19.3 %collective-permute-start.26 = (bf16[768,384]{1,0:T(8,128)(2,1)S(1)}, bf16[768,384]{1,0:T(8,128)(2,1)S(1)}, u32[]{:S(2)}, u32[]{:S(2)}) collective-permute-start(bf16[768,384]{1,0:T(8,128)(2,1)S(1)} %pad_maximum_fusion.1), channel_id=1, source_target_pairs={{0,16},{8,24},{16,0},{24,8},{1,17},{9,25},{17,1},{25,9},{2,18},{10... | collective-permute-start | bytes 1769480 | tf_op jit(solution)/shard_map/ppermute | solution.py:29
  163.7 16.1 %collective-permute-start.24 = (bf16[768,384]{1,0:T(8,128)(2,1)S(1)}, bf16[768,384]{1,0:T(8,128)(2,1)S(1)}, u32[]{:S(2)}, u32[]{:S(2)}) collective-permute-start(bf16[768,384]{1,0:T(8,128)(2,1)S(1)} %pad_maximum_fusion.1), channel_id=1, source_target_pairs={{0,8},{8,0},{16,24},{24,16},{1,9},{9,1},{17,25},{25,17},{2,10},{10... | collective-permute-start | bytes 1769480 | tf_op jit(solution)/shard_map/ppermute | solution.py:29
  169.8 13.8 %collective-permute-start.29 = (bf16[128,384]{1,0:T(8,128)(2,1)S(1)}, bf16[128,384]{1,0:T(8,128)(2,1)S(1)}, u32[]{:S(2)}, u32[]{:S(2)}) collective-permute-start(bf16[128,384]{1,0:T(8,128)(2,1)S(1)} %dynamic-slice_convert_fusion), channel_id=1, source_target_pairs={{0,1},{1,0},{2,3},{3,2},{4,5},{5,4},{6,7},{7,6},{8,9},{9,8},{10,11... | collective-permute-start | bytes 294920 | tf_op jit(solution)/shard_map/ppermute | solution.py:29
  181.4 1.4 collective-permute-start.25
  182.1 1.5 collective-permute-start.27
  (1 other events, 0.7 us)
Sparse Core Ops, SparseCore 0:
  10.9 86.8 all-gather.1
  143.5 63.4 reduce-scatter.1

commit v5 on v4

--- a/solution.py
+++ b/solution.py
@@ -286,7 +286,7 @@
         axis=1,
     )
     spans, chips = lax.axis_size("seq"), lax.axis_size("tp") // 2
-    summed = width - 3 * width // 8
+    summed = width // 2
     own = own_columns(output_weight[:, summed:], spans)
     first = [crossed(own, "seq", e) for e in range(spans)]
     tail = tail_of_previous(normed[rows - 8 :])

time: 219 us -> 210 us (0.959)
  waiting for transfers between devices: 96.6 us -> 80.3 us
  local copies, waits for them, and re-layouts: 21.5 us -> 26.3 us
  other arithmetic: 12.5 us -> 16 us
    reduce_scatter x1, waiting for transfers between devices: 23.3 us -> 6.61 us  [body(): mine = lax.psum_scatter(partial_out, 'tp', scatter_dimension=0, tiled=True)]
    ppermute x16, waiting for transfers between devices: 26 us -> 29.9 us  [crossed(): lax.ppermute(block, axis, [(i, i ^ mask) for i in range(lax.axis_size(axi...]
    all_gather x1, waiting for transfers between devices: 43.2 us -> 39.6 us  [body(): piece = lax.all_gather(normed, 'tp', axis=0, tiled=True)]
    dynamic_update_slice x4, other arithmetic: 1.19 us -> 3.92 us  [project_out(): out = lax.dynamic_update_slice_in_dim(out, done, start, axis=1)]
    slice x2 -> x1, local copies, waits for them, and re-layouts: 0.01 us -> 2.3 us  [body(): own = own_columns(output_weight[:, summed:], spans)]
  transfers between devices with their start and end apart: 32 -> 32, of which waited for: 12 -> 12; matrix products, arithmetic and copies ran while one was open for 21% -> 25% of each run, Pallas kernels for 5% -> 5%
where the time goes in v5:
time: 210 us; the launch traced here: 206 us
  waiting for transfers between devices  80.3 us (38%)
  starting transfers between devices  34.9 us (17%)
  local copies, waits for them, and re-layouts  26.3 us (13%)
  matrix products  22.7 us (11%)
  other arithmetic  16 us (8%)
  between operations  14 us (7%)
  Pallas kernels  12.2 us (6%)
    all_gather x1, waiting for transfers between devices, body(): piece = lax.all_gather(normed, 'tp', axis=0, tiled=True)  39.6 us
    ppermute x16, waiting for transfers between devices, crossed(): lax.ppermute(block, axis, [(i, i ^ mask) for i in range(lax.axis_size(axi...  29.9 us
    ppermute x16, starting transfers between devices, crossed(): lax.ppermute(block, axis, [(i, i ^ mask) for i in range(lax.axis_size(axi...  22.1 us
    dot_general x1, matrix products, body(): projected = jnp.dot(piece, matrix, preferred_element_type=jnp.float32)  12.3 us
    pallas_call x1, Pallas kernels, local_scan(): pl.pallas_call(lambda *refs: scan_kernel(heads, *refs), grid=(length // S...  10.8 us
    slice x1, local copies, waits for them, and re-layouts, body(): inner_weight[:, 0, :]  10.1 us
    ppermute x3, starting transfers between devices, entering_state(): lax.ppermute(packed, 'seq', [(i, i + e) for i in range(spans - e)])  6.69 us
    reduce_scatter x1, waiting for transfers between devices, body(): mine = lax.psum_scatter(partial_out, 'tp', scatter_dimension=0, tiled=True)  6.61 us
  transfers between devices with their start and end apart: 32, of which 12 were waited for; matrix products, arithmetic and copies ran while one was open for 25% of the time, Pallas kernels for 5%

profile of v5, /device:TPU:0, one launch (start us, length us, event | category | flops | bytes accessed | tf_op | source)
XLA Modules:
  0.0 206.3 jit_solution(17435393859424808450)
XLA Ops:
  6.6 1.6 fusion.6
  8.2 2.5 %fusion.8 = bf16[128,4096]{1,0:T(8,128)(2,1)} fusion(bf16[128,4096]{1,0:T(8,128)(2,1)} %param.13, f32[4096]{0:T(1024)} %param.14, f32[128]{0:T(128)S(1)} %add_rsqrt_fusion.1), kind=kLoop, calls=%fused_computation.11 | loop fusion | flops 2097152 | bytes 2114048 | tf_op jit(solution)/shard_map/convert_element_type | solution.py:274
  10.8 0.8 slice.82
  14.3 1.4 copy.23
  15.7 2.3 %slice.63 = bf16[256,2048]{1,0:T(8,128)(2,1)} slice(bf16[256,4096]{1,0:T(8,128)(2,1)} %param.24), slice={[0:256], [2048:4096]} | slice | bytes 2097152 | tf_op jit(solution)/shard_map/slice | solution.py:290
  19.9 1.0 constant_dynamic-slice_fusion.3
  20.9 0.7 compare_convert_fusion
  21.7 10.1 %fusion.45 = (bf16[4096,1,256]{2,1,0:T(2,128)(2,1)}, bf16[4096,1,256]{2,1,0:T(2,128)(2,1)S(1)}) fusion(bf16[4096,2,256]{2,1,0:T(2,128)(2,1)} %param.15), kind=kLoop, calls=%fused_computation.97 | loop fusion | bytes 8388608 | tf_op jit(solution)/shard_map/slice | solution.py:297
  31.8 2.6 %constant_dynamic-update-slice_fusion.2 = (bf16[4096,896]{1,0:T(8,128)(2,1)}, bf16[4096,256]{1,0:T(8,128)(2,1)}) fusion(bf16[4096,1,256]{2,1,0:T(2,128)(2,1)S(1)} %get-tuple-element.52), kind=kLoop, calls=%fused_computation.62 | loop fusion | bytes 6291456
  35.9 1.3 constant_dynamic-update-slice_fusion.1
  37.2 1.4 constant_dynamic-update-slice_fusion
  38.7 1.8 fusion.9
  42.5 1.3 pad_dynamic-update-slice_fusion
  43.8 3.6 %collective-permute-start = (bf16[256,512]{1,0:T(8,128)(2,1)S(1)}, bf16[256,512]{1,0:T(8,128)(2,1)S(1)}, u32[]{:S(2)}, u32[]{:S(2)}) collective-permute-start(bf16[256,512]{1,0:T(8,128)(2,1)S(1)} %constant_dynamic-slice_fusion.3), channel_id=1, source_target_pairs={{0,8},{8,0},{16,24},{24,16},{1,9},{9,1},{17,25},{25,17},{2,10},{10... | collective-permute-start | bytes 786440 | tf_op jit(solution)/shard_map/ppermute | solution.py:29
  47.4 1.5 collective-permute-start.1
  49.8 2.9 %collective-permute-done = bf16[256,512]{1,0:T(8,128)(2,1)S(1)} collective-permute-done((bf16[256,512]{1,0:T(8,128)(2,1)S(1)}, bf16[256,512]{1,0:T(8,128)(2,1)S(1)}, u32[]{:S(2)}, u32[]{:S(2)}) %collective-permute-start) | collective-permute-done | bytes 262176 | tf_op jit(solution)/shard_map/ppermute | solution.py:29
  52.7 2.6 %collective-permute-done.1 = bf16[256,512]{1,0:T(8,128)(2,1)S(1)} collective-permute-done((bf16[256,512]{1,0:T(8,128)(2,1)S(1)}, bf16[256,512]{1,0:T(8,128)(2,1)S(1)}, u32[]{:S(2)}, u32[]{:S(2)}) %collective-permute-start.1) | collective-permute-done | bytes 262176 | tf_op jit(solution)/shard_map/ppermute | solution.py:29
  55.3 3.0 %collective-permute-done.2 = bf16[256,512]{1,0:T(8,128)(2,1)S(1)} collective-permute-done((bf16[256,512]{1,0:T(8,128)(2,1)S(1)}, bf16[256,512]{1,0:T(8,128)(2,1)S(1)}, u32[]{:S(2)}, u32[]{:S(2)}) %collective-permute-start.2) | collective-permute-done | bytes 262176 | tf_op jit(solution)/shard_map/ppermute | solution.py:29
  58.3 39.6 %all-gather.2.cloned.1.call-done = bf16[1024,4096]{1,0:T(8,128)(2,1)} async-done(((bf16[128,4096]{1,0:T(8,128)(2,1)}), bf16[1024,4096]{1,0:T(8,128)(2,1)}) %all-gather.2.cloned.1.call-update) | async-done | bytes 8388624 | tf_op jit(solution)/shard_map/all_gather | solution.py:323
  97.9 2.3 %collective-permute-start.14 = (bf16[256,512]{1,0:T(8,128)(2,1)S(1)}, bf16[256,512]{1,0:T(8,128)(2,1)S(1)}, u32[]{:S(2)}, u32[]{:S(2)}) collective-permute-start(bf16[256,512]{1,0:T(8,128)(2,1)S(1)} %constant_dynamic-slice_fusion.3), channel_id=1, source_target_pairs={{0,4},{1,5},{2,6},{3,7},{4,0},{5,1},{6,2},{7,3},{8,12},{9,13},{10,... | collective-permute-start | bytes 786440 | tf_op jit(solution)/shard_map/ppermute | solution.py:29
  100.2 2.1 %collective-permute-start.15 = (bf16[256,512]{1,0:T(8,128)(2,1)S(1)}, bf16[256,512]{1,0:T(8,128)(2,1)S(1)}, u32[]{:S(2)}, u32[]{:S(2)}) collective-permute-start(bf16[256,512]{1,0:T(8,128)(2,1)S(1)} %constant_dynamic-slice_fusion.3), channel_id=1, source_target_pairs={{0,6},{1,7},{2,4},{3,5},{4,2},{5,3},{6,0},{7,1},{8,14},{9,15},{10,... | collective-permute-start | bytes 786440 | tf_op jit(solution)/shard_map/ppermute | solution.py:29
  102.3 12.3 %fusion.46.refs_0_.refs_3_ = f32[1024,896]{1,0:T(8,128)S(1)} fusion(bf16[1024,4096]{1,0:T(8,128)(2,1)} %all-gather.2.cloned.1.call-done, bf16[4096,896]{1,0:T(8,128)(2,1)} %pad_dynamic-update-slice_fusion), kind=kOutput, calls=%fused_computation.98 | convolution fusion | flops 7516192768 | bytes 19398656 | tf_op jit(solution)/shard_map/dot_general | solution.py:326
  114.6 10.8 %local_scan.1 = (f32[1024,256]{1,0:T(8,128)S(1)}, bf16[1024,128]{1,0:T(8,128)(2,1)S(1)}, f32[1024,128]{1,0:T(8,128)S(1)}, f32[136,256]{1,0:T(8,128)S(1)}) custom-call(f32[1024,896]{1,0:T(8,128)S(1)} %fusion.46.refs_0_.refs_3_, f32[8,512]{1,0:T(8,128)S(1)} %fusion.refs_1_, f32[1024,8]{1,0:T(8,128)S(1)} %copy.24.refs_2_, f32[8,1024]{1,0:T(8,128)S(1)} %stack.59.refs_3_, ...), custom_call_target="tpu_custom_call" | custom-call | flops 12000000000 | bytes 8000000 | tf_op jit(solution)/shard_map/local_scan/pallas_call | solution.py:137
  125.6 3.4 %collective-permute-start.16 = (f32[136,256]{1,0:T(8,128)S(1)}, f32[136,256]{1,0:T(8,128)S(1)}, u32[]{:S(2)}, u32[]{:S(2)}) collective-permute-start(f32[136,256]{1,0:T(8,128)S(1)} %get-tuple-element.35), channel_id=1, source_target_pairs={{0,8},{8,16},{16,24},{1,9},{9,17},{17,25},{2,10},{10,18},{18,26},{... | collective-permute-start | bytes 417800 | tf_op jit(solution)/shard_map/ppermute | solution.py:210
  128.9 1.8 collective-permute-start.17
  130.8 1.5 collective-permute-start.18
  132.3 2.9 %collective-permute-done.17 = f32[136,256]{1,0:T(8,128)S(1)} collective-permute-done((f32[136,256]{1,0:T(8,128)S(1)}, f32[136,256]{1,0:T(8,128)S(1)}, u32[]{:S(2)}, u32[]{:S(2)}) %collective-permute-start.17) | collective-permute-done | bytes 139296 | tf_op jit(solution)/shard_map/ppermute | solution.py:210
  135.3 1.4 gate_all.1
  136.9 1.2 collective-permute-done.19
  138.3 4.5 %convolution_convert_fusion = bf16[1024,2048]{1,0:T(8,128)(2,1)} fusion(bf16[1024,256]{1,0:T(8,128)(2,1)S(1)} %multiply_convert_fusion, bf16[256,4096]{1,0:T(8,128)(2,1)} %param.24), kind=kOutput, calls=%fused_computation.6 | convolution fusion | flops 1075838976 | bytes 5767168 | tf_op jit(solution)/shard_map/dot_general | solution.py:342
  143.9 2.4 %collective-permute-start.21 = (bf16[256,256]{1,0:T(8,128)(2,1)}, bf16[256,256]{1,0:T(8,128)(2,1)S(1)}, u32[]{:S(2)}, u32[]{:S(2)}) collective-permute-start(bf16[256,256]{1,0:T(8,128)(2,1)} %get-tuple-element.54), channel_id=1, source_target_pairs={{0,4},{1,5},{2,6},{3,7},{4,0},{5,1},{6,2},{7,3},{8,12},{9,13},{10,... | collective-permute-start | bytes 393224 | tf_op jit(solution)/shard_map/ppermute | solution.py:29
  146.2 3.8 %collective-permute-start.28 = (bf16[768,512]{1,0:T(8,128)(2,1)S(1)}, bf16[768,512]{1,0:T(8,128)(2,1)}, u32[]{:S(2)}, u32[]{:S(2)}) collective-permute-start(bf16[768,512]{1,0:T(8,128)(2,1)S(1)} %pad_maximum_fusion.1), channel_id=1, source_target_pairs={{0,24},{8,16},{16,8},{24,0},{1,25},{9,17},{17,9},{25,1},{2,26},{10... | collective-permute-start | bytes 2359304 | tf_op jit(solution)/shard_map/ppermute | solution.py:29
  150.0 1.8 collective-permute-start.22
  151.8 1.5 collective-permute-done.21
  153.3 7.2 %collective-permute-done.22 = bf16[256,256]{1,0:T(8,128)(2,1)S(1)} collective-permute-done((bf16[256,256]{1,0:T(8,128)(2,1)}, bf16[256,256]{1,0:T(8,128)(2,1)S(1)}, u32[]{:S(2)}, u32[]{:S(2)}) %collective-permute-start.22) | collective-permute-done | bytes 131104 | tf_op jit(solution)/shard_map/ppermute | solution.py:29
  160.9 1.0 convolution_add_fusion.3
  161.9 1.6 dynamic-slice_convert_fusion.3
  163.6 1.2 collective-permute-start.26
  164.9 2.4 %collective-permute-start.24 = (bf16[768,512]{1,0:T(8,128)(2,1)S(1)}, bf16[768,512]{1,0:T(8,128)(2,1)S(1)}, u32[]{:S(2)}, u32[]{:S(2)}) collective-permute-start(bf16[768,512]{1,0:T(8,128)(2,1)S(1)} %pad_maximum_fusion.1), channel_id=1, source_target_pairs={{0,8},{8,0},{16,24},{24,16},{1,9},{9,1},{17,25},{25,17},{2,10},{10... | collective-permute-start | bytes 2359304 | tf_op jit(solution)/shard_map/ppermute | solution.py:29
  167.3 0.9 broadcast_in_dim.24
  168.1 1.7 fusion.11
  169.9 1.5 fusion.50
  171.4 1.2 convolution_add_fusion
  172.7 12.5 %collective-permute-done.24 = bf16[768,512]{1,0:T(8,128)(2,1)S(1)} collective-permute-done((bf16[768,512]{1,0:T(8,128)(2,1)S(1)}, bf16[768,512]{1,0:T(8,128)(2,1)S(1)}, u32[]{:S(2)}, u32[]{:S(2)}) %collective-permute-start.24) | collective-permute-done | bytes 786464 | tf_op jit(solution)/shard_map/ppermute | solution.py:29
  188.9 0.7 fusion.14
  189.6 6.6 %reduce-scatter.2.cloned.1.call-done = bf16[128,2048]{1,0:T(8,128)(2,1)} async-done(((bf16[1024,2048]{1,0:T(8,128)(2,1)}), bf16[128,2048]{1,0:T(8,128)(2,1)}) %reduce-scatter.2.cloned.1.call-update) | async-done | bytes 524304 | tf_op jit(solution)/shard_map/reduce_scatter | solution.py:345
  196.2 1.2 add_convert_fusion
  197.4 2.1 %pad_maximum_fusion = bf16[128,4096]{1,0:T(8,128)(2,1)} fusion(bf16[128,2048]{1,0:T(8,128)(2,1)} %fusion.14, bf16[128,2048]{1,0:T(8,128)(2,1)S(1)} %add_convert_fusion), kind=kLoop, calls=%fused_computation.19 | loop fusion | flops 2097152 | bytes 2097152 | tf_op jit(solution)/shard_map/concatenate | solution.py:348
  (115 shorter events, 14.9 us)
Async XLA Ops:
  6.5 7.1 %copy-start.2 = (bf16[4096,128]{1,0:T(8,128)(2,1)S(1)}, bf16[4096,128]{1,0:T(8,128)(2,1)}, u32[]{:S(2)}) copy-start(bf16[4096,128]{1,0:T(8,128)(2,1)} %param.16) | copy-start | bytes 3145732
  6.5 7.7 %copy-start.11 = (bf16[4,128]{1,0:T(4,128)(2,1)S(1)}, bf16[4,128]{1,0:T(4,128)(2,1)}, u32[]{:S(2)}) copy-start(bf16[4,128]{1,0:T(4,128)(2,1)} %param.21) | copy-start | bytes 3076
  6.5 7.7 %copy-start.9 = (bf16[4096,4]{0,1:T(4,128)(2,1)S(1)}, bf16[4096,4]{0,1:T(4,128)(2,1)}, u32[]{:S(2)}) copy-start(bf16[4096,4]{0,1:T(4,128)(2,1)} %param.17) | copy-start | bytes 98308
  6.5 11.4 %copy-start.13 = (f32[4]{0:T(128)S(1)}, f32[4]{0:T(128)}, u32[]{:S(2)}) copy-start(f32[4]{0:T(128)} %param.22) | copy-start | bytes 52
  6.5 11.6 %copy-start.8 = (s32[4096]{0:T(1024)S(1)}, s32[4096]{0:T(1024)}, u32[]{:S(2)}) copy-start(s32[4096]{0:T(1024)} %param.25) | copy-start | bytes 49156
  6.5 91.4 %all-gather.2.cloned.1.call-start = ((), (), s32[]{:S(2)}) async-start(), calls=%async_computation.1 | async-start | bytes 9437184 | tf_op jit(solution)/shard_map/all_gather | solution.py:323
  10.8 185.5 %reduce-scatter.2.cloned.1.call-start = ((), (), s32[]{:S(2)}) async-start(), calls=%async_computation.2 | async-start | bytes 4718592 | tf_op jit(solution)/shard_map/reduce_scatter | solution.py:345
  11.7 28.8 %collective-permute-start.10 = (bf16[8,4096]{1,0:T(8,128)(2,1)S(1)}, bf16[8,4096]{1,0:T(8,128)(2,1)S(1)}, u32[]{:S(2)}, u32[]{:S(2)}) collective-permute-start(bf16[8,4096]{1,0:T(8,128)(2,1)S(1)} %slice.82), channel_id=1, source_target_pairs={{7,14},{15,22},{23,30}} | collective-permute-start | bytes 196616 | tf_op jit(solution)/shard_map/ppermute | solution.py:37
  12.3 28.8 %collective-permute-start.11 = (bf16[8,4096]{1,0:T(8,128)(2,1)S(1)}, bf16[8,4096]{1,0:T(8,128)(2,1)S(1)}, u32[]{:S(2)}, u32[]{:S(2)}) collective-permute-start(bf16[8,4096]{1,0:T(8,128)(2,1)S(1)} %slice.82), channel_id=1, source_target_pairs={{7,15},{15,23},{23,31}} | collective-permute-start | bytes 196616 | tf_op jit(solution)/shard_map/ppermute | solution.py:37
  13.0 28.8 %collective-permute-start.4 = (bf16[8,4096]{1,0:T(8,128)(2,1)S(1)}, bf16[8,4096]{1,0:T(8,128)(2,1)S(1)}, u32[]{:S(2)}, u32[]{:S(2)}) collective-permute-start(bf16[8,4096]{1,0:T(8,128)(2,1)S(1)} %slice.82), channel_id=1, source_target_pairs={{7,8},{15,16},{23,24}} | collective-permute-start | bytes 196616 | tf_op jit(solution)/shard_map/ppermute | solution.py:37
  13.7 21.6 %collective-permute-start.3 = (bf16[4096,128]{1,0:T(8,128)(2,1)S(1)}, bf16[4096,128]{1,0:T(8,128)(2,1)S(1)}, u32[]{:S(2)}, u32[]{:S(2)}) collective-permute-start(bf16[4096,128]{1,0:T(8,128)(2,1)S(1)} %copy-done.2), channel_id=1, source_target_pairs={{0,1},{1,0},{2,3},{3,2},{4,5},{5,4},{6,7},{7,6},{8,9},{9,8},{10,11... | collective-permute-start | bytes 3145736 | tf_op jit(solution)/shard_map/ppermute | solution.py:23
  14.2 20.3 %collective-permute-start.12 = (bf16[4,128]{1,0:T(4,128)(2,1)S(1)}, bf16[4,128]{1,0:T(4,128)(2,1)S(1)}, u32[]{:S(2)}, u32[]{:S(2)}) collective-permute-start(bf16[4,128]{1,0:T(4,128)(2,1)S(1)} %copy-done.11), channel_id=1, source_target_pairs={{0,1},{1,0},{2,3},{3,2},{4,5},{5,4},{6,7},{7,6},{8,9},{9,8},{10,11... | collective-permute-start | bytes 3080 | tf_op jit(solution)/shard_map/ppermute | solution.py:23
  31.8 2.6 %copy-start.14 = (f32[4]{0:T(128)S(1)}, f32[4]{0:T(128)}, u32[]{:S(2)}) copy-start(f32[4]{0:T(128)} %param.18) | copy-start | bytes 52
  31.8 2.6 %copy-start.15 = (f32[4]{0:T(128)S(1)}, f32[4]{0:T(128)}, u32[]{:S(2)}) copy-start(f32[4]{0:T(128)} %param.19) | copy-start | bytes 52
  31.8 3.4 %copy-start.10 = (bf16[4,256]{1,0:T(4,128)(2,1)S(1)}, bf16[4,256]{1,0:T(4,128)(2,1)}, u32[]{:S(2)}) copy-start(bf16[4,256]{1,0:T(4,128)(2,1)} %param.20) | copy-start | bytes 6148
  34.5 9.3 %collective-permute-start.5 = (bf16[8,4096]{1,0:T(8,128)(2,1)S(1)}, bf16[8,4096]{1,0:T(8,128)(2,1)S(1)}, u32[]{:S(2)}, u32[]{:S(2)}) collective-permute-start(bf16[8,4096]{1,0:T(8,128)(2,1)S(1)} %slice.82), channel_id=1, source_target_pairs={{7,9},{15,17},{23,25}} | collective-permute-start | bytes 196616 | tf_op jit(solution)/shard_map/ppermute | solution.py:37
  35.2 12.2 %collective-permute-start.6 = (bf16[8,4096]{1,0:T(8,128)(2,1)S(1)}, bf16[8,4096]{1,0:T(8,128)(2,1)S(1)}, u32[]{:S(2)}, u32[]{:S(2)}) collective-permute-start(bf16[8,4096]{1,0:T(8,128)(2,1)S(1)} %slice.82), channel_id=1, source_target_pairs={{7,10},{15,18},{23,26}} | collective-permute-start | bytes 196616 | tf_op jit(solution)/shard_map/ppermute | solution.py:37
  35.9 2.7 %copy-start = (bf16[4096,1,256]{2,1,0:T(2,128)(2,1)S(1)}, bf16[4096,1,256]{2,1,0:T(2,128)(2,1)}, u32[]{:S(2)}) copy-start(bf16[4096,1,256]{2,1,0:T(2,128)(2,1)} %get-tuple-element.51) | copy-start | bytes 6291460
  38.6 3.9 %copy-start.3 = (bf16[4096,4]{1,0:T(8,128)(2,1)S(1)}, bf16[4096,4]{1,0:T(8,128)(2,1)}, u32[]{:S(2)}) copy-start(bf16[4096,4]{1,0:T(8,128)(2,1)} %copy.23) | copy-start | bytes 98308
  38.7 10.3 %copy-start.4 = (bf16[4096,256]{1,0:T(8,128)(2,1)S(1)}, bf16[4096,256]{1,0:T(8,128)(2,1)}, u32[]{:S(2)}) copy-start(bf16[4096,256]{1,0:T(8,128)(2,1)} %get-tuple-element.50) | copy-start | bytes 6291460
  40.4 8.5 %collective-permute-start.7 = (bf16[8,4096]{1,0:T(8,128)(2,1)S(1)}, bf16[8,4096]{1,0:T(8,128)(2,1)S(1)}, u32[]{:S(2)}, u32[]{:S(2)}) collective-permute-start(bf16[8,4096]{1,0:T(8,128)(2,1)S(1)} %slice.82), channel_id=1, source_target_pairs={{7,11},{15,19},{23,27}} | collective-permute-start | bytes 196616 | tf_op jit(solution)/shard_map/ppermute | solution.py:37
  41.1 7.9 %collective-permute-start.8 = (bf16[8,4096]{1,0:T(8,128)(2,1)S(1)}, bf16[8,4096]{1,0:T(8,128)(2,1)S(1)}, u32[]{:S(2)}, u32[]{:S(2)}) collective-permute-start(bf16[8,4096]{1,0:T(8,128)(2,1)S(1)} %slice.82), channel_id=1, source_target_pairs={{7,12},{15,20},{23,28}} | collective-permute-start | bytes 196616 | tf_op jit(solution)/shard_map/ppermute | solution.py:37
  41.8 7.2 %collective-permute-start.9 = (bf16[8,4096]{1,0:T(8,128)(2,1)S(1)}, bf16[8,4096]{1,0:T(8,128)(2,1)S(1)}, u32[]{:S(2)}, u32[]{:S(2)}) collective-permute-start(bf16[8,4096]{1,0:T(8,128)(2,1)S(1)} %slice.82), channel_id=1, source_target_pairs={{7,13},{15,21},{23,29}} | collective-permute-start | bytes 196616 | tf_op jit(solution)/shard_map/ppermute | solution.py:37
  43.8 8.9 %collective-permute-start = (bf16[256,512]{1,0:T(8,128)(2,1)S(1)}, bf16[256,512]{1,0:T(8,128)(2,1)S(1)}, u32[]{:S(2)}, u32[]{:S(2)}) collective-permute-start(bf16[256,512]{1,0:T(8,128)(2,1)S(1)} %constant_dynamic-slice_fusion.3), channel_id=1, source_target_pairs={{0,8},{8,0},{16,24},{24,16},{1,9},{9,1},{17,25},{25,17},{2,10},{10... | collective-permute-start | bytes 786440 | tf_op jit(solution)/shard_map/ppermute | solution.py:29
  47.4 7.9 %collective-permute-start.1 = (bf16[256,512]{1,0:T(8,128)(2,1)S(1)}, bf16[256,512]{1,0:T(8,128)(2,1)S(1)}, u32[]{:S(2)}, u32[]{:S(2)}) collective-permute-start(bf16[256,512]{1,0:T(8,128)(2,1)S(1)} %constant_dynamic-slice_fusion.3), channel_id=1, source_target_pairs={{0,16},{8,24},{16,0},{24,8},{1,17},{9,25},{17,1},{25,9},{2,18},{10... | collective-permute-start | bytes 786440 | tf_op jit(solution)/shard_map/ppermute | solution.py:29
  48.9 9.4 %collective-permute-start.2 = (bf16[256,512]{1,0:T(8,128)(2,1)S(1)}, bf16[256,512]{1,0:T(8,128)(2,1)S(1)}, u32[]{:S(2)}, u32[]{:S(2)}) collective-permute-start(bf16[256,512]{1,0:T(8,128)(2,1)S(1)} %constant_dynamic-slice_fusion.3), channel_id=1, source_target_pairs={{0,24},{8,16},{16,8},{24,0},{1,25},{9,17},{17,9},{25,1},{2,26},{10... | collective-permute-start | bytes 786440 | tf_op jit(solution)/shard_map/ppermute | solution.py:29
  52.7 61.9 %copy-start.5 = (bf16[256,512]{1,0:T(8,128)(2,1)}, bf16[256,512]{1,0:T(8,128)(2,1)S(1)}, u32[]{:S(2)}) copy-start(bf16[256,512]{1,0:T(8,128)(2,1)S(1)} %collective-permute-done) | copy-start | bytes 786436
  58.3 56.3 %copy-start.7 = (bf16[256,512]{1,0:T(8,128)(2,1)}, bf16[256,512]{1,0:T(8,128)(2,1)S(1)}, u32[]{:S(2)}) copy-start(bf16[256,512]{1,0:T(8,128)(2,1)S(1)} %collective-permute-done.2) | copy-start | bytes 786436
  97.9 27.6 %collective-permute-start.13 = (bf16[256,512]{1,0:T(8,128)(2,1)S(1)}, bf16[256,512]{1,0:T(8,128)(2,1)S(1)}, u32[]{:S(2)}, u32[]{:S(2)}) collective-permute-start(bf16[256,512]{1,0:T(8,128)(2,1)S(1)} %constant_dynamic-slice_fusion.3), channel_id=1, source_target_pairs={{0,2},{1,3},{2,0},{3,1},{4,6},{5,7},{6,4},{7,5},{8,10},{9,11},{10,... | collective-permute-start | bytes 786440 | tf_op jit(solution)/shard_map/ppermute | solution.py:29
  97.9 27.6 %collective-permute-start.14 = (bf16[256,512]{1,0:T(8,128)(2,1)S(1)}, bf16[256,512]{1,0:T(8,128)(2,1)S(1)}, u32[]{:S(2)}, u32[]{:S(2)}) collective-permute-start(bf16[256,512]{1,0:T(8,128)(2,1)S(1)} %constant_dynamic-slice_fusion.3), channel_id=1, source_target_pairs={{0,4},{1,5},{2,6},{3,7},{4,0},{5,1},{6,2},{7,3},{8,12},{9,13},{10,... | collective-permute-start | bytes 786440 | tf_op jit(solution)/shard_map/ppermute | solution.py:29
  100.2 25.3 %collective-permute-start.15 = (bf16[256,512]{1,0:T(8,128)(2,1)S(1)}, bf16[256,512]{1,0:T(8,128)(2,1)S(1)}, u32[]{:S(2)}, u32[]{:S(2)}) collective-permute-start(bf16[256,512]{1,0:T(8,128)(2,1)S(1)} %constant_dynamic-slice_fusion.3), channel_id=1, source_target_pairs={{0,6},{1,7},{2,4},{3,5},{4,2},{5,3},{6,0},{7,1},{8,14},{9,15},{10,... | collective-permute-start | bytes 786440 | tf_op jit(solution)/shard_map/ppermute | solution.py:29
  125.5 12.6 %copy-start.12 = (f32[256]{0:T(256)S(1)}, f32[256]{0:T(256)}, u32[]{:S(2)}) copy-start(f32[256]{0:T(256)} %param.23) | copy-start | bytes 3076
  125.6 6.7 %collective-permute-start.16 = (f32[136,256]{1,0:T(8,128)S(1)}, f32[136,256]{1,0:T(8,128)S(1)}, u32[]{:S(2)}, u32[]{:S(2)}) collective-permute-start(f32[136,256]{1,0:T(8,128)S(1)} %get-tuple-element.35), channel_id=1, source_target_pairs={{0,8},{8,16},{16,24},{1,9},{9,17},{17,25},{2,10},{10,18},{18,26},{... | collective-permute-start | bytes 417800 | tf_op jit(solution)/shard_map/ppermute | solution.py:210
  128.9 6.3 %collective-permute-start.17 = (f32[136,256]{1,0:T(8,128)S(1)}, f32[136,256]{1,0:T(8,128)S(1)}, u32[]{:S(2)}, u32[]{:S(2)}) collective-permute-start(f32[136,256]{1,0:T(8,128)S(1)} %get-tuple-element.35), channel_id=1, source_target_pairs={{0,16},{8,24},{1,17},{9,25},{2,18},{10,26},{3,19},{11,27},{4,20},{... | collective-permute-start | bytes 417800 | tf_op jit(solution)/shard_map/ppermute | solution.py:210
  130.8 4.4 %collective-permute-start.18 = (f32[136,256]{1,0:T(8,128)S(1)}, f32[136,256]{1,0:T(8,128)S(1)}, u32[]{:S(2)}, u32[]{:S(2)}) collective-permute-start(f32[136,256]{1,0:T(8,128)S(1)} %get-tuple-element.35), channel_id=1, source_target_pairs={{0,24},{1,25},{2,26},{3,27},{4,28},{5,29},{6,30},{7,31}} | collective-permute-start | bytes 417800 | tf_op jit(solution)/shard_map/ppermute | solution.py:210
  136.9 1.2 collective-permute-start.19
  142.8 20.8 %copy-start.1 = (bf16[128,4096]{1,0:T(8,128)(2,1)S(1)}, bf16[128,4096]{1,0:T(8,128)(2,1)}, u32[]{:S(2)}) copy-start(bf16[128,4096]{1,0:T(8,128)(2,1)} %param.13) | copy-start | bytes 3145732
  143.6 8.2 %collective-permute-start.20 = (bf16[256,256]{1,0:T(8,128)(2,1)S(1)}, bf16[256,256]{1,0:T(8,128)(2,1)S(1)}, u32[]{:S(2)}, u32[]{:S(2)}) collective-permute-start(bf16[256,256]{1,0:T(8,128)(2,1)S(1)} %get-tuple-element.55), channel_id=1, source_target_pairs={{0,2},{1,3},{2,0},{3,1},{4,6},{5,7},{6,4},{7,5},{8,10},{9,11},{10,... | collective-permute-start | bytes 393224 | tf_op jit(solution)/shard_map/ppermute | solution.py:29
  143.9 9.4 %collective-permute-start.21 = (bf16[256,256]{1,0:T(8,128)(2,1)}, bf16[256,256]{1,0:T(8,128)(2,1)S(1)}, u32[]{:S(2)}, u32[]{:S(2)}) collective-permute-start(bf16[256,256]{1,0:T(8,128)(2,1)} %get-tuple-element.54), channel_id=1, source_target_pairs={{0,4},{1,5},{2,6},{3,7},{4,0},{5,1},{6,2},{7,3},{8,12},{9,13},{10,... | collective-permute-start | bytes 393224 | tf_op jit(solution)/shard_map/ppermute | solution.py:29
  146.2 23.7 %collective-permute-start.28 = (bf16[768,512]{1,0:T(8,128)(2,1)S(1)}, bf16[768,512]{1,0:T(8,128)(2,1)}, u32[]{:S(2)}, u32[]{:S(2)}) collective-permute-start(bf16[768,512]{1,0:T(8,128)(2,1)S(1)} %pad_maximum_fusion.1), channel_id=1, source_target_pairs={{0,24},{8,16},{16,8},{24,0},{1,25},{9,17},{17,9},{25,1},{2,26},{10... | collective-permute-start | bytes 2359304 | tf_op jit(solution)/shard_map/ppermute | solution.py:29
  150.0 10.5 %collective-permute-start.22 = (bf16[256,256]{1,0:T(8,128)(2,1)}, bf16[256,256]{1,0:T(8,128)(2,1)S(1)}, u32[]{:S(2)}, u32[]{:S(2)}) collective-permute-start(bf16[256,256]{1,0:T(8,128)(2,1)} %get-tuple-element.53), channel_id=1, source_target_pairs={{0,6},{1,7},{2,4},{3,5},{4,2},{5,3},{6,0},{7,1},{8,14},{9,15},{10,... | collective-permute-start | bytes 393224 | tf_op jit(solution)/shard_map/ppermute | solution.py:29
  163.6 3.7 %collective-permute-start.23 = (bf16[128,512]{1,0:T(8,128)(2,1)}, bf16[128,512]{1,0:T(8,128)(2,1)}, u32[]{:S(2)}, u32[]{:S(2)}) collective-permute-start(bf16[128,512]{1,0:T(8,128)(2,1)} %dynamic-slice_convert_fusion.3), channel_id=1, source_target_pairs={{0,1},{1,0},{2,3},{3,2},{4,5},{5,4},{6,7},{7,6},{8,9},{9,8},{10,11... | collective-permute-start | bytes 393224 | tf_op jit(solution)/shard_map/ppermute | solution.py:29
  163.6 21.9 %copy-start.6 = (bf16[256,512]{1,0:T(8,128)(2,1)S(1)}, bf16[256,512]{1,0:T(8,128)(2,1)}, u32[]{:S(2)}) copy-start(bf16[256,512]{1,0:T(8,128)(2,1)} %copy-done.5) | copy-start | bytes 786436
  163.6 22.3 %collective-permute-start.26 = (bf16[768,512]{1,0:T(8,128)(2,1)S(1)}, bf16[768,512]{1,0:T(8,128)(2,1)S(1)}, u32[]{:S(2)}, u32[]{:S(2)}) collective-permute-start(bf16[768,512]{1,0:T(8,128)(2,1)S(1)} %pad_maximum_fusion.1), channel_id=1, source_target_pairs={{0,16},{8,24},{16,0},{24,8},{1,17},{9,25},{17,1},{25,9},{2,18},{10... | collective-permute-start | bytes 2359304 | tf_op jit(solution)/shard_map/ppermute | solution.py:29
  164.9 20.3 %collective-permute-start.24 = (bf16[768,512]{1,0:T(8,128)(2,1)S(1)}, bf16[768,512]{1,0:T(8,128)(2,1)S(1)}, u32[]{:S(2)}, u32[]{:S(2)}) collective-permute-start(bf16[768,512]{1,0:T(8,128)(2,1)S(1)} %pad_maximum_fusion.1), channel_id=1, source_target_pairs={{0,8},{8,0},{16,24},{24,16},{1,9},{9,1},{17,25},{25,17},{2,10},{10... | collective-permute-start | bytes 2359304 | tf_op jit(solution)/shard_map/ppermute | solution.py:29
  172.6 16.2 %collective-permute-start.29 = (bf16[128,512]{1,0:T(8,128)(2,1)S(1)}, bf16[128,512]{1,0:T(8,128)(2,1)S(1)}, u32[]{:S(2)}, u32[]{:S(2)}) collective-permute-start(bf16[128,512]{1,0:T(8,128)(2,1)S(1)} %dynamic-slice_convert_fusion), channel_id=1, source_target_pairs={{0,1},{1,0},{2,3},{3,2},{4,5},{5,4},{6,7},{7,6},{8,9},{9,8},{10,11... | collective-permute-start | bytes 393224 | tf_op jit(solution)/shard_map/ppermute | solution.py:29
  185.9 1.4 collective-permute-start.25
  186.6 1.5 collective-permute-start.27
Sparse Core Ops, SparseCore 0:
  10.9 86.9 all-gather.1
  142.9 53.2 reduce-scatter.1
